TPU v7x, 32 devices: a whole 2x2x4 slice. The times are simulated.
32 devices in a mesh: batch: 4 (over y, x), seq: 8 (over z, core).
Axes of the slice: x: 2, y: 2, z: 4, core: 2. Of those that a mesh axis runs over, the one named last changes fastest.
Arguments:
- tokens_in: bfloat16 [4, 4096, 1024], P('batch', 'seq'), may hold values from -6 to 6
- skip_in: bfloat16 [4, 4096, 1024], P('batch', 'seq'), may hold values from -6 to 6
- condition: bfloat16 [4, 4096, 1024], P('batch', 'seq'), may hold values from -3 to 3
- cotangent: bfloat16 [4, 4096, 1024], P('batch', 'seq'), may hold values from -6 to 6
- time_embed: float32 [4, 8, 1024], P('batch'), may hold values from -6 to 6
- lengths: int32 [4, 8], P('batch'), may hold values from 1 to 2048, 4096 in all within a row
- key_mask: int32 [4, 4096], P('batch'), may hold values 0 or 1
- drop_mask: int32 [4, 8], P('batch'), may hold values 0 or 1
- loss_mask: int32 [4, 4096], P('batch', 'seq'), may hold values from 0 to 1, as said below
- w_skip: bfloat16 [2048, 1024], replicated, may hold values from -0.125 to 0.125
- b_skip: bfloat16 [1024], replicated, may hold values from -2 to 2
- w_ada: bfloat16 [1024, 6144], replicated, may hold values from -0.1875 to 0.1875
- b_ada: bfloat16 [6144], replicated, may hold values from -3 to 3
- w_qkv: bfloat16 [1024, 3072], replicated, may hold values from -0.1875 to 0.1875
- b_qkv: bfloat16 [3072], replicated, may hold values from -2 to 2
- w_out: bfloat16 [1024, 1024], replicated, may hold values from -1.5 to 1.5
- b_out: bfloat16 [1024], replicated, may hold values from -2 to 2
- w_up: bfloat16 [1024, 4096], replicated, may hold values from -0.1875 to 0.1875
- b_up: bfloat16 [4096], replicated, may hold values from -2 to 2
- w_down: bfloat16 [4096, 1024], replicated, may hold values from -0.09375 to 0.09375
- b_down: bfloat16 [1024], replicated, may hold values from -2 to 2
Outputs:
- output: bfloat16 [4, 4096, 1024], P('batch', 'seq')
- grad_tokens: float32 [4, 4096, 1024], P('batch', 'seq')
- grad_skip: float32 [4, 4096, 1024], P('batch', 'seq')
- grad_w_skip: float32 [2048, 1024], P('seq')
- grad_b_skip: float32 [1024], P('seq')
- grad_w_ada: float32 [1024, 6144], P('seq')
- grad_b_ada: float32 [6144], P('seq')
- grad_w_qkv: float32 [1024, 3072], P('seq')
- grad_b_qkv: float32 [3072], P('seq')
- grad_w_out: float32 [1024, 1024], P('seq')
- grad_b_out: float32 [1024], P('seq')
- grad_w_up: float32 [1024, 4096], P('seq')
- grad_b_up: float32 [4096], P('seq')
- grad_w_down: float32 [4096, 1024], P('seq')
- grad_b_down: float32 [1024], P('seq')
Inputs may be any that keep to these rules, and one draw needn't show every extreme that they name: Each group's 8 lengths sum to 4096; in every group the longest is exactly 2048. `loss_mask`: the last frame of every group is a loss frame.
All inputs are finite; a program needn't handle non-finite values. No bound on the sum of `key_mask` or of `drop_mask` on one device may be relied on, other than what follows from the above.
Results may differ from a plain program's by a relative error of at most 0.02.
Values may be sent and summed in bfloat16 or wider, within the bound.
No kernel may reach another device: no remote copies, remote signals or barrier semaphores. Data moves between devices by JAX's collectives and lax.ppermute only.
A program may use at most 320 MiB of HBM per device.

v0:
```python
import functools

import jax
import jax.numpy as jnp
from jax import lax
from jax.experimental import pallas as pl
from jax.experimental.pallas import tpu as pltpu
from jax.sharding import PartitionSpec as P

HEADS = 16
HEAD_DIM = 64
PARTS = 8
BIG = 1e30
DH = 64
BQ = 512
BK = 512


def cost(weight):
    return pl.CostEstimate(flops=weight * 100000000, bytes_accessed=weight * 100000, transcendentals=0)


def onehot_rows(lengths_ref, utts, rows, base, width):
    row = lax.broadcasted_iota(jnp.int32, (rows, width), 0)
    col = base + lax.broadcasted_iota(jnp.int32, (rows, width), 1)
    start = jnp.int32(0)
    hot = jnp.zeros((rows, width), jnp.float32)
    for u in range(utts):
        end = start + lengths_ref[u]
        hot = jnp.where((row == u) & (col >= start) & (col < end), 1.0, hot)
        start = end
    return hot


def key_range(lengths_ref, utts, first, last):
    start = jnp.int32(0)
    low, high = jnp.int32(0), jnp.int32(0)
    for u in range(utts):
        end = start + lengths_ref[u]
        low = jnp.where((start <= first) & (first < end), start, low)
        high = jnp.where((start <= last) & (last < end), end, high)
        start = end
    return low // BK, (high + BK - 1) // BK


def aug_rows(utts):
    return -(-utts // 16) * 16


def split3(row):
    a = row.astype(jnp.bfloat16)
    rest = row - a.astype(jnp.float32)
    b = rest.astype(jnp.bfloat16)
    c = (rest - b.astype(jnp.float32)).astype(jnp.bfloat16)
    return a, b, c


def pad_rows(parts, total):
    have = sum(p.shape[0] for p in parts)
    if have < total:
        parts = parts + [jnp.zeros((total - have, parts[0].shape[1]), parts[0].dtype)]
    return jnp.concatenate(parts, axis=0)


def rows16(rows, width):
    idx = lax.broadcasted_iota(jnp.int32, (16, width), 0)
    out = jnp.zeros((16, width), jnp.float32)
    for i, r in enumerate(rows):
        out = jnp.where(idx == i, r, out)
    return out.astype(jnp.bfloat16)


def fwd_kernel(utts, lengths_ref, qkv_ref, ok_ref, out_ref, lse_ref, kaug, vaug):
    sources, _, frames = qkv_ref.shape
    per = frames // BQ
    pad_u = aug_rows(utts)
    step = pl.program_id(0)

    @pl.when(step == 0)
    def _():
        def build(s, c):
            hot = onehot_rows(lengths_ref, utts, pad_u, s * frames, frames)
            ok = ok_ref[s].astype(jnp.float32)
            block = qkv_ref[s]
            one = jnp.ones((1, frames), jnp.float32)
            kT = pad_rows(
                [block[DH : 2 * DH], (1.0 - hot).astype(jnp.bfloat16), rows16([1.0 - ok], frames)], 128
            )
            kaug[pl.ds(pl.multiple_of(s * frames, frames), frames), :] = kT.T
            vT = jnp.concatenate([block[2 * DH :], rows16([one], frames)], axis=0)
            for t in range(frames // BK):
                vaug[s * (frames // BK) + t] = vT[:, t * BK : (t + 1) * BK]
            return c

        lax.fori_loop(0, sources, build, 0)

    block = qkv_ref[step]
    hot_q = onehot_rows(lengths_ref, utts, pad_u, step * frames, frames)
    qT = (block[:DH].astype(jnp.float32) * 0.125)
    one = jnp.ones((1, frames), jnp.float32)
    qaug = pad_rows(
        [qT.astype(jnp.bfloat16), (hot_q * -BIG).astype(jnp.bfloat16), rows16([one * -BIG], frames)], 128
    )
    kT = block[DH : 2 * DH].astype(jnp.float32)
    vT = block[2 * DH :].astype(jnp.float32)
    ok = ok_ref[step] > 0
    s_self = jnp.sum(qT * kT, axis=0, keepdims=True)
    m0 = jnp.where(ok, -3e38, s_self)
    acc0 = jnp.concatenate([jnp.where(ok, 0.0, vT), jnp.where(ok, 0.0, jnp.ones((16, frames), jnp.float32))], axis=0)
    for t in range(per):
        cols = slice(t * BQ, (t + 1) * BQ)
        low, high = key_range(lengths_ref, utts, step * frames + t * BQ, step * frames + (t + 1) * BQ - 1)
        q_b = qaug[:, cols]

        def body(j, carry):
            m, acc = carry
            s = jnp.dot(kaug[pl.ds(pl.multiple_of(j * BK, BK), BK), :], q_b, preferred_element_type=jnp.float32)
            m_new = jnp.maximum(m, jnp.max(s, axis=0, keepdims=True))
            p = jnp.exp(s - m_new).astype(jnp.bfloat16)
            alpha = jnp.exp(m - m_new)
            acc = acc * alpha + jnp.dot(vaug[j], p, preferred_element_type=jnp.float32)
            return m_new, acc

        m, acc = lax.fori_loop(low, high, body, (m0[:, cols], acc0[:, cols]))
        total = acc[DH : DH + 1]
        out_ref[0, :, cols] = (acc[:DH] / total).astype(jnp.bfloat16)
        lse_ref[0, :, cols] = m + jnp.log(total)


def attend(lengths, qkv, ok):
    sources, _, frames = qkv.shape
    total = sources * frames
    utts = lengths.shape[0]
    whole = lambda shape: pl.BlockSpec(shape, lambda i, *_: (0,) * len(shape))
    return pl.pallas_call(
        functools.partial(fwd_kernel, utts),
        out_shape=(
            jax.ShapeDtypeStruct((sources, DH, frames), jnp.bfloat16),
            jax.ShapeDtypeStruct((sources, 1, frames), jnp.float32),
        ),
        grid_spec=pltpu.PrefetchScalarGridSpec(
            num_scalar_prefetch=1,
            grid=(sources,),
            in_specs=[whole(qkv.shape), whole(ok.shape)],
            out_specs=(
                pl.BlockSpec((1, DH, frames), lambda i, *_: (i, 0, 0)),
                pl.BlockSpec((1, 1, frames), lambda i, *_: (i, 0, 0)),
            ),
            scratch_shapes=[
                pltpu.VMEM((total, 128), jnp.bfloat16),
                pltpu.VMEM((total // BK, DH + 16, BK), jnp.bfloat16),
            ],
        ),
        cost_estimate=cost(250),
        name="attend",
    )(lengths, qkv, ok)


def bwd_kernel(utts, chunk, lengths_ref, qkv_ref, ok_ref, o_ref, do_ref, lse_ref, out_ref, kaug, vnat, kT_s, dk, dv):
    sources, _, frames = qkv_ref.shape
    per = frames // BK
    pad_u = aug_rows(utts)
    step = pl.program_id(0)
    f32 = jnp.float32

    @pl.when(step == 0)
    def _():
        def build(s, c):
            hot = onehot_rows(lengths_ref, utts, pad_u, s * frames, frames)
            ok = ok_ref[s]
            block = qkv_ref[s]
            one = jnp.ones((1, frames), f32)
            kT = block[DH : 2 * DH]
            vT = block[2 * DH :]
            kA = pad_rows(
                [kT, (1.0 - hot).astype(jnp.bfloat16), rows16([1.0 - ok.astype(f32), one, one, one], frames)], 128
            )
            rows = pl.ds(pl.multiple_of(s * frames, frames), frames)
            kaug[rows, :] = kA.T
            vnat[rows, :] = pad_rows([vT, rows16([one, one, one], frames)], 128).T
            qT = block[:DH].astype(f32) * 0.125
            do = do_ref[s, chunk * DH : (chunk + 1) * DH, :].astype(f32)
            s_self = jnp.sum(qT * kT.astype(f32), axis=0, keepdims=True)
            delta = jnp.sum(do * o_ref[s].astype(f32), axis=0, keepdims=True)
            p_self = jnp.where(ok > 0, 0.0, jnp.exp(s_self - lse_ref[s]))
            ds_self = p_self * (jnp.sum(do * vT.astype(f32), axis=0, keepdims=True) - delta)
            dk0 = ds_self * qT
            dv0 = p_self * do
            for t in range(per):
                cols = slice(t * BK, (t + 1) * BK)
                kT_s[s * per + t] = kT[:, cols]
                dk[s * per + t] = dk0[:, cols]
                dv[s * per + t] = dv0[:, cols]
            return c

        lax.fori_loop(0, sources, build, 0)

    block = qkv_ref[step]
    one = jnp.ones((1, frames), f32)
    hot_q = onehot_rows(lengths_ref, utts, pad_u, step * frames, frames)
    qT = block[:DH].astype(f32) * 0.125
    qTb = qT.astype(jnp.bfloat16)
    kT = block[DH : 2 * DH].astype(f32)
    vT = block[2 * DH :].astype(f32)
    ok = ok_ref[step]
    dob = do_ref[step, chunk * DH : (chunk + 1) * DH, :]
    do = dob.astype(f32)
    lse = lse_ref[step]
    delta = jnp.sum(do * o_ref[step].astype(f32), axis=0, keepdims=True)
    l3 = [-r.astype(f32) for r in split3(lse)]
    d3 = [-r.astype(f32) for r in split3(delta)]
    qaug = pad_rows([qTb, (hot_q * -BIG).astype(jnp.bfloat16), rows16([one * -BIG] + l3, frames)], 128)
    doaug = pad_rows([dob, rows16(d3, frames)], 128)
    s_self = jnp.sum(qT * kT, axis=0, keepdims=True)
    p_self = jnp.where(ok > 0, 0.0, jnp.exp(s_self - lse))
    ds_self = p_self * (jnp.sum(do * vT, axis=0, keepdims=True) - delta)
    dq0 = ds_self * kT
    nt = (((1,), (1,)), ((), ()))
    for t in range(frames // BQ):
        cols = slice(t * BQ, (t + 1) * BQ)
        low, high = key_range(lengths_ref, utts, step * frames + t * BQ, step * frames + (t + 1) * BQ - 1)
        q_a = qaug[:, cols]
        q_b = qTb[:, cols]
        do_a = doaug[:, cols]
        do_b = dob[:, cols]

        def body(j, dq):
            rows = pl.ds(pl.multiple_of(j * BK, BK), BK)
            s = jnp.dot(kaug[rows, :], q_a, preferred_element_type=f32)
            dp = jnp.dot(vnat[rows, :], do_a, preferred_element_type=f32)
            p = jnp.exp(s)
            ds = (p * dp).astype(jnp.bfloat16)
            dv[j] += lax.dot_general(do_b, p.astype(jnp.bfloat16), nt, preferred_element_type=f32)
            dk[j] += lax.dot_general(q_b, ds, nt, preferred_element_type=f32)
            return dq + jnp.dot(kT_s[j], ds, preferred_element_type=f32)

        dq = lax.fori_loop(low, high, body, dq0[:, cols])
        out_ref[step, :DH, cols] = (dq * 0.125).astype(jnp.bfloat16)

    @pl.when(step == sources - 1)
    def _():
        def finish(s, c):
            for t in range(per):
                cols = slice(t * BK, (t + 1) * BK)
                out_ref[s, DH : 2 * DH, cols] = dk[s * per + t].astype(jnp.bfloat16)
                out_ref[s, 2 * DH :, cols] = dv[s * per + t].astype(jnp.bfloat16)
            return c

        lax.fori_loop(0, sources, finish, 0)


def attend_back(lengths, qkv, ok, out, grad, lse, chunk):
    sources, _, frames = qkv.shape
    total = sources * frames
    utts = lengths.shape[0]
    whole = lambda shape: pl.BlockSpec(shape, lambda i, *_: (0,) * len(shape))
    return pl.pallas_call(
        functools.partial(bwd_kernel, utts, chunk),
        out_shape=jax.ShapeDtypeStruct(qkv.shape, jnp.bfloat16),
        grid_spec=pltpu.PrefetchScalarGridSpec(
            num_scalar_prefetch=1,
            grid=(sources,),
            in_specs=[whole(a.shape) for a in (qkv, ok, out, grad, lse)],
            out_specs=whole(qkv.shape),
            scratch_shapes=[
                pltpu.VMEM((total, 128), jnp.bfloat16),
                pltpu.VMEM((total, 128), jnp.bfloat16),
                pltpu.VMEM((total // BK, DH, BK), jnp.bfloat16),
                pltpu.VMEM((total // BK, DH, BK), jnp.float32),
                pltpu.VMEM((total // BK, DH, BK), jnp.float32),
            ],
        ),
        cost_estimate=cost(320),
        name="attend_back",
    )(lengths, qkv, ok, out, grad, lse)


FF_TILE = 512
EPS = 1e-06


def dot(left, right):
    return jnp.dot(left, right, preferred_element_type=jnp.float32)


def dot_nt(left, right):
    return lax.dot_general(left, right, (((1,), (1,)), ((), ())), preferred_element_type=jnp.float32)


def norm_stats(x):
    mean = jnp.mean(x, axis=1, keepdims=True)
    centred = x - mean
    rstd = lax.rsqrt(jnp.mean(centred * centred, axis=1, keepdims=True) + EPS)
    return centred * rstd, rstd


def norm_back(grad, normed, rstd):
    first = jnp.mean(grad, axis=1, keepdims=True)
    second = jnp.mean(grad * normed, axis=1, keepdims=True)
    return rstd * (grad - first - normed * second)


def mods_operand(mods_ref):
    rows = mods_ref[...]
    return pad_rows(list(split3(rows)), 128)


def table_rows(utts):
    return -(-utts // 8) * 8


def sum_rows(hot, utts_pad, frames):
    idx = lax.broadcasted_iota(jnp.int32, (16, frames), 0)
    ones = jnp.where(idx == 0, 1.0, 0.0).astype(jnp.bfloat16)
    return jnp.concatenate([hot.astype(jnp.bfloat16), ones], axis=0)


def mid_kernel(
    dims,
    lengths_ref,
    ids_ref,
    *refs,
):
    seq_ways, heads_local, utts, ff = dims
    att_refs = refs[:heads_local]
    (
        hidden_ref,
        mods_ref,
        cot_ref,
        loss_ref,
        w_out_ref,
        b_out_ref,
        w_up_ref,
        b_up_ref,
        w_down_ref,
        b_down_ref,
    ) = refs[heads_local : heads_local + 10]
    outs = refs[heads_local + 10 :]
    output_ref, after_grad_ref, small_ref, gatt_ref = outs[:4]
    refs_out = outs[4:6]
    (
        attT,
        attn_proj,
        after,
        nf,
        nfT,
        gff,
        ff_acc,
        gnf_acc,
        sums,
        cols,
        madd,
        grads,
        sems,
    ) = outs[6:]
    f32, bf16 = jnp.float32, jnp.bfloat16
    step = pl.program_id(0)
    steps = pl.num_programs(0)
    core = ids_ref[0]
    rank = ids_ref[1]
    frames, width = hidden_ref.shape
    up_rows = width // seq_ways
    down_rows = FF_TILE
    z_ways = seq_ways // 2
    parts = grads.shape[1]
    pad_u = table_rows(utts)
    ff_total = ff
    up_part = ff_total // width * up_rows // parts
    down_block = ff_total // seq_ways
    down_part = down_block // parts
    out_part = up_rows // parts

    def mod(index):
        return dot(cols[...], madd[:, index * width : (index + 1) * width])

    def grad_out():
        loss = cols[:, 48:49].astype(f32)
        return cot_ref[...].astype(f32) * loss

    @pl.when(step == 0)
    def _():
        hot = onehot_rows(lengths_ref, utts, 16, rank * frames, frames)
        hotb = hot.astype(bf16)
        idx = lax.broadcasted_iota(jnp.int32, (16, frames), 0)
        loss = jnp.where(idx == 0, loss_ref[...].astype(f32), 0.0).astype(bf16)
        cols[...] = pad_rows([hotb, hotb, hotb, loss], 128).T
        sums[...] = sum_rows(hot, 16, frames)
        madd[...] = mods_operand(mods_ref)
        for c in range(heads_local):
            for s in range(seq_ways):
                attT[(c * seq_ways + s) * DH : (c * seq_ways + s + 1) * DH, :] = att_refs[c][s]
        proj = dot(attT[...].T, w_out_ref[...]) + b_out_ref[...].astype(f32)
        attn_proj[...] = proj
        mixed = hidden_ref[...] + mod(0) * proj
        after[...] = mixed
        normed, _ = norm_stats(mixed)
        value = (normed * (1.0 + mod(2)) + mod(1)).astype(bf16)
        nf[...] = value
        nfT[...] = value.T
        gff[...] = (grad_out() * mod(3)).astype(bf16)
        small_ref[4 * pad_u :, :] = jnp.zeros((8, width), f32)

    up = dot(nf[...], w_up_ref[...]) + b_up_ref[...].astype(f32)
    inner = 0.7978845608028654 * (up + 0.044715 * (up * up * up))
    tanh = jnp.tanh(inner)
    cdf = 0.5 * (1.0 + tanh)
    act = (up * cdf).astype(bf16)
    slope = cdf + 0.5 * up * (1.0 - tanh * tanh) * (
        0.7978845608028654 * (1.0 + (3 * 0.044715) * (up * up))
    )
    ff_part = dot(act, w_down_ref[...])
    gup = (dot_nt(gff[...], w_down_ref[...]) * slope).astype(bf16)
    gnf_part = dot_nt(gup, w_up_ref[...])

    @pl.when(step == 0)
    def _():
        ff_acc[...] = ff_part
        gnf_acc[...] = gnf_part

    @pl.when(step > 0)
    def _():
        ff_acc[...] += ff_part
        gnf_acc[...] += gnf_part

    halves = width // FF_TILE
    chunk = step // halves
    half = step % halves
    col = pl.ds(pl.multiple_of(half * FF_TILE, FF_TILE), FF_TILE)
    per_chunk = up_rows // up_part
    small_ref[pl.ds(4 * pad_u + 2 + chunk, 1), col] = dot(sums[16:32, :], gup)[:1]
    grad_w_up = dot(nfT[...], gup).astype(bf16)
    for s in range(seq_ways):
        side = jnp.where(core == s % 2, 0, 1)
        for h in range(per_chunk):
            lo = s * up_rows + h * up_part
            grads[side, chunk * per_chunk + h, s // 2, 0:up_part, col] = grad_w_up[lo : lo + up_part]
    grad_w_down = dot(act.T, gff[...]).astype(bf16)
    blocks = FF_TILE // down_block
    copies = []
    for b in range(blocks):
        s = step * blocks + b
        side = jnp.where(core == s % 2, 0, 1)
        for k in range(parts):
            lo = b * down_block + k * down_part
            grads[side, k, s // 2, up_part : up_part + down_part, :] = grad_w_down[lo : lo + down_part]

    def region_copy(side, where, index):
        return pltpu.make_async_copy(
            grads.at[side].at[where], refs_out[side].at[where], sems.at[side, index]
        )

    def up_copy(side, j):
        where = (
            pl.ds((j // halves) * per_chunk, per_chunk),
            slice(None),
            pl.ds(0, up_part),
            pl.ds(pl.multiple_of((j % halves) * FF_TILE, FF_TILE), FF_TILE),
        )
        return region_copy(side, where, j)

    def down_copy(side, z, index):
        return region_copy(side, (slice(None), pl.ds(z, 1), pl.ds(up_part, down_part)), index)

    def out_copy(side):
        where = (slice(None), slice(None), pl.ds(up_part + down_part, out_part))
        return region_copy(side, where, ff_total // FF_TILE + z_ways)

    base = ff_total // FF_TILE
    for side in range(2):
        up_copy(side, step).start()
    for b in range(blocks):
        s = step * blocks + b
        for side in range(2):

            @pl.when(lax.rem(s + core, 2) == side)
            def _():
                down_copy(side, s // 2, base + s // 2).start()

    @pl.when(step == steps - 1)
    def _():
        ff_out = ff_acc[...] + b_down_ref[...].astype(f32)
        mixed = after[...]
        go = grad_out()
        output_ref[...] = (mixed + mod(3) * ff_out).astype(bf16)
        rows = sums[...]
        small_ref[3 * pad_u : 4 * pad_u, :] = dot(rows, (go * ff_out).astype(bf16))[:pad_u]
        normed, rstd = norm_stats(mixed)
        gnf = gnf_acc[...]
        small_ref[pad_u : 2 * pad_u, :] = dot(rows, gnf.astype(bf16))[:pad_u]
        small_ref[2 * pad_u : 3 * pad_u, :] = dot(rows, (gnf * normed).astype(bf16))[:pad_u]
        g_after = go + norm_back(gnf * (1.0 + mod(2)), normed, rstd)
        after_grad_ref[...] = g_after
        small_ref[0:pad_u, :] = dot(rows, (g_after * attn_proj[...]).astype(bf16))[:pad_u]
        gattn = (g_after * mod(0)).astype(bf16)
        small_ref[4 * pad_u : 4 * pad_u + 1, :] = dot(rows, gattn)[16:17]
        small_ref[4 * pad_u + 1 : 4 * pad_u + 2, :] = dot(rows, gff[...])[16:17]
        gattT = dot_nt(w_out_ref[...], gattn).astype(bf16)
        for c in range(heads_local):
            for s in range(seq_ways):
                lo = (c * seq_ways + s) * DH
                gatt_ref[s, c * DH : (c + 1) * DH, :] = gattT[lo : lo + DH]
        grad_w_out = dot(attT[...], gattn).astype(bf16)
        for s in range(seq_ways):
            side = jnp.where(core == s % 2, 0, 1)
            for k in range(parts):
                lo = s * up_rows + k * out_part
                grads[side, k, s // 2, up_part + down_part : up_part + down_part + out_part, :] = grad_w_out[
                    lo : lo + out_part
                ]
        for side in range(2):
            out_copy(side).start()
        for side in range(2):
            for j in range(ff_total // FF_TILE):
                up_copy(side, j).wait()
            for z in range(z_ways):
                down_copy(side, z, base + z).wait()
            out_copy(side).wait()


def mid_block(
    lengths, ids, att, hidden, mods, cot, loss, w_out, b_out, w_up, b_up, w_down, b_down, parts
):
    frames, width = hidden.shape
    heads_local = len(att)
    seq_ways = att[0].shape[0]
    ff = w_up.shape[1]
    up_rows = width // seq_ways
    rows = (ff // width * up_rows + ff // seq_ways + up_rows) // parts
    utts = lengths.shape[0]
    f32, bf16 = jnp.float32, jnp.bfloat16
    steps = ff // FF_TILE

    def whole(shape):
        return pl.BlockSpec(shape, lambda j, *_: (0,) * len(shape), pipeline_mode=pl.Buffered(1))

    hbm = pl.BlockSpec(memory_space=pl.ANY)
    gshape = (parts, seq_ways // 2, rows, width)
    out_shape = [
        jax.ShapeDtypeStruct((frames, width), bf16),
        jax.ShapeDtypeStruct((frames, width), f32),
        jax.ShapeDtypeStruct((4 * table_rows(utts) + 8, width), f32),
    ]
    out_shape += [jax.ShapeDtypeStruct((seq_ways, heads_local * DH, frames), bf16)]
    out_specs = [whole(o.shape) for o in out_shape] + [hbm] * 2
    out_shape += [jax.ShapeDtypeStruct(gshape, bf16)] * 2
    ins = list(att) + [hidden, mods, cot, loss, w_out, b_out]
    return pl.pallas_call(
        functools.partial(mid_kernel, (seq_ways, heads_local, utts, ff)),
        out_shape=out_shape,
        grid_spec=pltpu.PrefetchScalarGridSpec(
            num_scalar_prefetch=2,
            grid=(steps,),
            in_specs=[whole(a.shape) for a in ins]
            + [
                pl.BlockSpec((width, FF_TILE), lambda j, *_: (0, j)),
                pl.BlockSpec((1, FF_TILE), lambda j, *_: (0, j)),
                pl.BlockSpec((FF_TILE, width), lambda j, *_: (j, 0)),
                whole((1, width)),
            ],
            out_specs=out_specs,
            scratch_shapes=[
                pltpu.VMEM((width, frames), bf16),
                pltpu.VMEM((frames, width), f32),
                pltpu.VMEM((frames, width), f32),
                pltpu.VMEM((frames, width), bf16),
                pltpu.VMEM((width, frames), bf16),
                pltpu.VMEM((frames, width), bf16),
                pltpu.VMEM((frames, width), f32),
                pltpu.VMEM((frames, width), f32),
                pltpu.VMEM((32, frames), bf16),
                pltpu.VMEM((frames, 128), bf16),
                pltpu.VMEM((128, 4 * width), bf16),
                pltpu.VMEM((2,) + gshape, bf16),
                pltpu.SemaphoreType.DMA((2, steps + seq_ways // 2 + 1)),
            ],
        ),
        compiler_params=pltpu.CompilerParams(vmem_limit_bytes=63 << 20),
        cost_estimate=cost(500),
        name="mid_block",
    )(lengths, ids, *ins, w_up, b_up, w_down, b_down)


def whole_block(shape):
    return pl.BlockSpec(shape, lambda *_: (0,) * len(shape), pipeline_mode=pl.Buffered(1))


def segment_rows(lengths_ref, drop_ref, utts, base, width):
    col = base + lax.broadcasted_iota(jnp.int32, (1, width), 1)
    start = jnp.int32(0)
    kept = jnp.zeros((1, width), jnp.float32)
    place = jnp.zeros((1, width), jnp.int32)
    for u in range(utts):
        end = start + lengths_ref[u]
        inside = (col >= start) & (col < end)
        kept = jnp.where(inside, (1 - drop_ref[u]).astype(jnp.float32), kept)
        place = jnp.where(inside, col - start, place)
        start = end
    return kept, place.astype(jnp.float32)


def rotary_rows(place, half):
    index = lax.broadcasted_iota(jnp.int32, (half, 1), 0).astype(jnp.float32)
    inverse = jnp.exp(index * (-9.210340371976184 / half))
    angles = inverse * place
    return jnp.cos(angles), jnp.sin(angles)


def frame_columns(hot, extra):
    hotb = hot.astype(jnp.bfloat16)
    idx = lax.broadcasted_iota(jnp.int32, hot.shape, 0)
    last = jnp.where(idx == 0, extra, 0.0).astype(jnp.bfloat16)
    return pad_rows([hotb, hotb, hotb, last], 128).T


def head_kernel(
    utts,
    lengths_ref,
    ids_ref,
    drop_ref,
    tokens_ref,
    skip_ref,
    cond_ref,
    mods_ref,
    w_skip_ref,
    b_skip_ref,
    hidden_ref,
    joinedT_ref,
    naT_ref,
    na_ref,
    cols,
):
    f32, bf16 = jnp.float32, jnp.bfloat16
    step = pl.program_id(0)
    frames, width = tokens_ref.shape
    rank = ids_ref[1]

    @pl.when(step == 0)
    def _():
        hot = onehot_rows(lengths_ref, utts, 16, rank * frames, frames)
        kept, _ = segment_rows(lengths_ref, drop_ref, utts, rank * frames, frames)
        cols[...] = frame_columns(hot, kept)
        keep = cols[:, 48:49].astype(f32)
        mixed = (tokens_ref[...].astype(f32) + keep * cond_ref[...].astype(f32)).astype(bf16)
        joinedT_ref[0:width, :] = mixed.T
        hidden_ref[...] = dot(mixed, w_skip_ref[...]) + b_skip_ref[...].astype(f32)

    @pl.when(step == 1)
    def _():
        skip = skip_ref[...]
        joinedT_ref[width : 2 * width, :] = skip.T
        hidden = hidden_ref[...] + dot(skip, w_skip_ref[...])
        hidden_ref[...] = hidden
        madd = mods_operand(mods_ref)
        shift = dot(cols[...], madd[:, :width])
        scale = dot(cols[...], madd[:, width:])
        normed, _ = norm_stats(hidden)
        value = (normed * (1.0 + scale) + shift).astype(bf16)
        na_ref[...] = value
        naT_ref[...] = value.T


def head_block(lengths, ids, drop, tokens, skip, cond, mods, w_skip, b_skip):
    frames, width = tokens.shape
    utts = lengths.shape[0]
    f32, bf16 = jnp.float32, jnp.bfloat16

    def whole(shape):
        return pl.BlockSpec(shape, lambda j, *_: (0,) * len(shape), pipeline_mode=pl.Buffered(1))

    out_shape = [
        jax.ShapeDtypeStruct((frames, width), f32),
        jax.ShapeDtypeStruct((2 * width, frames), bf16),
        jax.ShapeDtypeStruct((width, frames), bf16),
        jax.ShapeDtypeStruct((frames, width), bf16),
    ]
    return pl.pallas_call(
        functools.partial(head_kernel, utts),
        out_shape=out_shape,
        grid_spec=pltpu.PrefetchScalarGridSpec(
            num_scalar_prefetch=3,
            grid=(2,),
            in_specs=[whole(a.shape) for a in (tokens, skip, cond, mods)]
            + [pl.BlockSpec((width, width), lambda j, *_: (j, 0)), whole((1, width))],
            out_specs=[whole(o.shape) for o in out_shape],
            scratch_shapes=[pltpu.VMEM((frames, 128), bf16)],
        ),
        compiler_params=pltpu.CompilerParams(vmem_limit_bytes=48 << 20),
        cost_estimate=cost(100),
        name="head_block",
    )(lengths, ids, drop, tokens, skip, cond, mods, w_skip, b_skip)


def turn_heads(tensor, cosine, sine):
    half = DH // 2
    first, second = tensor[:, :half], tensor[:, half:]
    return jnp.concatenate([first * cosine - second * sine, second * cosine + first * sine], axis=1)


def qkv_kernel(utts, seq_ways, lengths_ref, ids_ref, drop_ref, na_ref, w_ref, b_ref, out_ref, trig):
    f32, bf16 = jnp.float32, jnp.bfloat16
    part = pl.program_id(0)
    frames = na_ref.shape[0]

    @pl.when(part == 0)
    def _():
        _, place = segment_rows(lengths_ref, drop_ref, utts, ids_ref[1] * frames, frames)
        cosine, sine = rotary_rows(place, DH // 2)
        trig[0] = cosine
        trig[1] = sine

    raw = dot(na_ref[...], w_ref[...]) + b_ref[...].astype(f32)
    rawT = raw.T.reshape(seq_ways, DH, frames)
    turned = part < 2
    cosine = jnp.where(turned, trig[0], 1.0)[None]
    sine = jnp.where(turned, trig[1], 0.0)[None]
    out_ref[:, pl.ds(pl.multiple_of(part * DH, DH), DH), :] = turn_heads(rawT, cosine, sine).astype(bf16)


def qkv_block(lengths, ids, drop, na, w_qkv, b_qkv, chunk, seq_ways):
    frames, width = na.shape
    cols = seq_ways * DH
    chunks = width // cols
    utts = lengths.shape[0]

    def whole(shape):
        return pl.BlockSpec(shape, lambda j, *_: (0,) * len(shape), pipeline_mode=pl.Buffered(1))

    shape = (seq_ways, 3 * DH, frames)
    return pl.pallas_call(
        functools.partial(qkv_kernel, utts, seq_ways),
        out_shape=jax.ShapeDtypeStruct(shape, jnp.bfloat16),
        grid_spec=pltpu.PrefetchScalarGridSpec(
            num_scalar_prefetch=3,
            grid=(3,),
            in_specs=[
                whole(na.shape),
                pl.BlockSpec((width, cols), lambda j, *_: (0, j * chunks + chunk)),
                pl.BlockSpec((1, cols), lambda j, *_: (0, j * chunks + chunk)),
            ],
            out_specs=whole(shape),
            scratch_shapes=[pltpu.VMEM((2, DH // 2, frames), jnp.float32)],
        ),
        cost_estimate=cost(75),
        name="qkv_block",
    )(lengths, ids, drop, na, w_qkv, b_qkv)


def back_kernel(utts, seq_ways, chunk, lengths_ref, ids_ref, drop_ref, grad_ref, naT_ref, w_ref, *refs):
    first = chunk == 0
    acc_in = None if first else refs[0]
    acc_ref, bias_ref, keep_ref, send_ref, trig, grads, sems = refs[0 if first else 3 :]
    f32, bf16 = jnp.float32, jnp.bfloat16
    part = pl.program_id(0)
    width, frames = naT_ref.shape
    core = ids_ref[0]
    parts = keep_ref.shape[0]
    own = width // seq_ways
    rows = own // parts

    @pl.when(part == 0)
    def _():
        _, place = segment_rows(lengths_ref, drop_ref, utts, ids_ref[1] * frames, frames)
        cosine, sine = rotary_rows(place, DH // 2)
        trig[0] = cosine
        trig[1] = sine

    turned = part < 2
    cosine = jnp.where(turned, trig[0], 1.0)[None]
    sine = jnp.where(turned, trig[1], 0.0)[None]
    raw = grad_ref[:, pl.ds(pl.multiple_of(part * DH, DH), DH), :].astype(f32)
    gpT = turn_heads(raw, cosine, -sine).astype(bf16).reshape(seq_ways * DH, frames)
    gna = dot(w_ref[...], gpT)

    @pl.when(part == 0)
    def _():
        acc_ref[...] = gna if first else acc_in[...] + gna

    @pl.when(part > 0)
    def _():
        acc_ref[...] += gna

    ones = jnp.ones((8, frames), bf16)
    bias_ref[0] = dot_nt(ones, gpT)
    grad_w = dot_nt(naT_ref[...], gpT).astype(bf16)
    cols = seq_ways * DH
    at = pl.ds(pl.multiple_of(part * rows, rows), rows)
    for s in range(seq_ways):
        side = jnp.where(core == s % 2, 0, 1)
        for k in range(parts):
            lo = s * own + k * rows
            grads[side, k, s // 2, at, :] = grad_w[lo : lo + rows]

    def copy(side, p):
        where = (slice(None), slice(None), pl.ds(pl.multiple_of(p * rows, rows), rows))
        return pltpu.make_async_copy(
            grads.at[side].at[where],
            (keep_ref, send_ref)[side].at[(*where, pl.ds(chunk * cols, cols))],
            sems.at[side, p],
        )

    for side in (1, 0):
        copy(side, part).start()

    @pl.when(part == 2)
    def _():
        for side in (1, 0):
            for p in range(3):
                copy(side, p).wait()


def back_block(lengths, ids, drop, grad, naT, w_qkv, before, chunk, parts):
    seq_ways, _, frames = grad.shape
    width = naT.shape[0]
    cols = seq_ways * DH
    chunks = width // cols
    utts = lengths.shape[0]
    f32, bf16 = jnp.float32, jnp.bfloat16
    rows = width // seq_ways // parts

    def whole(shape):
        return pl.BlockSpec(shape, lambda j, *_: (0,) * len(shape), pipeline_mode=pl.Buffered(1))

    gspec = pl.BlockSpec(memory_space=pl.ANY)
    gshape = jax.ShapeDtypeStruct((parts, seq_ways // 2, 3 * rows, width), bf16)
    ins = [grad, naT, w_qkv, *before]
    in_specs = [whole(grad.shape), whole(naT.shape)]
    in_specs += [pl.BlockSpec((width, cols), lambda j, *_: (0, j * chunks + chunk))]
    aliases = {}
    if before:
        in_specs += [whole(before[0].shape), gspec, gspec]
        aliases = {7: 2, 8: 3}
    return pl.pallas_call(
        functools.partial(back_kernel, utts, seq_ways, chunk),
        out_shape=[
            jax.ShapeDtypeStruct((width, frames), f32),
            jax.ShapeDtypeStruct((3, 8, cols), f32),
            gshape,
            gshape,
        ],
        grid_spec=pltpu.PrefetchScalarGridSpec(
            num_scalar_prefetch=3,
            grid=(3,),
            in_specs=in_specs,
            out_specs=[
                whole((width, frames)),
                pl.BlockSpec((1, 8, cols), lambda j, *_: (j, 0, 0)),
                gspec,
                gspec,
            ],
            scratch_shapes=[
                pltpu.VMEM((2, DH // 2, frames), f32),
                pltpu.VMEM((2, parts, seq_ways // 2, 3 * rows, cols), bf16),
                pltpu.SemaphoreType.DMA((2, 3)),
            ],
        ),
        compiler_params=pltpu.CompilerParams(vmem_limit_bytes=48 << 20),
        cost_estimate=cost(100),
        input_output_aliases=aliases,
        name="back_block",
    )(lengths, ids, drop, *ins)


def norm_kernel(
    utts, heads_local, lengths_ref, ids_ref, acc_ref, hidden_ref, after_ref, mods_ref, loss_ref, mid_ref, *refs
):
    f32, bf16 = jnp.float32, jnp.bfloat16
    bias_refs, (gh_ref, small_ref) = refs[:heads_local], refs[heads_local:]
    frames, width = hidden_ref.shape
    pad_u = table_rows(utts)
    base = 6 * pad_u
    hot = onehot_rows(lengths_ref, utts, 16, ids_ref[1] * frames, frames)
    cols = frame_columns(hot, jnp.zeros((1, frames), f32))
    madd = mods_operand(mods_ref)
    scale = dot(cols, madd[:, width:])
    gna = acc_ref[...].T
    normed, rstd = norm_stats(hidden_ref[...])
    sums = sum_rows(hot, 16, frames)
    small_ref[0:pad_u, :] = dot(sums, gna.astype(bf16))[:pad_u]
    small_ref[pad_u : 2 * pad_u, :] = dot(sums, (gna * normed).astype(bf16))[:pad_u]
    gh = (after_ref[...] + norm_back(gna * (1.0 + scale), normed, rstd)).astype(bf16)
    gh_ref[...] = gh
    small_ref[2 * pad_u : base, :] = mid_ref[0 : 4 * pad_u, :]
    cols_local = width // heads_local
    for c in range(heads_local):
        for p in range(3):
            small_ref[base + p : base + p + 1, c * cols_local : (c + 1) * cols_local] = bias_refs[c][p, 0:1, :]
    small_ref[base + 3 : base + 4, :] = dot(sums, gh)[16:17]
    small_ref[base + 4 : base + 12, :] = mid_ref[4 * pad_u : 4 * pad_u + 8, :]
    count = jnp.sum(loss_ref[...].astype(f32), axis=1, keepdims=True)
    small_ref[base + 12 : base + 16, :] = jnp.broadcast_to(count, (4, width))


def norm_block(lengths, ids, acc, hidden, after, mods, loss, mid_small, biases):
    frames, width = hidden.shape
    utts = lengths.shape[0]
    out_shape = [
        jax.ShapeDtypeStruct((frames, width), jnp.bfloat16),
        jax.ShapeDtypeStruct((6 * table_rows(utts) + 16, width), jnp.float32),
    ]
    return pl.pallas_call(
        functools.partial(norm_kernel, utts, len(biases)),
        out_shape=out_shape,
        grid_spec=pltpu.PrefetchScalarGridSpec(
            num_scalar_prefetch=2,
            grid=(1,),
            in_specs=[whole_block(a.shape) for a in (acc, hidden, after, mods, loss, mid_small, *biases)],
            out_specs=[whole_block(o.shape) for o in out_shape],
        ),
        compiler_params=pltpu.CompilerParams(vmem_limit_bytes=48 << 20),
        cost_estimate=cost(50),
        name="norm_block",
    )(lengths, ids, acc, hidden, after, mods, loss, mid_small, *biases)


def skip_kernel(seq_ways, ids_ref, joinedT_ref, gh_ref, keep_ref, send_ref, grads, sems):
    step = pl.program_id(0)
    core = ids_ref[0]
    parts = keep_ref.shape[0]
    width = joinedT_ref.shape[0]
    block = 2 * width // seq_ways
    rows = block // parts
    z_step = seq_ways // 4
    grad_w = dot(joinedT_ref[...], gh_ref[...]).astype(jnp.bfloat16)
    for b in range(width // block):
        side = jnp.where(core == b % 2, 0, 1)
        for k in range(parts):
            lo = b * block + k * rows
            grads[side, k, step * z_step + b // 2] = grad_w[lo : lo + rows]

    def copy(side, at):
        where = (slice(None), pl.ds(at * z_step, z_step))
        return pltpu.make_async_copy(
            grads.at[side].at[where], (keep_ref, send_ref)[side].at[where], sems.at[side, at]
        )

    for side in (1, 0):
        copy(side, step).start()

    @pl.when(step == 1)
    def _():
        for side in (1, 0):
            for at in range(2):
                copy(side, at).wait()


def skip_block(ids, joinedT, gh, seq_ways, parts):
    frames, width = gh.shape
    rows = 2 * width // seq_ways // parts
    gshape = (parts, seq_ways // 2, rows, width)
    return pl.pallas_call(
        functools.partial(skip_kernel, seq_ways),
        out_shape=[jax.ShapeDtypeStruct(gshape, jnp.bfloat16)] * 2,
        grid_spec=pltpu.PrefetchScalarGridSpec(
            num_scalar_prefetch=1,
            grid=(2,),
            in_specs=[pl.BlockSpec((width, frames), lambda j, *_: (j, 0)), whole_block(gh.shape)],
            out_specs=[pl.BlockSpec(memory_space=pl.ANY)] * 2,
            scratch_shapes=[pltpu.VMEM((2,) + gshape, jnp.bfloat16), pltpu.SemaphoreType.DMA((2, 2))],
        ),
        compiler_params=pltpu.CompilerParams(vmem_limit_bytes=32 << 20),
        cost_estimate=cost(50),
        name="skip_block",
    )(ids, joinedT, gh)


def joined_kernel(gh_ref, w_ref, scale_ref, first_ref, second_ref):
    step = pl.program_id(0)
    value = dot_nt(gh_ref[...], w_ref[...]) * scale_ref[0:1, 0:1]

    @pl.when(step == 0)
    def _():
        first_ref[...] = value

    @pl.when(step == 1)
    def _():
        second_ref[...] = value


def joined_block(gh, w_skip, scale):
    frames, width = gh.shape
    out = jax.ShapeDtypeStruct((frames, width), jnp.float32)
    return pl.pallas_call(
        joined_kernel,
        out_shape=[out, out],
        grid_spec=pltpu.PrefetchScalarGridSpec(
            num_scalar_prefetch=0,
            grid=(2,),
            in_specs=[
                whole_block(gh.shape),
                pl.BlockSpec((width, width), lambda j: (j, 0)),
                whole_block(scale.shape),
            ],
            out_specs=[whole_block(out.shape)] * 2,
        ),
        compiler_params=pltpu.CompilerParams(vmem_limit_bytes=32 << 20),
        cost_estimate=cost(50),
        name="joined_block",
    )(gh, w_skip, scale)


def add_bf16(left, right):
    return (left.astype(jnp.float32) + right.astype(jnp.float32)).astype(jnp.bfloat16)


def first_kernel(pairs, splits, ids_ref, *refs):
    ins, outs = refs[: 8 * pairs], list(refs[8 * pairs :])
    for i in range(4):
        own = [outs.pop(0) for _ in range(splits if i < 2 else 1)]
        at = 0
        for p in range(pairs):
            left, right = ins[2 * (i * pairs + p)], ins[2 * (i * pairs + p) + 1]
            rows = left.shape[-2]
            value = add_bf16(left[0, 0, 0], right[0, 0, 0])
            if len(own) == 1:
                own[0][0, :, at : at + rows, :] = value
            else:
                for out in own:
                    out[0] = value[:, at : at + out.shape[2], :]
                    at += out.shape[2]
            at += rows


def first_sum(ids, pairs, splits):
    _, _, _, z_ways, _, width = pairs[0][0].shape
    total = sum(k.shape[4] for k, _ in pairs)
    step = 1 if total > 100 else z_ways

    def source(half, axis, mine, rows):
        def at(g, z, ids):
            bit = ids[axis]
            return half, bit if mine else 1 - bit, g, z, 0, 0

        return pl.BlockSpec((1, 1, 1, step, rows, width), at)

    order = [(0, 2, False), (1, 3, False), (0, 2, True), (1, 3, True)]
    sizes = [*splits, *splits, total, total]
    return pl.pallas_call(
        functools.partial(first_kernel, len(pairs), len(splits)),
        out_shape=[jax.ShapeDtypeStruct((2, z_ways, n, width), jnp.bfloat16) for n in sizes],
        grid_spec=pltpu.PrefetchScalarGridSpec(
            num_scalar_prefetch=1,
            grid=(2, z_ways // step),
            in_specs=[source(*o, a.shape[4]) for o in order for pair in pairs for a in pair],
            out_specs=[pl.BlockSpec((1, step, n, width), lambda g, z, ids: (g, z, 0, 0)) for n in sizes],
        ),
        compiler_params=pltpu.CompilerParams(vmem_limit_bytes=48 << 20),
        cost_estimate=cost(60),
        name="first_sum",
    )(ids, *([a for pair in pairs for a in pair] * 4))


def second_kernel(pieces, ids_ref, *refs):
    for i in range(4):
        keep, *got = refs[(pieces + 1) * i : (pieces + 1) * (i + 1)]
        out = refs[4 * (pieces + 1) + i]
        at = 0
        for g in got:
            rows = g.shape[2]
            out[:, at : at + rows, :] = add_bf16(keep[0, :, at : at + rows, :], g[0])
            at += rows


def second_sum(ids, keep_a, got_a, keep_b, got_b):
    _, z_ways, rows, width = keep_a.shape
    step = z_ways // 2 if rows > 100 else z_ways

    def source(axis, mine, value):
        def at(z, ids):
            bit = ids[axis]
            return bit if mine else 1 - bit, z, 0, 0

        return pl.BlockSpec((1, step, *value.shape[2:]), at)

    order = [(3, False), (2, False), (3, True), (2, True)]
    sides = [[keep_a, *got_a], [keep_b, *got_b]]
    out = jax.ShapeDtypeStruct((z_ways, rows, width), jnp.bfloat16)
    return pl.pallas_call(
        functools.partial(second_kernel, len(got_a)),
        out_shape=[out] * 4,
        grid_spec=pltpu.PrefetchScalarGridSpec(
            num_scalar_prefetch=1,
            grid=(z_ways // step,),
            in_specs=[source(*o, v) for i, o in enumerate(order) for v in sides[i % 2]],
            out_specs=[pl.BlockSpec((step, rows, width), lambda z, ids: (z, 0, 0))] * 4,
        ),
        compiler_params=pltpu.CompilerParams(vmem_limit_bytes=48 << 20),
        cost_estimate=cost(30),
        name="second_sum",
    )(ids, *((sides[0] + sides[1]) * 2))


def third_kernel(ids_ref, keep_a, got_a, keep_b, got_b, *outs):
    for j, out in enumerate(outs):
        at = ids_ref[4] ^ j
        out[0] = add_bf16(keep_a[at], got_a[at])
        out[1] = add_bf16(keep_b[at], got_b[at])


def third_sum(ids, keep_a, got_a, keep_b, got_b):
    z_ways, rows, width = keep_a.shape
    out = jax.ShapeDtypeStruct((2, rows, width), jnp.bfloat16)
    return pl.pallas_call(
        third_kernel,
        out_shape=[out] * z_ways,
        grid_spec=pltpu.PrefetchScalarGridSpec(
            num_scalar_prefetch=1,
            grid=(1,),
            in_specs=[whole_block(keep_a.shape)] * 4,
            out_specs=[whole_block(out.shape)] * z_ways,
        ),
        cost_estimate=cost(10),
        name="third_sum",
    )(ids, keep_a, got_a, keep_b, got_b)


def third_all_kernel(ids_ref, keep_a, got_a, keep_b, got_b, out):
    for z in range(keep_a.shape[0]):
        out[z, 0] = add_bf16(keep_a[z], got_a[z])
        out[z, 1] = add_bf16(keep_b[z], got_b[z])


def third_sum_all(ids, keep_a, got_a, keep_b, got_b):
    z_ways, rows, width = keep_a.shape
    out = jax.ShapeDtypeStruct((z_ways, 2, rows, width), jnp.bfloat16)
    step = max(1, z_ways // 2)
    return pl.pallas_call(
        third_all_kernel,
        out_shape=out,
        grid_spec=pltpu.PrefetchScalarGridSpec(
            num_scalar_prefetch=1,
            grid=(z_ways // step,),
            in_specs=[pl.BlockSpec((step, rows, width), lambda i, *_: (i, 0, 0))] * 4,
            out_specs=pl.BlockSpec((step, 2, rows, width), lambda i, *_: (i, 0, 0, 0)),
        ),
        cost_estimate=cost(10),
        name="third_sum_all",
    )(ids, keep_a, got_a, keep_b, got_b)


def fourth_all_kernel(x, out):
    total = x[0].astype(jnp.float32)
    for z in range(1, x.shape[0]):
        total = total + x[z].astype(jnp.float32)
    out[...] = total.astype(jnp.bfloat16)


def fourth_sum_all(terms):
    return pl.pallas_call(
        fourth_all_kernel,
        out_shape=jax.ShapeDtypeStruct(terms.shape[1:], jnp.bfloat16),
        grid=(1,),
        in_specs=[whole_block(terms.shape)],
        out_specs=whole_block(terms.shape[1:]),
        cost_estimate=cost(10),
        name="fourth_sum_all",
    )(terms)


def fourth_kernel(*refs):
    total = refs[0][...].astype(jnp.float32)
    for r in refs[1:-1]:
        total = total + r[...].astype(jnp.float32)
    refs[-1][...] = total.astype(jnp.bfloat16)


def fourth_sum(terms):
    shape = terms[0].shape
    return pl.pallas_call(
        fourth_kernel,
        out_shape=jax.ShapeDtypeStruct(shape, jnp.bfloat16),
        grid=(1,),
        in_specs=[whole_block(shape)] * len(terms),
        out_specs=whole_block(shape),
        cost_estimate=cost(10),
        name="fourth_sum",
    )(*terms)


def place_kernel(streams, plan, ids_ref, scale_ref, *refs):
    blocks, outs = refs[: 4 * streams], refs[4 * streams :]
    x, y = ids_ref[2], ids_ref[3]
    scale = scale_ref[0:1, 0:1]
    for stream, row, rows, lane, lanes, out, row_of, lane_of in plan:
        for d in range(4):
            own_x, own_y = x ^ (d & 1), y ^ (d >> 1)
            for half in range(2):
                k = own_x * 2 + own_y if half == 0 else 4 + own_y * 2 + own_x
                tile = blocks[4 * stream + d][half, row : row + rows, lane : lane + lanes]
                outs[out][row_of(k), lane_of(k)] = tile.astype(jnp.float32) * scale


def place_blocks(ids, scale, streams, plan, shapes):
    blocks = [b for s in streams for b in s]
    outs = [jax.ShapeDtypeStruct(s, jnp.float32) for s in shapes]
    return pl.pallas_call(
        functools.partial(place_kernel, len(streams), plan),
        out_shape=outs,
        grid_spec=pltpu.PrefetchScalarGridSpec(
            num_scalar_prefetch=1,
            grid=(1,),
            in_specs=[whole_block(a.shape) for a in (scale, *blocks)],
            out_specs=[whole_block(o.shape) for o in outs],
        ),
        compiler_params=pltpu.CompilerParams(vmem_limit_bytes=32 << 20),
        cost_estimate=cost(20),
        name="place_blocks",
    )(ids, scale, *blocks)


def span(start, size):
    return pl.ds(pl.multiple_of(start, size), size)


def ada_kernel(groups, pad_u, numerator, time_ref, *refs):
    f32 = jnp.float32
    parts, (weight_ref, vector_ref, scale_ref) = refs[:groups], refs[groups:]
    table = pl.program_id(0)
    base = 6 * pad_u
    count = parts[0][base + 12 : base + 13, 0:1]
    for p in parts[1:]:
        count = count + p[base + 12 : base + 13, 0:1]
    scale = numerator / count
    rows = jnp.concatenate([p[pl.ds(pl.multiple_of(table * pad_u, 8), pad_u), :] for p in parts], axis=0) * scale
    vector_ref[pl.ds(table, 1), :] = jnp.sum(rows, axis=0, keepdims=True)
    operand = jnp.concatenate(list(split3(rows)), axis=0)
    weight_ref[...] = dot(time_ref[...], operand)

    @pl.when(table == 0)
    def _():
        total = parts[0][base : base + 16, :]
        for p in parts[1:]:
            total = total + p[base : base + 16, :]
        vector_ref[8:24, :] = total * scale
        scale_ref[...] = jnp.broadcast_to(scale, scale_ref.shape)


def ada_block(time3, parts, utts, numerator):
    pad_u = table_rows(utts)
    width = parts[0].shape[1]
    own = time3.shape[0]
    f32 = jnp.float32
    return pl.pallas_call(
        functools.partial(ada_kernel, len(parts), pad_u, numerator),
        out_shape=[
            jax.ShapeDtypeStruct((own, 6 * width), f32),
            jax.ShapeDtypeStruct((24, width), f32),
            jax.ShapeDtypeStruct((8, 128), f32),
        ],
        grid=(6,),
        in_specs=[whole_block(time3.shape)] + [whole_block(p.shape) for p in parts],
        out_specs=[
            pl.BlockSpec((own, width), lambda j: (0, j)),
            whole_block((24, width)),
            whole_block((8, 128)),
        ],
        cost_estimate=cost(50),
        name="ada_block",
    )(time3, *parts)


def sum_exchange(value, axis, bit):
    ways = lax.axis_size(axis)
    return lax.ppermute(value, axis, [(i, i ^ bit) for i in range(ways)])


def axis_bits(ways):
    return [1 << i for i in range(ways.bit_length() - 1)]


def reduce_stages(ids, blocks, splits, whole_z):
    batch_ways = lax.axis_size("batch")
    x_bit, y_bit = 1, 1 << ((batch_ways.bit_length() - 1) // 2)
    pairs = []
    for keep, send in blocks:
        shape = (2, 2, 2) + keep.shape[1:]
        pairs.append((keep.reshape(shape), sum_exchange(send, "seq", 1).reshape(shape)))
    *sends, keep_a, keep_b = first_sum(ids, pairs, splits)
    sends = follow(sends, (yield sends))
    got, token = [[], []], None
    for i in range(len(splits)):
        pieces = follow([sends[i], sends[len(splits) + i]], token)
        for side, bit in enumerate((x_bit, y_bit)):
            got[side].append(sum_exchange(pieces[side], "batch", bit))
        token = yield [got[0][i], got[1][i]]
    got_a, got_b = (follow(g, token) for g in got)
    send_a, send_b, keep_a, keep_b = second_sum(ids, keep_a, got_a, keep_b, got_b)
    send_a, send_b = follow([send_a, send_b], (yield [send_a, send_b]))
    got = [sum_exchange(send_a, "batch", y_bit), sum_exchange(send_b, "batch", x_bit)]
    got_a, got_b = follow(got, (yield got))
    if whole_z:
        ways = lax.axis_size("seq")
        groups = [list(range(c, ways, 2)) for c in range(2)]
        away = [third_sum_all(ids, keep_a, got_a, keep_b, got_b)]
        away = follow(away, (yield away))
        got = [lax.all_to_all(away[0], "seq", 0, 0, axis_index_groups=groups, tiled=True)]
        got = follow(got, (yield got))
        block = fourth_sum_all(got[0])
    else:
        own, *away = third_sum(ids, keep_a, got_a, keep_b, got_b)
        away = follow(away, (yield away))
        got = [sum_exchange(a, "seq", 2 * (j + 1)) for j, a in enumerate(away)]
        got = follow(got, (yield got))
        block = fourth_sum([own] + got)
    for bit in axis_bits(batch_ways):
        if bit not in (x_bit, y_bit):
            block = add_bf16(block, sum_exchange(block, "batch", bit))
    (block,) = follow([block], (yield [block]))
    yield [block] + [sum_exchange(block, "batch", bit) for bit in (x_bit, y_bit, x_bit | y_bit)]


def advance(stages, steps, token=None):
    value = next(stages) if token is None else stages.send(token)
    for _ in range(steps - 1):
        value = next(stages)
    return value


def last_stage(stages, token=None):
    value = stages.send(token)
    for value in stages:
        pass
    return value


def follow(values, token):
    return values if token is None else [after(v, token) for v in values]


def after(value, *others):
    return lax.optimization_barrier((value,) + others)[0]


def gather_groups(value):
    return [value] + [sum_exchange(value, "batch", i) for i in range(1, lax.axis_size("batch"))]


def sum_seq(value):
    for bit in axis_bits(lax.axis_size("seq")):
        value = value + sum_exchange(value, "seq", bit)
    return value


def shards(
    tokens_in,
    skip_in,
    condition,
    cotangent,
    time_embed,
    lengths,
    key_mask,
    drop_mask,
    loss_mask,
    w_skip,
    b_skip,
    w_ada,
    b_ada,
    w_qkv,
    b_qkv,
    w_out,
    b_out,
    w_up,
    b_up,
    w_down,
    b_down,
):
    f32, bf16 = jnp.float32, jnp.bfloat16
    seq_ways, batch_ways = lax.axis_size("seq"), lax.axis_size("batch")
    seq_rank = lax.axis_index("seq")
    frames, width = tokens_in.shape[1:]
    group_frames = frames * seq_ways
    heads_local = HEADS // seq_ways
    utts = lengths.shape[1]
    lengths_row, drop = lengths[0], drop_mask[0]
    batch_rank = lax.axis_index("batch")
    side = 1 << ((batch_ways.bit_length() - 1) // 2)
    ids = [lax.rem(seq_rank, 2), seq_rank, lax.rem(batch_rank, 2), lax.rem(batch_rank // side, 2), seq_rank // 2]
    ids = jnp.stack(ids).astype(jnp.int32)
    ok = key_mask.reshape(seq_ways, 1, frames)
    exchange = functools.partial(lax.all_to_all, axis_name="seq", split_axis=0, concat_axis=0, tiled=True)

    time_act = jax.nn.silu(time_embed[0]).astype(bf16)
    time_rows = jnp.pad(time_act, ((0, 16 - utts), (0, 0)))

    def modulation(first, last):
        return jnp.dot(time_rows, w_ada[:, first:last], preferred_element_type=f32) + b_ada[
            first:last
        ].astype(f32)

    mods_a = modulation(0, 2 * width)
    hidden, joinedT, naT, na = head_block(
        lengths_row, ids, drop, tokens_in[0], skip_in[0], condition[0], mods_a, w_skip, b_skip[None]
    )
    mods_rest = modulation(2 * width, 6 * width)
    received = []
    for c in range(heads_local):
        packed = qkv_block(lengths_row, ids, drop, na, w_qkv, b_qkv[None], c, seq_ways)
        if c == 0:
            na = after(na, mods_rest)
        received.append(exchange(packed))

    own = width // seq_ways
    pad_u = table_rows(utts)
    time_own = lax.dynamic_slice_in_dim(jnp.concatenate(gather_groups(time_rows[:pad_u])), seq_rank * own, own, axis=1)
    time3 = jnp.tile(time_own.T, (1, 3))

    received[0] = after(received[0], mods_rest)
    head_out, log_totals, returned = [], [], []
    for c in range(heads_local):
        out, log_total = attend(lengths_row, received[c], ok)
        head_out.append(out)
        log_totals.append(log_total)
        returned.append(exchange(after(out, *returned)))
        if c < heads_local - 1:
            received[c + 1] = after(received[c + 1], out, time3)
    mid = mid_block(
        lengths_row,
        ids,
        returned,
        hidden,
        mods_rest,
        cotangent[0],
        loss_mask,
        w_out,
        b_out[None],
        w_up,
        b_up[None],
        w_down,
        b_down[None],
        PARTS,
    )
    output, after_grad, mid_small, grad_att, keep, send = mid
    grad_heads = exchange(grad_att)
    front = keep.shape[2] * 4 // 9 // 16 * 16
    feed = reduce_stages(ids, [(keep, send)], [front, keep.shape[2] - front], True)

    ahead = next(feed)
    grad_local = []
    for c in range(heads_local):
        operand = after(grad_heads, *ahead)
        moving = feed.send(grad if c else None) if c < 2 else []
        grad = attend_back(lengths_row, received[c], ok, head_out[c], operand, log_totals[c], c)
        grad_local.append(exchange(after(grad, *moving)))
        ahead = [grad]
    if heads_local == 1:
        next(feed)
    ahead = ahead + advance(feed, 1, ahead[0])
    before, biases = (), []
    for c in range(heads_local):
        acc, bias, keep, send = back_block(
            lengths_row, ids, drop, after(grad_local[c], *ahead), naT, w_qkv, before, c, PARTS
        )
        before = (acc, keep, send)
        biases.append(bias)
        ahead = next(feed) and advance(feed, 1, acc) if c == 0 else []
    moving = next(feed)
    gh, small = norm_block(lengths_row, ids, acc, hidden, after_grad, mods_a, loss_mask, mid_small, biases)
    rest = reduce_stages(ids, [skip_block(ids, joinedT, gh, seq_ways, PARTS), (keep, send)], [5 * own // PARTS], False)
    small = after(small, *moving, *advance(rest, 3))
    token = advance(rest, 2)[0]
    groups = gather_groups(sum_seq(small))
    numerator = float(group_frames * batch_ways)
    grad_w_ada, vectors, scale = ada_block(time3, groups, utts, numerator)
    grad_tokens, grad_skip = joined_block(gh, w_skip, scale)
    next(feed)
    feed = last_stage(feed, token)
    rest = last_stage(rest)

    ff = w_up.shape[1]
    chunks = ff // width
    up_part = chunks * own // PARTS
    down_part = ff // seq_ways // PARTS
    out_part = own // PARTS
    per_chunk = own // up_part
    whole_lanes = lambda k: span(0, width)
    grad_w_up, grad_w_down, grad_w_out = place_blocks(
        ids,
        scale,
        [feed],
        [
            (
                *(0, 0, up_part, 0, width, 0),
                lambda k: span(lax.rem(k, per_chunk) * up_part, up_part),
                lambda k: span(k // per_chunk * width, width),
            ),
            (0, up_part, down_part, 0, width, 1, lambda k: span(k * down_part, down_part), whole_lanes),
            (0, up_part + down_part, out_part, 0, width, 2, lambda k: span(k * out_part, out_part), whole_lanes),
        ],
        [(own, ff), (ff // seq_ways, width), (own, width)],
    )
    skip_part = 2 * own // PARTS
    grad_w_skip, grad_w_qkv = place_blocks(
        ids,
        scale,
        [rest],
        [(0, 0, skip_part, 0, width, 0, lambda k: span(k * skip_part, skip_part), whole_lanes)]
        + [
            (
                *(0, skip_part + p * out_part, out_part, 0, width, 1),
                lambda k: span(k * out_part, out_part),
                lambda k, at=p * width: span(at, width),
            )
            for p in range(3)
        ],
        [(2 * own, width), (own, 3 * width)],
    )

    def own_slice(vector):
        vector = vector.reshape(-1)
        size = vector.shape[0] // seq_ways
        return lax.dynamic_slice_in_dim(vector, seq_rank * size, size)

    grad_b_ada = own_slice(vectors[:6])
    grad_b_qkv = own_slice(vectors[8:11])
    grad_b_skip = own_slice(vectors[11])
    grad_b_out = own_slice(vectors[12])
    grad_b_down = own_slice(vectors[13])
    grad_b_up = own_slice(vectors[14 : 14 + chunks])
    return (
        output[None],
        grad_tokens[None],
        grad_skip[None],
        grad_w_skip,
        grad_b_skip,
        grad_w_ada,
        grad_b_ada,
        grad_w_qkv,
        grad_b_qkv,
        grad_w_out,
        grad_b_out,
        grad_w_up,
        grad_b_up,
        grad_w_down,
        grad_b_down,
    )


def solution(mesh):
    in_specs = (
        P("batch", "seq", None),
        P("batch", "seq", None),
        P("batch", "seq", None),
        P("batch", "seq", None),
        P("batch", None, None),
        P("batch", None),
        P("batch", None),
        P("batch", None),
        P("batch", "seq"),
        P(),
        P(),
        P(),
        P(),
        P(),
        P(),
        P(),
        P(),
        P(),
        P(),
        P(),
        P(),
    )
    out_specs = (
        P("batch", "seq", None),
        P("batch", "seq", None),
        P("batch", "seq", None),
        P("seq", None),
        P("seq"),
        P("seq", None),
        P("seq"),
        P("seq", None),
        P("seq"),
        P("seq", None),
        P("seq"),
        P("seq", None),
        P("seq"),
        P("seq", None),
        P("seq"),
    )
    return jax.shard_map(shards, mesh=mesh, in_specs=in_specs, out_specs=out_specs, check_vma=False)
```

profile of v0, /device:TPU:0, one launch (start us, length us, event | category | flops | bytes accessed | tf_op | source)
XLA Modules:
  0.0 538.9 jit_solution(7562498536897563364)
XLA Ops:
  7.3 8.0 %head_block.1 = (f32[512,1024]{1,0:T(8,128)}, bf16[2048,512]{1,0:T(8,128)(2,1)}, bf16[1024,512]{1,0:T(8,128)(2,1)S(1)}, bf16[512,1024]{1,0:T(8,128)(2,1)S(1)}) custom-call(s32[8]{0:T(128)S(1)} %bitcast.67, s32[5]{0:T(128)S(1)} %stack.23.ids_ref, s32[8]{0:T(128)S(1)} %bitcast.57, bf16[512,1024]{1,0:T(8,128)(2,1)S(1)} %bitcast.52, ...), custom_call_target="tpu_custom_call" | custom-call | flops 10000000000 | bytes 10000000 | tf_op jit(solution)/shard_map/head_block/pallas_call | solution.py:676
  17.2 6.7 %qkv_block.2 = bf16[8,192,512]{2,1,0:T(8,128)(2,1)} custom-call(s32[8]{0:T(128)} %bitcast.60, s32[5]{0:T(128)} %copy-done.4, s32[8]{0:T(128)} %bitcast.55, bf16[512,1024]{1,0:T(8,128)(2,1)} %copy-done.28, bf16[1024,3072]{1,0:T(8,128)(2,1)} %w_ref.8, bf16[1,3072]{1,0:T(2,128)(2,1)} %broadcast_in_dim.28.b_ref), custom_call_target="tpu_custom_call" | custom-call | flops 7500000256 | bytes 7500000 | tf_op jit(solution)/shard_map/qkv_block/pallas_call | solution.py:729
  24.0 6.5 %all-to-all-start = ((bf16[8,192,512]{2,1,0:T(8,128)(2,1)}), bf16[8,192,512]{2,1,0:T(8,128)(2,1)S(1)}, u32[]{:S(2)}, u32[]{:S(2)}) async-start(bf16[8,192,512]{2,1,0:T(8,128)(2,1)} %qkv_block.2), calls=%async_computation | async-start | bytes 3145728 | tf_op jit(solution)/shard_map/all_to_all | solution.py:1399
  30.4 5.3 fusion.2.refs_3_
  35.7 6.8 %qkv_block.3 = bf16[8,192,512]{2,1,0:T(8,128)(2,1)} custom-call(s32[8]{0:T(128)} %bitcast.61, s32[5]{0:T(128)} %copy-done.4, s32[8]{0:T(128)} %bitcast.56, bf16[512,1024]{1,0:T(8,128)(2,1)} %copy-done.28, bf16[1024,3072]{1,0:T(8,128)(2,1)} %w_ref.8, bf16[1,3072]{1,0:T(2,128)(2,1)} %broadcast_in_dim.28.b_ref), custom_call_target="tpu_custom_call" | custom-call | flops 7500000256 | bytes 7500000 | tf_op jit(solution)/shard_map/qkv_block/pallas_call | solution.py:729
  42.5 25.8 %all-to-all-done.qkv_ref = bf16[8,192,512]{2,1,0:T(8,128)(2,1)S(1)} async-done(((bf16[8,192,512]{2,1,0:T(8,128)(2,1)}), bf16[8,192,512]{2,1,0:T(8,128)(2,1)S(1)}, u32[]{:S(2)}, u32[]{:S(2)}) %all-to-all-start) | async-done | bytes 1572896 | tf_op jit(solution)/shard_map/all_to_all | solution.py:1399
  79.6 24.8 %attend.2 = (bf16[8,64,512]{2,1,0:T(8,128)(2,1)}, f32[8,1,512]{2,1,0:T(1,128)}) custom-call(s32[8]{0:T(128)} %bitcast.62, bf16[8,192,512]{2,1,0:T(8,128)(2,1)} %copy-done.35, s32[8,1,512]{2,1,0:T(1,128)} %bitcast.82), custom_call_target="tpu_custom_call" | custom-call | flops 24999999488 | bytes 25000000 | tf_op jit(solution)/shard_map/attend/pallas_call | solution.py:135
  113.8 25.0 %attend.3 = (bf16[8,64,512]{2,1,0:T(8,128)(2,1)}, f32[8,1,512]{2,1,0:T(1,128)}) custom-call(s32[8]{0:T(128)} %bitcast.63, bf16[8,192,512]{2,1,0:T(8,128)(2,1)} %copy-done.34, s32[8,1,512]{2,1,0:T(1,128)} %bitcast.83), custom_call_target="tpu_custom_call" | custom-call | flops 24999999488 | bytes 25000000 | tf_op jit(solution)/shard_map/attend/pallas_call | solution.py:135
  138.8 5.2 all-to-all-start.3
  145.8 13.6 %all-to-all-done.3.refs_1_ = bf16[8,64,512]{2,1,0:T(8,128)(2,1)} async-done(((bf16[8,64,512]{2,1,0:T(8,128)(2,1)}), bf16[8,64,512]{2,1,0:T(8,128)(2,1)}, u32[]{:S(2)}, u32[]{:S(2)}) %all-to-all-start.3) | async-done | bytes 524320 | tf_op jit(solution)/shard_map/all_to_all | solution.py:1412
  159.4 50.9 %mid_block.1 = (bf16[512,1024]{1,0:T(8,128)(2,1)}, f32[512,1024]{1,0:T(8,128)}, f32[40,1024]{1,0:T(8,128)}, bf16[8,128,512]{2,1,0:T(8,128)(2,1)}, bf16[8,4,144,1...) custom-call(s32[8]{0:T(128)} %bitcast.64, s32[5]{0:T(128)} %copy-done.4, bf16[8,64,512]{2,1,0:T(8,128)(2,1)} %copy-done.38, ...), custom_call_target="tpu_custom_call" | custom-call | flops 49999998976 | bytes 50000000 | tf_op jit(solution)/shard_map/mid_block/pallas_call | solution.py:547
  214.9 10.5 %collective-permute-done.3 = bf16[8,4,144,1024]{3,2,1,0:T(8,128)(2,1)} collective-permute-done((bf16[8,4,144,1024]{3,2,1,0:T(8,128)(2,1)}, bf16[8,4,144,1024]{3,2,1,0:T(8,128)(2,1)}, u32[]{:S(2)}, u32[]{:S(2)}) %collective-permute-start.3) | collective-permute-done | bytes 9437216 | tf_op jit(solution)/shard_map/ppermute | solution.py:1263
  225.4 11.3 %first_sum.2 = (bf16[2,4,64,1024]{3,2,1,0:T(8,128)(2,1)}, bf16[2,4,80,1024]{3,2,1,0:T(8,128)(2,1)S(1)}, bf16[2,4,64,1024]{3,2,1,0:T(8,128)(2,1)}, bf16[2,4,80,10...) custom-call(s32[5]{0:T(128)S(1)} %copy-done.5, ...), custom_call_target="tpu_custom_call" | custom-call | flops 6000000000 | bytes 6000000 | tf_op jit(solution)/shard_map/first_sum/pallas_call | solution.py:1037
  242.0 32.2 %attend_back.2 = bf16[8,192,512]{2,1,0:T(8,128)(2,1)} custom-call(s32[8]{0:T(128)} %bitcast.65, bf16[8,192,512]{2,1,0:T(8,128)(2,1)} %copy-done.35, s32[8,1,512]{2,1,0:T(1,128)} %bitcast.84, bf16[8,64,512]{2,1,0:T(8,128)(2,1)} %get-tuple-element.95.o_ref, bf16[8,128,512]{2,1,0:T(8,128)(2,1)} %all-to-all-done.4.do_ref, f32[8,1,512]{2,1,0:T(1,128)} %get-tuple-element.110.lse_ref), custom_call_target="tpu_custom_call" | custom-call | flops 32000000000 | bytes 32000000 | tf_op jit(solution)/shard_map/attend_back/pallas_call | solution.py:257
  283.7 32.1 %attend_back.3 = bf16[8,192,512]{2,1,0:T(8,128)(2,1)} custom-call(s32[8]{0:T(128)} %bitcast.66, bf16[8,192,512]{2,1,0:T(8,128)(2,1)} %copy-done.34, s32[8,1,512]{2,1,0:T(1,128)} %bitcast.85, bf16[8,64,512]{2,1,0:T(8,128)(2,1)} %get-tuple-element.99.o_ref, bf16[8,128,512]{2,1,0:T(8,128)(2,1)} %all-to-all-done.4.do_ref, f32[8,1,512]{2,1,0:T(1,128)} %get-tuple-element.112.lse_ref), custom_call_target="tpu_custom_call" | custom-call | flops 32000000000 | bytes 32000000 | tf_op jit(solution)/shard_map/attend_back/pallas_call | solution.py:257
  315.8 5.7 %all-to-all-done.6.grad_ref = bf16[8,192,512]{2,1,0:T(8,128)(2,1)} async-done(((bf16[8,192,512]{2,1,0:T(8,128)(2,1)}), bf16[8,192,512]{2,1,0:T(8,128)(2,1)}, u32[]{:S(2)}, u32[]{:S(2)}) %all-to-all-start.6) | async-done | bytes 1572896 | tf_op jit(solution)/shard_map/all_to_all | solution.py:1442
  331.9 9.1 %back_block.2 = (f32[1024,512]{1,0:T(8,128)S(1)}, f32[3,8,512]{2,1,0:T(8,128)S(1)}, bf16[8,4,48,1024]{3,2,1,0:T(8,128)(2,1)}, bf16[8,4,48,1024]{3,2,1,0:T(8,128)(2,1)}) custom-call(s32[8]{0:T(128)S(1)} %bitcast.68, s32[5]{0:T(128)S(1)} %copy-done.5, s32[8]{0:T(128)S(1)} %bitcast.58, bf16[8,192,512]{2,1,0:T(8,128)(2,1)} %all-to-all-done.6.grad_ref, ...), custom_call_target="tpu_custom_call" | custom-call | flops 10000000000 | bytes 10000000 | tf_op jit(solution)/shard_map/back_block/pallas_call | solution.py:832
  342.3 17.8 %collective-permute-done.9.got_b = bf16[4,144,1024]{2,1,0:T(8,128)(2,1)S(1)} collective-permute-done((bf16[4,144,1024]{2,1,0:T(8,128)(2,1)S(1)}, bf16[4,144,1024]{2,1,0:T(8,128)(2,1)S(1)}, u32[]{:S(2)}, u32[]{:S(2)}) %collective-permute-start.9) | collective-permute-done | bytes 1179680 | tf_op jit(solution)/shard_map/ppermute | solution.py:1263
  366.0 10.0 %back_block.3 = (f32[1024,512]{1,0:T(8,128)S(1)}, f32[3,8,512]{2,1,0:T(8,128)S(1)}, bf16[8,4,48,1024]{3,2,1,0:T(8,128)(2,1)}, bf16[8,4,48,1024]{3,2,1,0:T(8,128)(2,1)}) custom-call(s32[8]{0:T(128)S(1)} %bitcast.69, s32[5]{0:T(128)S(1)} %copy-done.6, s32[8]{0:T(128)S(1)} %bitcast.59, ...), custom_call_target="tpu_custom_call", output_to_operand_aliasing={{2}: (7, {}), {3}: (8, {})} | custom-call | flops 10000000000 | bytes 10000000 | tf_op jit(solution)/shard_map/back_block/pallas_call | solution.py:832
  391.1 5.4 %first_sum.3 = (bf16[2,4,80,1024]{3,2,1,0:T(8,128)(2,1)S(1)}, bf16[2,4,80,1024]{3,2,1,0:T(8,128)(2,1)S(1)}, bf16[2,4,80,1024]{3,2,1,0:T(8,128)(2,1)S(1)}, bf16[2,4,80,1024]{3,2,1,0:T(8,128)(2,1)S(1)}) custom-call(s32[5]{0:T(128)S(1)} %copy-done.6, bf16[2,2,2,4,32,1024]{5,4,3,2,1,0:T(8,128)(2,1)} %bitcast.48, ...), custom_call_target="tpu_custom_call" | custom-call | flops 6000000000 | bytes 6000000 | tf_op jit(solution)/shard_map/first_sum/pallas_call | solution.py:1037
  399.3 28.8 %collective-permute-done.12.refs_1_.refs_5_ = bf16[2,4,80,1024]{3,2,1,0:T(8,128)(2,1)S(1)} collective-permute-done((bf16[2,4,80,1024]{3,2,1,0:T(8,128)(2,1)S(1)}, bf16[2,4,80,1024]{3,2,1,0:T(8,128)(2,1)S(1)}, u32[]{:S(2)}, u32[]{:S(2)}) %collective-permute-start.12) | collective-permute-done | bytes 1310752 | tf_op jit(solution)/shard_map/ppermute | solution.py:1263
  435.7 9.5 %all-to-all-done.7.x = bf16[4,2,144,1024]{3,2,1,0:T(8,128)(2,1)} async-done(((bf16[4,2,144,1024]{3,2,1,0:T(8,128)(2,1)}), bf16[4,2,144,1024]{3,2,1,0:T(8,128)(2,1)}, u32[]{:S(2)}, u32[]{:S(2)}) %all-to-all-start.7) | async-done | bytes 2359328 | tf_op jit(solution)/shard_map/all_to_all | solution.py:1295
  461.7 24.3 %collective-permute-done.16 = f32[64,1024]{1,0:T(8,128)S(1)} collective-permute-done((f32[64,1024]{1,0:T(8,128)S(1)}, f32[64,1024]{1,0:T(8,128)S(1)}, u32[]{:S(2)}, u32[]{:S(2)}) %collective-permute-start.16) | collective-permute-done | bytes 262176 | tf_op jit(solution)/shard_map/ppermute | solution.py:1263
  521.8 5.8 %collective-permute-done.29.refs_2_ = bf16[2,144,1024]{2,1,0:T(8,128)(2,1)S(1)} collective-permute-done((bf16[2,144,1024]{2,1,0:T(8,128)(2,1)}, bf16[2,144,1024]{2,1,0:T(8,128)(2,1)S(1)}, u32[]{:S(2)}, u32[]{:S(2)}) %collective-permute-start.29) | collective-permute-done | bytes 589856 | tf_op jit(solution)/shard_map/ppermute | solution.py:1263
  (213 shorter events, 156.1 us)
Async XLA Ops:
  24.0 44.3 %all-to-all-start = ((bf16[8,192,512]{2,1,0:T(8,128)(2,1)}), bf16[8,192,512]{2,1,0:T(8,128)(2,1)S(1)}, u32[]{:S(2)}, u32[]{:S(2)}) async-start(bf16[8,192,512]{2,1,0:T(8,128)(2,1)} %qkv_block.2), calls=%async_computation | async-start | bytes 3145728 | tf_op jit(solution)/shard_map/all_to_all | solution.py:1399
  68.3 41.3 %all-to-all-start.2 = ((bf16[8,192,512]{2,1,0:T(8,128)(2,1)}), bf16[8,192,512]{2,1,0:T(8,128)(2,1)S(1)}, u32[]{:S(2)}, u32[]{:S(2)}) async-start(bf16[8,192,512]{2,1,0:T(8,128)(2,1)} %qkv_block.3), calls=%async_computation.2 | async-start | bytes 3145728 | tf_op jit(solution)/shard_map/all_to_all | solution.py:1399
  110.2 28.5 %all-to-all-start.1 = ((bf16[8,64,512]{2,1,0:T(8,128)(2,1)}), bf16[8,64,512]{2,1,0:T(8,128)(2,1)S(1)}, u32[]{:S(2)}, u32[]{:S(2)}) async-start(bf16[8,64,512]{2,1,0:T(8,128)(2,1)} %get-tuple-element.95.o_ref), calls=%async_computation.1 | async-start | bytes 1048576 | tf_op jit(solution)/shard_map/all_to_all | solution.py:1412
  210.4 31.6 %all-to-all-start.4 = ((bf16[8,128,512]{2,1,0:T(8,128)(2,1)}), bf16[8,128,512]{2,1,0:T(8,128)(2,1)}, u32[]{:S(2)}, u32[]{:S(2)}) async-start(bf16[8,128,512]{2,1,0:T(8,128)(2,1)} %get-tuple-element.102), calls=%async_computation.4 | async-start | bytes 2097152 | tf_op jit(solution)/shard_map/all_to_all | solution.py:1432
  237.8 41.6 %collective-permute-start.6 = (bf16[2,4,64,1024]{3,2,1,0:T(8,128)(2,1)}, bf16[2,4,64,1024]{3,2,1,0:T(8,128)(2,1)S(1)}, u32[]{:S(2)}, u32[]{:S(2)}) collective-permute-start(bf16[2,4,64,1024]{3,2,1,0:T(8,128)(2,1)} %get-tuple-element.105), channel_id=1, source_target_pairs={{0,8},{8,0},{16,24},{24,16},{1,9},{9,1},{17,25},{25,17},{2,10},{10... | collective-permute-start | bytes 3145736 | tf_op jit(solution)/shard_map/ppermute | solution.py:1263
  237.8 41.6 %collective-permute-start.7 = (bf16[2,4,64,1024]{3,2,1,0:T(8,128)(2,1)}, bf16[2,4,64,1024]{3,2,1,0:T(8,128)(2,1)S(1)}, u32[]{:S(2)}, u32[]{:S(2)}) collective-permute-start(bf16[2,4,64,1024]{3,2,1,0:T(8,128)(2,1)} %get-tuple-element.107), channel_id=1, source_target_pairs={{0,16},{8,24},{16,0},{24,8},{1,17},{9,25},{17,1},{25,9},{2,18},{10... | collective-permute-start | bytes 3145736 | tf_op jit(solution)/shard_map/ppermute | solution.py:1263
  274.2 41.6 %collective-permute-start.5 = (bf16[2,4,80,1024]{3,2,1,0:T(8,128)(2,1)}, bf16[2,4,80,1024]{3,2,1,0:T(8,128)(2,1)}, u32[]{:S(2)}, u32[]{:S(2)}) collective-permute-start(bf16[2,4,80,1024]{3,2,1,0:T(8,128)(2,1)} %copy-done.9), channel_id=1, source_target_pairs={{0,16},{8,24},{16,0},{24,8},{1,17},{9,25},{17,1},{25,9},{2,18},{10... | collective-permute-start | bytes 3932168 | tf_op jit(solution)/shard_map/ppermute | solution.py:1263
  274.2 41.6 %collective-permute-start.4 = (bf16[2,4,80,1024]{3,2,1,0:T(8,128)(2,1)S(1)}, bf16[2,4,80,1024]{3,2,1,0:T(8,128)(2,1)}, u32[]{:S(2)}, u32[]{:S(2)}) collective-permute-start(bf16[2,4,80,1024]{3,2,1,0:T(8,128)(2,1)S(1)} %get-tuple-element.113), channel_id=1, source_target_pairs={{0,8},{8,0},{16,24},{24,16},{1,9},{9,1},{17,25},{25,17},{2,10},{10... | collective-permute-start | bytes 3932168 | tf_op jit(solution)/shard_map/ppermute | solution.py:1263
  279.4 42.1 %all-to-all-start.6 = ((bf16[8,192,512]{2,1,0:T(8,128)(2,1)}), bf16[8,192,512]{2,1,0:T(8,128)(2,1)}, u32[]{:S(2)}, u32[]{:S(2)}) async-start(bf16[8,192,512]{2,1,0:T(8,128)(2,1)} %attend_back.2), calls=%async_computation.6 | async-start | bytes 3145728 | tf_op jit(solution)/shard_map/all_to_all | solution.py:1442
  321.5 44.4 %all-to-all-start.5 = ((bf16[8,192,512]{2,1,0:T(8,128)(2,1)}), bf16[8,192,512]{2,1,0:T(8,128)(2,1)}, u32[]{:S(2)}, u32[]{:S(2)}) async-start(bf16[8,192,512]{2,1,0:T(8,128)(2,1)} %attend_back.3), calls=%async_computation.5 | async-start | bytes 3145728 | tf_op jit(solution)/shard_map/all_to_all | solution.py:1442
  331.8 28.2 %collective-permute-start.9 = (bf16[4,144,1024]{2,1,0:T(8,128)(2,1)S(1)}, bf16[4,144,1024]{2,1,0:T(8,128)(2,1)S(1)}, u32[]{:S(2)}, u32[]{:S(2)}) collective-permute-start(bf16[4,144,1024]{2,1,0:T(8,128)(2,1)S(1)} %get-tuple-element.125), channel_id=1, source_target_pairs={{0,8},{8,0},{16,24},{24,16},{1,9},{9,1},{17,25},{25,17},{2,10},{10... | collective-permute-start | bytes 3538952 | tf_op jit(solution)/shard_map/ppermute | solution.py:1263
  331.9 28.2 %collective-permute-start.8 = (bf16[4,144,1024]{2,1,0:T(8,128)(2,1)S(1)}, bf16[4,144,1024]{2,1,0:T(8,128)(2,1)S(1)}, u32[]{:S(2)}, u32[]{:S(2)}) collective-permute-start(bf16[4,144,1024]{2,1,0:T(8,128)(2,1)S(1)} %get-tuple-element.123), channel_id=1, source_target_pairs={{0,16},{8,24},{16,0},{24,8},{1,17},{9,25},{17,1},{25,9},{2,18},{10... | collective-permute-start | bytes 3538952 | tf_op jit(solution)/shard_map/ppermute | solution.py:1263
  386.1 59.1 %all-to-all-start.7 = ((bf16[4,2,144,1024]{3,2,1,0:T(8,128)(2,1)}), bf16[4,2,144,1024]{3,2,1,0:T(8,128)(2,1)}, u32[]{:S(2)}, u32[]{:S(2)}) async-start(bf16[4,2,144,1024]{3,2,1,0:T(8,128)(2,1)} %third_sum_all.1), calls=%async_computation.7 | async-start | bytes 4718592 | tf_op jit(solution)/shard_map/all_to_all | solution.py:1295
  397.7 30.5 %collective-permute-start.12 = (bf16[2,4,80,1024]{3,2,1,0:T(8,128)(2,1)S(1)}, bf16[2,4,80,1024]{3,2,1,0:T(8,128)(2,1)S(1)}, u32[]{:S(2)}, u32[]{:S(2)}) collective-permute-start(bf16[2,4,80,1024]{3,2,1,0:T(8,128)(2,1)S(1)} %get-tuple-element.148), channel_id=1, source_target_pairs={{0,8},{8,0},{16,24},{24,16},{1,9},{9,1},{17,25},{25,17},{2,10},{10... | collective-permute-start | bytes 3932168 | tf_op jit(solution)/shard_map/ppermute | solution.py:1263
  399.0 30.2 %collective-permute-start.13 = (bf16[2,4,80,1024]{3,2,1,0:T(8,128)(2,1)S(1)}, bf16[2,4,80,1024]{3,2,1,0:T(8,128)(2,1)S(1)}, u32[]{:S(2)}, u32[]{:S(2)}) collective-permute-start(bf16[2,4,80,1024]{3,2,1,0:T(8,128)(2,1)S(1)} %get-tuple-element.150), channel_id=1, source_target_pairs={{0,16},{8,24},{16,0},{24,8},{1,17},{9,25},{17,1},{25,9},{2,18},{10... | collective-permute-start | bytes 3932168 | tf_op jit(solution)/shard_map/ppermute | solution.py:1263
  454.8 33.2 %collective-permute-start.22 = (bf16[2,80,1024]{2,1,0:T(8,128)(2,1)}, bf16[2,80,1024]{2,1,0:T(8,128)(2,1)S(1)}, u32[]{:S(2)}, u32[]{:S(2)}) collective-permute-start(bf16[2,80,1024]{2,1,0:T(8,128)(2,1)} %get-tuple-element.160), channel_id=1, source_target_pairs={{0,2},{1,3},{2,0},{3,1},{4,6},{5,7},{6,4},{7,5},{8,10},{9,11},{10,... | collective-permute-start | bytes 983048 | tf_op jit(solution)/shard_map/ppermute | solution.py:1263
  456.3 29.6 %collective-permute-start.16 = (f32[64,1024]{1,0:T(8,128)S(1)}, f32[64,1024]{1,0:T(8,128)S(1)}, u32[]{:S(2)}, u32[]{:S(2)}) collective-permute-start(f32[64,1024]{1,0:T(8,128)S(1)} %add.55), channel_id=1, source_target_pairs={{0,4},{1,5},{2,6},{3,7},{4,0},{5,1},{6,2},{7,3},{8,12},{9,13},{10,... | collective-permute-start | bytes 786440 | tf_op jit(solution)/shard_map/ppermute | solution.py:1263
  458.6 34.4 %collective-permute-start.23 = (bf16[2,80,1024]{2,1,0:T(8,128)(2,1)}, bf16[2,80,1024]{2,1,0:T(8,128)(2,1)S(1)}, u32[]{:S(2)}, u32[]{:S(2)}) collective-permute-start(bf16[2,80,1024]{2,1,0:T(8,128)(2,1)} %get-tuple-element.161), channel_id=1, source_target_pairs={{0,4},{1,5},{2,6},{3,7},{4,0},{5,1},{6,2},{7,3},{8,12},{9,13},{10,... | collective-permute-start | bytes 983048 | tf_op jit(solution)/shard_map/ppermute | solution.py:1263
  459.3 34.6 %collective-permute-start.24 = (bf16[2,80,1024]{2,1,0:T(8,128)(2,1)}, bf16[2,80,1024]{2,1,0:T(8,128)(2,1)S(1)}, u32[]{:S(2)}, u32[]{:S(2)}) collective-permute-start(bf16[2,80,1024]{2,1,0:T(8,128)(2,1)} %get-tuple-element.162), channel_id=1, source_target_pairs={{0,6},{1,7},{2,4},{3,5},{4,2},{5,3},{6,0},{7,1},{8,14},{9,15},{10,... | collective-permute-start | bytes 983048 | tf_op jit(solution)/shard_map/ppermute | solution.py:1263
  493.0 24.1 %collective-permute-start.28 = (bf16[2,144,1024]{2,1,0:T(8,128)(2,1)}, bf16[2,144,1024]{2,1,0:T(8,128)(2,1)S(1)}, u32[]{:S(2)}, u32[]{:S(2)}) collective-permute-start(bf16[2,144,1024]{2,1,0:T(8,128)(2,1)} %fourth_sum_all.1.refs_0_), channel_id=1, source_target_pairs={{0,8},{8,0},{16,24},{24,16},{1,9},{9,1},{17,25},{25,17},{2,10},{10... | collective-permute-start | bytes 1769480 | tf_op jit(solution)/shard_map/ppermute | solution.py:1263
  493.9 33.8 %collective-permute-start.29 = (bf16[2,144,1024]{2,1,0:T(8,128)(2,1)}, bf16[2,144,1024]{2,1,0:T(8,128)(2,1)S(1)}, u32[]{:S(2)}, u32[]{:S(2)}) collective-permute-start(bf16[2,144,1024]{2,1,0:T(8,128)(2,1)} %fourth_sum_all.1.refs_0_), channel_id=1, source_target_pairs={{0,16},{8,24},{16,0},{24,8},{1,17},{9,25},{17,1},{25,9},{2,18},{10... | collective-permute-start | bytes 1769480 | tf_op jit(solution)/shard_map/ppermute | solution.py:1263
  497.3 30.4 %collective-permute-start.30 = (bf16[2,144,1024]{2,1,0:T(8,128)(2,1)S(1)}, bf16[2,144,1024]{2,1,0:T(8,128)(2,1)S(1)}, u32[]{:S(2)}, u32[]{:S(2)}) collective-permute-start(bf16[2,144,1024]{2,1,0:T(8,128)(2,1)S(1)} %copy-done.14), channel_id=1, source_target_pairs={{0,24},{8,16},{16,8},{24,0},{1,25},{9,17},{17,9},{25,1},{2,26},{10... | collective-permute-start | bytes 1769480 | tf_op jit(solution)/shard_map/ppermute | solution.py:1263
  498.9 32.2 %collective-permute-start.25 = (bf16[2,80,1024]{2,1,0:T(8,128)(2,1)}, bf16[2,80,1024]{2,1,0:T(8,128)(2,1)S(1)}, u32[]{:S(2)}, u32[]{:S(2)}) collective-permute-start(bf16[2,80,1024]{2,1,0:T(8,128)(2,1)} %fourth_sum.1.refs_0_), channel_id=1, source_target_pairs={{0,8},{8,0},{16,24},{24,16},{1,9},{9,1},{17,25},{25,17},{2,10},{10... | collective-permute-start | bytes 983048 | tf_op jit(solution)/shard_map/ppermute | solution.py:1263
  501.5 33.8 %collective-permute-start.26 = (bf16[2,80,1024]{2,1,0:T(8,128)(2,1)}, bf16[2,80,1024]{2,1,0:T(8,128)(2,1)S(1)}, u32[]{:S(2)}, u32[]{:S(2)}) collective-permute-start(bf16[2,80,1024]{2,1,0:T(8,128)(2,1)} %fourth_sum.1.refs_0_), channel_id=1, source_target_pairs={{0,16},{8,24},{16,0},{24,8},{1,17},{9,25},{17,1},{25,9},{2,18},{10... | collective-permute-start | bytes 983048 | tf_op jit(solution)/shard_map/ppermute | solution.py:1263
  (68 other events, 548.6 us)
where the time goes:
time: 547 us; the launch traced here: 539 us
  Pallas kernels  267 us (49%)
  waiting for transfers between devices  164 us (30%)
  starting transfers between devices  69.5 us (13%)
  local copies, waits for them, and re-layouts  27.2 us (5%)
  matrix products  8.28 us (2%)
    ppermute x31, waiting for transfers between devices, sum_exchange(): return lax.ppermute(value, axis, [(i, i ^ bit) for i in range(ways)])  104 us
    pallas_call x2, Pallas kernels, attend_back(): pl.pallas_call(functools.partial(bwd_kernel, utts, chunk), out_shape=jax....  64.3 us
    pallas_call x1, Pallas kernels, mid_block(): pl.pallas_call(functools.partial(mid_kernel, (seq_ways, heads_local, utts...  50.9 us
    pallas_call x2, Pallas kernels, attend(): pl.pallas_call(functools.partial(fwd_kernel, utts), out_shape=(jax.ShapeD...  49.8 us
    ppermute x31, starting transfers between devices, sum_exchange(): return lax.ppermute(value, axis, [(i, i ^ bit) for i in range(ways)])  32.6 us
    all_to_all x2, waiting for transfers between devices, shards(): received.append(exchange(packed))  31 us
    pallas_call x2, Pallas kernels, back_block(): pl.pallas_call(functools.partial(back_kernel, utts, seq_ways, chunk), out...  19.1 us
    unnamed x108, local copies, waits for them, and re-layouts  18 us
  transfers between devices with their start and end apart: 39, of which 19 were waited for; matrix products, arithmetic and copies ran while one was open for 2% of the time, Pallas kernels for 35%

commit v1 on v0

--- a/solution.py
+++ b/solution.py
@@ -1334,9 +1334,11 @@
     return [value] + [sum_exchange(value, "batch", i) for i in range(1, lax.axis_size("batch"))]
 
 
-def sum_seq(value):
-    for bit in axis_bits(lax.axis_size("seq")):
-        value = value + sum_exchange(value, "seq", bit)
+def sum_seq(value, token):
+    value = value + sum_exchange(value, "seq", 1)
+    away = after(value, *token)
+    for j in range(1, lax.axis_size("seq") // 2):
+        value = value + sum_exchange(away, "seq", 2 * j)
     return value
 
 
@@ -1455,15 +1457,15 @@
     moving = next(feed)
     gh, small = norm_block(lengths_row, ids, acc, hidden, after_grad, mods_a, loss_mask, mid_small, biases)
     rest = reduce_stages(ids, [skip_block(ids, joinedT, gh, seq_ways, PARTS), (keep, send)], [5 * own // PARTS], False)
-    small = after(small, *moving, *advance(rest, 3))
-    token = advance(rest, 2)[0]
-    groups = gather_groups(sum_seq(small))
+    small = sum_seq(small, [*moving, *advance(rest, 3)])
+    next(rest)
+    groups = gather_groups(after(small, *next(rest)))
     numerator = float(group_frames * batch_ways)
     grad_w_ada, vectors, scale = ada_block(time3, groups, utts, numerator)
     grad_tokens, grad_skip = joined_block(gh, w_skip, scale)
     next(feed)
-    feed = last_stage(feed, token)
-    rest = last_stage(rest)
+    feed = last_stage(feed, groups[-1])
+    rest = last_stage(rest, small)
 
     ff = w_up.shape[1]
     chunks = ff // width

time: 547 us -> 541 us (0.989)
  Pallas kernels: 267 us -> 244 us
  starting transfers between devices: 69.5 us -> 84.2 us
    ppermute x31 -> x32, starting transfers between devices: 32.6 us -> 47.3 us  [sum_exchange(): return lax.ppermute(value, axis, [(i, i ^ bit) for i in range(ways)])]
    pallas_call x2, Pallas kernels: 64.3 us -> 52.1 us  [attend_back(): pl.pallas_call(functools.partial(bwd_kernel, utts, chunk), out_shape=jax....]
    pallas_call x2, Pallas kernels: 49.8 us -> 40.2 us  [attend(): pl.pallas_call(functools.partial(fwd_kernel, utts), out_shape=(jax.ShapeD...]
    ppermute x31 -> x32, waiting for transfers between devices: 104 us -> 95.8 us  [sum_exchange(): return lax.ppermute(value, axis, [(i, i ^ bit) for i in range(ways)])]
    all_to_all x2, waiting for transfers between devices: 5.75 us -> 11.8 us  [shards(): grad_local.append(exchange(after(grad, *moving)))]
    unnamed x108 -> x106, local copies, waits for them, and re-layouts: 18 us -> 17.1 us
  transfers between devices with their start and end apart: 39 -> 40, of which waited for: 19 -> 18; matrix products, arithmetic and copies ran while one was open for 2% -> 2% of each run, Pallas kernels for 35% -> 30%
where the time goes in v1:
time: 541 us; the launch traced here: 532 us
  Pallas kernels  244 us (45%)
  waiting for transfers between devices  166 us (31%)
  starting transfers between devices  84.2 us (16%)
  local copies, waits for them, and re-layouts  25.4 us (5%)
  matrix products  8.28 us (2%)
    ppermute x32, waiting for transfers between devices, sum_exchange(): return lax.ppermute(value, axis, [(i, i ^ bit) for i in range(ways)])  95.8 us
    pallas_call x2, Pallas kernels, attend_back(): pl.pallas_call(functools.partial(bwd_kernel, utts, chunk), out_shape=jax....  52.1 us
    pallas_call x1, Pallas kernels, mid_block(): pl.pallas_call(functools.partial(mid_kernel, (seq_ways, heads_local, utts...  50.9 us
    ppermute x32, starting transfers between devices, sum_exchange(): return lax.ppermute(value, axis, [(i, i ^ bit) for i in range(ways)])  47.3 us
    pallas_call x2, Pallas kernels, attend(): pl.pallas_call(functools.partial(fwd_kernel, utts), out_shape=(jax.ShapeD...  40.2 us
    all_to_all x2, waiting for transfers between devices, shards(): received.append(exchange(packed))  35.8 us
    pallas_call x2, Pallas kernels, back_block(): pl.pallas_call(functools.partial(back_kernel, utts, seq_ways, chunk), out...  19.1 us
    unnamed x106, local copies, waits for them, and re-layouts  17.1 us
  transfers between devices with their start and end apart: 40, of which 18 were waited for; matrix products, arithmetic and copies ran while one was open for 2% of the time, Pallas kernels for 30%

profile of v1, /device:TPU:0, one launch (start us, length us, event | category | flops | bytes accessed | tf_op | source)
XLA Modules:
  0.0 531.6 jit_solution(17426626386846342201)
XLA Ops:
  7.3 8.0 %head_block.1 = (f32[512,1024]{1,0:T(8,128)}, bf16[2048,512]{1,0:T(8,128)(2,1)}, bf16[1024,512]{1,0:T(8,128)(2,1)S(1)}, bf16[512,1024]{1,0:T(8,128)(2,1)S(1)}) custom-call(s32[8]{0:T(128)S(1)} %bitcast.67, s32[5]{0:T(128)S(1)} %stack.23.ids_ref, s32[8]{0:T(128)S(1)} %bitcast.57, bf16[512,1024]{1,0:T(8,128)(2,1)S(1)} %bitcast.52, ...), custom_call_target="tpu_custom_call" | custom-call | flops 10000000000 | bytes 10000000 | tf_op jit(solution)/shard_map/head_block/pallas_call | solution.py:676
  17.2 6.7 %qkv_block.2 = bf16[8,192,512]{2,1,0:T(8,128)(2,1)} custom-call(s32[8]{0:T(128)} %bitcast.60, s32[5]{0:T(128)} %copy-done.4, s32[8]{0:T(128)} %bitcast.55, bf16[512,1024]{1,0:T(8,128)(2,1)} %copy-done.28, bf16[1024,3072]{1,0:T(8,128)(2,1)} %w_ref.8, bf16[1,3072]{1,0:T(2,128)(2,1)} %broadcast_in_dim.28.b_ref), custom_call_target="tpu_custom_call" | custom-call | flops 7500000256 | bytes 7500000 | tf_op jit(solution)/shard_map/qkv_block/pallas_call | solution.py:729
  24.0 6.5 %all-to-all-start = ((bf16[8,192,512]{2,1,0:T(8,128)(2,1)}), bf16[8,192,512]{2,1,0:T(8,128)(2,1)S(1)}, u32[]{:S(2)}, u32[]{:S(2)}) async-start(bf16[8,192,512]{2,1,0:T(8,128)(2,1)} %qkv_block.2), calls=%async_computation | async-start | bytes 3145728 | tf_op jit(solution)/shard_map/all_to_all | solution.py:1401
  35.7 6.8 %qkv_block.3 = bf16[8,192,512]{2,1,0:T(8,128)(2,1)} custom-call(s32[8]{0:T(128)} %bitcast.61, s32[5]{0:T(128)} %copy-done.4, s32[8]{0:T(128)} %bitcast.56, bf16[512,1024]{1,0:T(8,128)(2,1)} %copy-done.28, bf16[1024,3072]{1,0:T(8,128)(2,1)} %w_ref.8, bf16[1,3072]{1,0:T(2,128)(2,1)} %broadcast_in_dim.28.b_ref), custom_call_target="tpu_custom_call" | custom-call | flops 7500000256 | bytes 7500000 | tf_op jit(solution)/shard_map/qkv_block/pallas_call | solution.py:729
  42.5 25.8 %all-to-all-done.qkv_ref = bf16[8,192,512]{2,1,0:T(8,128)(2,1)S(1)} async-done(((bf16[8,192,512]{2,1,0:T(8,128)(2,1)}), bf16[8,192,512]{2,1,0:T(8,128)(2,1)S(1)}, u32[]{:S(2)}, u32[]{:S(2)}) %all-to-all-start) | async-done | bytes 1572896 | tf_op jit(solution)/shard_map/all_to_all | solution.py:1401
  79.6 20.0 %attend.2 = (bf16[8,64,512]{2,1,0:T(8,128)(2,1)}, f32[8,1,512]{2,1,0:T(1,128)}) custom-call(s32[8]{0:T(128)} %bitcast.62, bf16[8,192,512]{2,1,0:T(8,128)(2,1)} %copy-done.34, s32[8,1,512]{2,1,0:T(1,128)} %bitcast.82), custom_call_target="tpu_custom_call" | custom-call | flops 24999999488 | bytes 25000000 | tf_op jit(solution)/shard_map/attend/pallas_call | solution.py:135
  99.6 10.0 %all-to-all-done.2.qkv_ref = bf16[8,192,512]{2,1,0:T(8,128)(2,1)S(1)} async-done(((bf16[8,192,512]{2,1,0:T(8,128)(2,1)}), bf16[8,192,512]{2,1,0:T(8,128)(2,1)S(1)}, u32[]{:S(2)}, u32[]{:S(2)}) %all-to-all-start.2) | async-done | bytes 1572896 | tf_op jit(solution)/shard_map/all_to_all | solution.py:1401
  113.8 20.2 %attend.3 = (bf16[8,64,512]{2,1,0:T(8,128)(2,1)}, f32[8,1,512]{2,1,0:T(1,128)}) custom-call(s32[8]{0:T(128)} %bitcast.63, bf16[8,192,512]{2,1,0:T(8,128)(2,1)} %copy-done.33, s32[8,1,512]{2,1,0:T(1,128)} %bitcast.83), custom_call_target="tpu_custom_call" | custom-call | flops 24999999488 | bytes 25000000 | tf_op jit(solution)/shard_map/attend/pallas_call | solution.py:135
  141.1 13.6 %all-to-all-done.3.refs_1_ = bf16[8,64,512]{2,1,0:T(8,128)(2,1)} async-done(((bf16[8,64,512]{2,1,0:T(8,128)(2,1)}), bf16[8,64,512]{2,1,0:T(8,128)(2,1)}, u32[]{:S(2)}, u32[]{:S(2)}) %all-to-all-start.3) | async-done | bytes 524320 | tf_op jit(solution)/shard_map/all_to_all | solution.py:1414
  154.6 50.9 %mid_block.1 = (bf16[512,1024]{1,0:T(8,128)(2,1)}, f32[512,1024]{1,0:T(8,128)}, f32[40,1024]{1,0:T(8,128)}, bf16[8,128,512]{2,1,0:T(8,128)(2,1)}, bf16[8,4,144,1...) custom-call(s32[8]{0:T(128)} %bitcast.64, s32[5]{0:T(128)} %copy-done.4, bf16[8,64,512]{2,1,0:T(8,128)(2,1)} %copy-done.37, ...), custom_call_target="tpu_custom_call" | custom-call | flops 49999998976 | bytes 50000000 | tf_op jit(solution)/shard_map/mid_block/pallas_call | solution.py:547
  210.1 10.5 %collective-permute-done.3 = bf16[8,4,144,1024]{3,2,1,0:T(8,128)(2,1)} collective-permute-done((bf16[8,4,144,1024]{3,2,1,0:T(8,128)(2,1)}, bf16[8,4,144,1024]{3,2,1,0:T(8,128)(2,1)}, u32[]{:S(2)}, u32[]{:S(2)}) %collective-permute-start.3) | collective-permute-done | bytes 9437216 | tf_op jit(solution)/shard_map/ppermute | solution.py:1263
  220.6 11.3 %first_sum.2 = (bf16[2,4,64,1024]{3,2,1,0:T(8,128)(2,1)}, bf16[2,4,80,1024]{3,2,1,0:T(8,128)(2,1)S(1)}, bf16[2,4,64,1024]{3,2,1,0:T(8,128)(2,1)}, bf16[2,4,80,10...) custom-call(s32[5]{0:T(128)S(1)} %copy-done.5, ...), custom_call_target="tpu_custom_call" | custom-call | flops 6000000000 | bytes 6000000 | tf_op jit(solution)/shard_map/first_sum/pallas_call | solution.py:1037
  240.8 26.1 %attend_back.2 = bf16[8,192,512]{2,1,0:T(8,128)(2,1)} custom-call(s32[8]{0:T(128)} %bitcast.65, bf16[8,192,512]{2,1,0:T(8,128)(2,1)} %copy-done.34, s32[8,1,512]{2,1,0:T(1,128)} %bitcast.84, bf16[8,64,512]{2,1,0:T(8,128)(2,1)} %get-tuple-element.99.o_ref, bf16[8,128,512]{2,1,0:T(8,128)(2,1)} %all-to-all-done.4.do_ref, f32[8,1,512]{2,1,0:T(1,128)} %get-tuple-element.114.lse_ref), custom_call_target="tpu_custom_call" | custom-call | flops 32000000000 | bytes 32000000 | tf_op jit(solution)/shard_map/attend_back/pallas_call | solution.py:257
  266.9 8.2 %collective-permute-start.5 = (bf16[2,4,80,1024]{3,2,1,0:T(8,128)(2,1)}, bf16[2,4,80,1024]{3,2,1,0:T(8,128)(2,1)}, u32[]{:S(2)}, u32[]{:S(2)}) collective-permute-start(bf16[2,4,80,1024]{3,2,1,0:T(8,128)(2,1)} %copy-done.9), channel_id=1, source_target_pairs={{0,16},{8,24},{16,0},{24,8},{1,17},{9,25},{17,1},{25,9},{2,18},{10... | collective-permute-start | bytes 3932168 | tf_op jit(solution)/shard_map/ppermute | solution.py:1263
  281.0 26.0 %attend_back.3 = bf16[8,192,512]{2,1,0:T(8,128)(2,1)} custom-call(s32[8]{0:T(128)} %bitcast.66, bf16[8,192,512]{2,1,0:T(8,128)(2,1)} %copy-done.33, s32[8,1,512]{2,1,0:T(1,128)} %bitcast.85, bf16[8,64,512]{2,1,0:T(8,128)(2,1)} %get-tuple-element.103.o_ref, bf16[8,128,512]{2,1,0:T(8,128)(2,1)} %all-to-all-done.4.do_ref, f32[8,1,512]{2,1,0:T(1,128)} %get-tuple-element.116.lse_ref), custom_call_target="tpu_custom_call" | custom-call | flops 32000000000 | bytes 32000000 | tf_op jit(solution)/shard_map/attend_back/pallas_call | solution.py:257
  307.0 11.8 %all-to-all-done.6.grad_ref = bf16[8,192,512]{2,1,0:T(8,128)(2,1)} async-done(((bf16[8,192,512]{2,1,0:T(8,128)(2,1)}), bf16[8,192,512]{2,1,0:T(8,128)(2,1)}, u32[]{:S(2)}, u32[]{:S(2)}) %all-to-all-start.6) | async-done | bytes 1572896 | tf_op jit(solution)/shard_map/all_to_all | solution.py:1444
  329.7 9.1 %back_block.2 = (f32[1024,512]{1,0:T(8,128)S(1)}, f32[3,8,512]{2,1,0:T(8,128)S(1)}, bf16[8,4,48,1024]{3,2,1,0:T(8,128)(2,1)}, bf16[8,4,48,1024]{3,2,1,0:T(8,128)(2,1)}) custom-call(s32[8]{0:T(128)S(1)} %bitcast.68, s32[5]{0:T(128)S(1)} %copy-done.5, s32[8]{0:T(128)S(1)} %bitcast.58, bf16[8,192,512]{2,1,0:T(8,128)(2,1)} %all-to-all-done.6.grad_ref, ...), custom_call_target="tpu_custom_call" | custom-call | flops 10000000000 | bytes 10000000 | tf_op jit(solution)/shard_map/back_block/pallas_call | solution.py:832
  340.1 17.2 %collective-permute-done.9.got_b = bf16[4,144,1024]{2,1,0:T(8,128)(2,1)S(1)} collective-permute-done((bf16[4,144,1024]{2,1,0:T(8,128)(2,1)S(1)}, bf16[4,144,1024]{2,1,0:T(8,128)(2,1)S(1)}, u32[]{:S(2)}, u32[]{:S(2)}) %collective-permute-start.9) | collective-permute-done | bytes 1179680 | tf_op jit(solution)/shard_map/ppermute | solution.py:1263
  363.3 10.0 %back_block.3 = (f32[1024,512]{1,0:T(8,128)S(1)}, f32[3,8,512]{2,1,0:T(8,128)S(1)}, bf16[8,4,48,1024]{3,2,1,0:T(8,128)(2,1)}, bf16[8,4,48,1024]{3,2,1,0:T(8,128)(2,1)}) custom-call(s32[8]{0:T(128)S(1)} %bitcast.69, s32[5]{0:T(128)S(1)} %copy-done.6, s32[8]{0:T(128)S(1)} %bitcast.59, ...), custom_call_target="tpu_custom_call", output_to_operand_aliasing={{2}: (7, {}), {3}: (8, {})} | custom-call | flops 10000000000 | bytes 10000000 | tf_op jit(solution)/shard_map/back_block/pallas_call | solution.py:832
  396.8 28.6 %collective-permute-done.13.refs_1_.refs_5_ = bf16[2,4,80,1024]{3,2,1,0:T(8,128)(2,1)S(1)} collective-permute-done((bf16[2,4,80,1024]{3,2,1,0:T(8,128)(2,1)S(1)}, bf16[2,4,80,1024]{3,2,1,0:T(8,128)(2,1)S(1)}, u32[]{:S(2)}, u32[]{:S(2)}) %collective-permute-start.13) | collective-permute-done | bytes 1310752 | tf_op jit(solution)/shard_map/ppermute | solution.py:1263
  433.3 9.3 %all-to-all-done.7.x = bf16[4,2,144,1024]{3,2,1,0:T(8,128)(2,1)} async-done(((bf16[4,2,144,1024]{3,2,1,0:T(8,128)(2,1)}), bf16[4,2,144,1024]{3,2,1,0:T(8,128)(2,1)}, u32[]{:S(2)}, u32[]{:S(2)}) %all-to-all-start.7) | async-done | bytes 2359328 | tf_op jit(solution)/shard_map/all_to_all | solution.py:1295
  446.9 7.6 %collective-permute-done.15 = f32[64,1024]{1,0:T(8,128)S(1)} collective-permute-done((f32[64,1024]{1,0:T(8,128)S(1)}, f32[64,1024]{1,0:T(8,128)S(1)}, u32[]{:S(2)}, u32[]{:S(2)}) %collective-permute-start.15) | collective-permute-done | bytes 262176 | tf_op jit(solution)/shard_map/ppermute | solution.py:1263
  454.5 9.4 %collective-permute-done.16 = f32[64,1024]{1,0:T(8,128)S(1)} collective-permute-done((f32[64,1024]{1,0:T(8,128)S(1)}, f32[64,1024]{1,0:T(8,128)S(1)}, u32[]{:S(2)}, u32[]{:S(2)}) %collective-permute-start.16) | collective-permute-done | bytes 262176 | tf_op jit(solution)/shard_map/ppermute | solution.py:1263
  492.5 11.7 %collective-permute-done.24.refs_2_ = bf16[2,80,1024]{2,1,0:T(8,128)(2,1)} collective-permute-done((bf16[2,80,1024]{2,1,0:T(8,128)(2,1)S(1)}, bf16[2,80,1024]{2,1,0:T(8,128)(2,1)}, u32[]{:S(2)}, u32[]{:S(2)}) %collective-permute-start.24) | collective-permute-done | bytes 327712 | tf_op jit(solution)/shard_map/ppermute | solution.py:1263
  (212 shorter events, 164.6 us)
Async XLA Ops:
  24.0 44.3 %all-to-all-start = ((bf16[8,192,512]{2,1,0:T(8,128)(2,1)}), bf16[8,192,512]{2,1,0:T(8,128)(2,1)S(1)}, u32[]{:S(2)}, u32[]{:S(2)}) async-start(bf16[8,192,512]{2,1,0:T(8,128)(2,1)} %qkv_block.2), calls=%async_computation | async-start | bytes 3145728 | tf_op jit(solution)/shard_map/all_to_all | solution.py:1401
  68.3 41.3 %all-to-all-start.2 = ((bf16[8,192,512]{2,1,0:T(8,128)(2,1)}), bf16[8,192,512]{2,1,0:T(8,128)(2,1)S(1)}, u32[]{:S(2)}, u32[]{:S(2)}) async-start(bf16[8,192,512]{2,1,0:T(8,128)(2,1)} %qkv_block.3), calls=%async_computation.2 | async-start | bytes 3145728 | tf_op jit(solution)/shard_map/all_to_all | solution.py:1401
  110.2 23.7 %all-to-all-start.1 = ((bf16[8,64,512]{2,1,0:T(8,128)(2,1)}), bf16[8,64,512]{2,1,0:T(8,128)(2,1)S(1)}, u32[]{:S(2)}, u32[]{:S(2)}) async-start(bf16[8,64,512]{2,1,0:T(8,128)(2,1)} %get-tuple-element.99.o_ref), calls=%async_computation.1 | async-start | bytes 1048576 | tf_op jit(solution)/shard_map/all_to_all | solution.py:1414
  205.6 35.2 %all-to-all-start.4 = ((bf16[8,128,512]{2,1,0:T(8,128)(2,1)}), bf16[8,128,512]{2,1,0:T(8,128)(2,1)}, u32[]{:S(2)}, u32[]{:S(2)}) async-start(bf16[8,128,512]{2,1,0:T(8,128)(2,1)} %get-tuple-element.106), calls=%async_computation.4 | async-start | bytes 2097152 | tf_op jit(solution)/shard_map/all_to_all | solution.py:1434
  233.0 43.7 %collective-permute-start.6 = (bf16[2,4,64,1024]{3,2,1,0:T(8,128)(2,1)}, bf16[2,4,64,1024]{3,2,1,0:T(8,128)(2,1)S(1)}, u32[]{:S(2)}, u32[]{:S(2)}) collective-permute-start(bf16[2,4,64,1024]{3,2,1,0:T(8,128)(2,1)} %get-tuple-element.109), channel_id=1, source_target_pairs={{0,8},{8,0},{16,24},{24,16},{1,9},{9,1},{17,25},{25,17},{2,10},{10... | collective-permute-start | bytes 3145736 | tf_op jit(solution)/shard_map/ppermute | solution.py:1263
  239.3 37.4 %collective-permute-start.7 = (bf16[2,4,64,1024]{3,2,1,0:T(8,128)(2,1)}, bf16[2,4,64,1024]{3,2,1,0:T(8,128)(2,1)S(1)}, u32[]{:S(2)}, u32[]{:S(2)}) collective-permute-start(bf16[2,4,64,1024]{3,2,1,0:T(8,128)(2,1)} %get-tuple-element.111), channel_id=1, source_target_pairs={{0,16},{8,24},{16,0},{24,8},{1,17},{9,25},{17,1},{25,9},{2,18},{10... | collective-permute-start | bytes 3145736 | tf_op jit(solution)/shard_map/ppermute | solution.py:1263
  266.9 40.1 %collective-permute-start.5 = (bf16[2,4,80,1024]{3,2,1,0:T(8,128)(2,1)}, bf16[2,4,80,1024]{3,2,1,0:T(8,128)(2,1)}, u32[]{:S(2)}, u32[]{:S(2)}) collective-permute-start(bf16[2,4,80,1024]{3,2,1,0:T(8,128)(2,1)} %copy-done.9), channel_id=1, source_target_pairs={{0,16},{8,24},{16,0},{24,8},{1,17},{9,25},{17,1},{25,9},{2,18},{10... | collective-permute-start | bytes 3932168 | tf_op jit(solution)/shard_map/ppermute | solution.py:1263
  275.1 31.8 %collective-permute-start.4 = (bf16[2,4,80,1024]{3,2,1,0:T(8,128)(2,1)S(1)}, bf16[2,4,80,1024]{3,2,1,0:T(8,128)(2,1)}, u32[]{:S(2)}, u32[]{:S(2)}) collective-permute-start(bf16[2,4,80,1024]{3,2,1,0:T(8,128)(2,1)S(1)} %get-tuple-element.117), channel_id=1, source_target_pairs={{0,8},{8,0},{16,24},{24,16},{1,9},{9,1},{17,25},{25,17},{2,10},{10... | collective-permute-start | bytes 3932168 | tf_op jit(solution)/shard_map/ppermute | solution.py:1263
  276.6 42.1 %all-to-all-start.6 = ((bf16[8,192,512]{2,1,0:T(8,128)(2,1)}), bf16[8,192,512]{2,1,0:T(8,128)(2,1)}, u32[]{:S(2)}, u32[]{:S(2)}) async-start(bf16[8,192,512]{2,1,0:T(8,128)(2,1)} %attend_back.2), calls=%async_computation.6 | async-start | bytes 3145728 | tf_op jit(solution)/shard_map/all_to_all | solution.py:1444
  318.8 44.4 %all-to-all-start.5 = ((bf16[8,192,512]{2,1,0:T(8,128)(2,1)}), bf16[8,192,512]{2,1,0:T(8,128)(2,1)}, u32[]{:S(2)}, u32[]{:S(2)}) async-start(bf16[8,192,512]{2,1,0:T(8,128)(2,1)} %attend_back.3), calls=%async_computation.5 | async-start | bytes 3145728 | tf_op jit(solution)/shard_map/all_to_all | solution.py:1444
  329.1 28.2 %collective-permute-start.9 = (bf16[4,144,1024]{2,1,0:T(8,128)(2,1)S(1)}, bf16[4,144,1024]{2,1,0:T(8,128)(2,1)S(1)}, u32[]{:S(2)}, u32[]{:S(2)}) collective-permute-start(bf16[4,144,1024]{2,1,0:T(8,128)(2,1)S(1)} %get-tuple-element.129), channel_id=1, source_target_pairs={{0,8},{8,0},{16,24},{24,16},{1,9},{9,1},{17,25},{25,17},{2,10},{10... | collective-permute-start | bytes 3538952 | tf_op jit(solution)/shard_map/ppermute | solution.py:1263
  329.7 27.9 %collective-permute-start.8 = (bf16[4,144,1024]{2,1,0:T(8,128)(2,1)S(1)}, bf16[4,144,1024]{2,1,0:T(8,128)(2,1)S(1)}, u32[]{:S(2)}, u32[]{:S(2)}) collective-permute-start(bf16[4,144,1024]{2,1,0:T(8,128)(2,1)S(1)} %get-tuple-element.127), channel_id=1, source_target_pairs={{0,16},{8,24},{16,0},{24,8},{1,17},{9,25},{17,1},{25,9},{2,18},{10... | collective-permute-start | bytes 3538952 | tf_op jit(solution)/shard_map/ppermute | solution.py:1263
  383.4 59.1 %all-to-all-start.7 = ((bf16[4,2,144,1024]{3,2,1,0:T(8,128)(2,1)}), bf16[4,2,144,1024]{3,2,1,0:T(8,128)(2,1)}, u32[]{:S(2)}, u32[]{:S(2)}) async-start(bf16[4,2,144,1024]{3,2,1,0:T(8,128)(2,1)} %third_sum_all.1), calls=%async_computation.7 | async-start | bytes 4718592 | tf_op jit(solution)/shard_map/all_to_all | solution.py:1295
  394.9 30.5 %collective-permute-start.13 = (bf16[2,4,80,1024]{3,2,1,0:T(8,128)(2,1)S(1)}, bf16[2,4,80,1024]{3,2,1,0:T(8,128)(2,1)S(1)}, u32[]{:S(2)}, u32[]{:S(2)}) collective-permute-start(bf16[2,4,80,1024]{3,2,1,0:T(8,128)(2,1)S(1)} %get-tuple-element.152), channel_id=1, source_target_pairs={{0,8},{8,0},{16,24},{24,16},{1,9},{9,1},{17,25},{25,17},{2,10},{10... | collective-permute-start | bytes 3932168 | tf_op jit(solution)/shard_map/ppermute | solution.py:1263
  396.3 30.2 %collective-permute-start.14 = (bf16[2,4,80,1024]{3,2,1,0:T(8,128)(2,1)S(1)}, bf16[2,4,80,1024]{3,2,1,0:T(8,128)(2,1)S(1)}, u32[]{:S(2)}, u32[]{:S(2)}) collective-permute-start(bf16[2,4,80,1024]{3,2,1,0:T(8,128)(2,1)S(1)} %get-tuple-element.154), channel_id=1, source_target_pairs={{0,16},{8,24},{16,0},{24,8},{1,17},{9,25},{17,1},{25,9},{2,18},{10... | collective-permute-start | bytes 3932168 | tf_op jit(solution)/shard_map/ppermute | solution.py:1263
  396.8 36.4 %collective-permute-start.10 = (f32[64,1024]{1,0:T(8,128)S(1)}, f32[64,1024]{1,0:T(8,128)S(1)}, u32[]{:S(2)}, u32[]{:S(2)}) collective-permute-start(f32[64,1024]{1,0:T(8,128)S(1)} %get-tuple-element.145), channel_id=1, source_target_pairs={{0,1},{1,0},{2,3},{3,2},{4,5},{5,4},{6,7},{7,6},{8,9},{9,8},{10,11... | collective-permute-start | bytes 786440 | tf_op jit(solution)/shard_map/ppermute | solution.py:1263
  432.0 32.0 %collective-permute-start.18 = (bf16[4,80,1024]{2,1,0:T(8,128)(2,1)S(1)}, bf16[4,80,1024]{2,1,0:T(8,128)(2,1)S(1)}, u32[]{:S(2)}, u32[]{:S(2)}) collective-permute-start(bf16[4,80,1024]{2,1,0:T(8,128)(2,1)S(1)} %get-tuple-element.155), channel_id=1, source_target_pairs={{0,16},{8,24},{16,0},{24,8},{1,17},{9,25},{17,1},{25,9},{2,18},{10... | collective-permute-start | bytes 1966088 | tf_op jit(solution)/shard_map/ppermute | solution.py:1263
  432.5 31.5 %collective-permute-start.19 = (bf16[4,80,1024]{2,1,0:T(8,128)(2,1)S(1)}, bf16[4,80,1024]{2,1,0:T(8,128)(2,1)S(1)}, u32[]{:S(2)}, u32[]{:S(2)}) collective-permute-start(bf16[4,80,1024]{2,1,0:T(8,128)(2,1)S(1)} %get-tuple-element.156), channel_id=1, source_target_pairs={{0,8},{8,0},{16,24},{24,16},{1,9},{9,1},{17,25},{25,17},{2,10},{10... | collective-permute-start | bytes 1966088 | tf_op jit(solution)/shard_map/ppermute | solution.py:1263
  442.5 21.4 %collective-permute-start.16 = (f32[64,1024]{1,0:T(8,128)S(1)}, f32[64,1024]{1,0:T(8,128)S(1)}, u32[]{:S(2)}, u32[]{:S(2)}) collective-permute-start(f32[64,1024]{1,0:T(8,128)S(1)} %add.57), channel_id=1, source_target_pairs={{0,4},{1,5},{2,6},{3,7},{4,0},{5,1},{6,2},{7,3},{8,12},{9,13},{10,... | collective-permute-start | bytes 786440 | tf_op jit(solution)/shard_map/ppermute | solution.py:1263
  477.3 26.9 %collective-permute-start.24 = (bf16[2,80,1024]{2,1,0:T(8,128)(2,1)S(1)}, bf16[2,80,1024]{2,1,0:T(8,128)(2,1)}, u32[]{:S(2)}, u32[]{:S(2)}) collective-permute-start(bf16[2,80,1024]{2,1,0:T(8,128)(2,1)S(1)} %copy-done.49), channel_id=1, source_target_pairs={{0,4},{1,5},{2,6},{3,7},{4,0},{5,1},{6,2},{7,3},{8,12},{9,13},{10,... | collective-permute-start | bytes 983048 | tf_op jit(solution)/shard_map/ppermute | solution.py:1263
  481.6 22.6 %collective-permute-start.23 = (bf16[2,80,1024]{2,1,0:T(8,128)(2,1)S(1)}, bf16[2,80,1024]{2,1,0:T(8,128)(2,1)}, u32[]{:S(2)}, u32[]{:S(2)}) collective-permute-start(bf16[2,80,1024]{2,1,0:T(8,128)(2,1)S(1)} %copy-done.48), channel_id=1, source_target_pairs={{0,2},{1,3},{2,0},{3,1},{4,6},{5,7},{6,4},{7,5},{8,10},{9,11},{10,... | collective-permute-start | bytes 983048 | tf_op jit(solution)/shard_map/ppermute | solution.py:1263
  483.2 45.1 %collective-permute-start.29 = (bf16[2,144,1024]{2,1,0:T(8,128)(2,1)}, bf16[2,144,1024]{2,1,0:T(8,128)(2,1)S(1)}, u32[]{:S(2)}, u32[]{:S(2)}) collective-permute-start(bf16[2,144,1024]{2,1,0:T(8,128)(2,1)} %fourth_sum_all.1.refs_0_), channel_id=1, source_target_pairs={{0,8},{8,0},{16,24},{24,16},{1,9},{9,1},{17,25},{25,17},{2,10},{10... | collective-permute-start | bytes 1769480 | tf_op jit(solution)/shard_map/ppermute | solution.py:1263
  484.5 43.8 %collective-permute-start.30 = (bf16[2,144,1024]{2,1,0:T(8,128)(2,1)}, bf16[2,144,1024]{2,1,0:T(8,128)(2,1)S(1)}, u32[]{:S(2)}, u32[]{:S(2)}) collective-permute-start(bf16[2,144,1024]{2,1,0:T(8,128)(2,1)} %fourth_sum_all.1.refs_0_), channel_id=1, source_target_pairs={{0,16},{8,24},{16,0},{24,8},{1,17},{9,25},{17,1},{25,9},{2,18},{10... | collective-permute-start | bytes 1769480 | tf_op jit(solution)/shard_map/ppermute | solution.py:1263
  490.8 37.5 %collective-permute-start.31 = (bf16[2,144,1024]{2,1,0:T(8,128)(2,1)S(1)}, bf16[2,144,1024]{2,1,0:T(8,128)(2,1)S(1)}, u32[]{:S(2)}, u32[]{:S(2)}) collective-permute-start(bf16[2,144,1024]{2,1,0:T(8,128)(2,1)S(1)} %copy-done.14), channel_id=1, source_target_pairs={{0,24},{8,16},{16,8},{24,0},{1,25},{9,17},{17,9},{25,1},{2,26},{10... | collective-permute-start | bytes 1769480 | tf_op jit(solution)/shard_map/ppermute | solution.py:1263
  (68 other events, 572.6 us)

commit v2 on v1

--- a/solution.py
+++ b/solution.py
@@ -887,7 +887,9 @@
     small_ref[base + 3 : base + 4, :] = dot(sums, gh)[16:17]
     small_ref[base + 4 : base + 12, :] = mid_ref[4 * pad_u : 4 * pad_u + 8, :]
     count = jnp.sum(loss_ref[...].astype(f32), axis=1, keepdims=True)
-    small_ref[base + 12 : base + 16, :] = jnp.broadcast_to(count, (4, width))
+    high = jnp.floor(count / 32.0) * 32.0
+    small_ref[base + 12 : base + 13, :] = jnp.broadcast_to(high, (1, width))
+    small_ref[base + 13 : base + 16, :] = jnp.broadcast_to(count - high, (3, width))
 
 
 def norm_block(lengths, ids, acc, hidden, after, mods, loss, mid_small, biases):
@@ -1216,9 +1218,9 @@
     parts, (weight_ref, vector_ref, scale_ref) = refs[:groups], refs[groups:]
     table = pl.program_id(0)
     base = 6 * pad_u
-    count = parts[0][base + 12 : base + 13, 0:1]
+    count = parts[0][base + 12 : base + 13, 0:1] + parts[0][base + 13 : base + 14, 0:1]
     for p in parts[1:]:
-        count = count + p[base + 12 : base + 13, 0:1]
+        count = count + p[base + 12 : base + 13, 0:1] + p[base + 13 : base + 14, 0:1]
     scale = numerator / count
     rows = jnp.concatenate([p[pl.ds(pl.multiple_of(table * pad_u, 8), pad_u), :] for p in parts], axis=0) * scale
     vector_ref[pl.ds(table, 1), :] = jnp.sum(rows, axis=0, keepdims=True)
@@ -1334,11 +1336,10 @@
     return [value] + [sum_exchange(value, "batch", i) for i in range(1, lax.axis_size("batch"))]
 
 
-def sum_seq(value, token):
-    value = value + sum_exchange(value, "seq", 1)
-    away = after(value, *token)
+def sum_z(value):
+    away = value.astype(jnp.bfloat16)
     for j in range(1, lax.axis_size("seq") // 2):
-        value = value + sum_exchange(away, "seq", 2 * j)
+        value = value + sum_exchange(away, "seq", 2 * j).astype(jnp.float32)
     return value
 
 
@@ -1454,18 +1455,21 @@
         before = (acc, keep, send)
         biases.append(bias)
         ahead = next(feed) and advance(feed, 1, acc) if c == 0 else []
-    moving = next(feed)
     gh, small = norm_block(lengths_row, ids, acc, hidden, after_grad, mods_a, loss_mask, mid_small, biases)
-    rest = reduce_stages(ids, [skip_block(ids, joinedT, gh, seq_ways, PARTS), (keep, send)], [5 * own // PARTS], False)
-    small = sum_seq(small, [*moving, *advance(rest, 3)])
-    next(rest)
-    groups = gather_groups(after(small, *next(rest)))
+    small = small + sum_exchange(small, "seq", 1)
+    small = sum_z(small)
+    moving = feed.send(small)
+    skip_keep, skip_send = skip_block(ids, joinedT, gh, seq_ways, PARTS)
+    blocks = [(after(skip_keep, small), skip_send), (keep, send)]
+    rest = reduce_stages(ids, blocks, [5 * own // PARTS], False)
+    advance(rest, 4)
+    groups = gather_groups(after(small, *rest.send(moving[0])))
     numerator = float(group_frames * batch_ways)
     grad_w_ada, vectors, scale = ada_block(time3, groups, utts, numerator)
     grad_tokens, grad_skip = joined_block(gh, w_skip, scale)
     next(feed)
     feed = last_stage(feed, groups[-1])
-    rest = last_stage(rest, small)
+    rest = last_stage(rest)
 
     ff = w_up.shape[1]
     chunks = ff // width

time: 541 us -> 538 us (level)
  Pallas kernels: 244 us -> 266 us
  starting transfers between devices: 84.2 us -> 69.2 us
  waiting for transfers between devices: 166 us -> 156 us
    ppermute x32, starting transfers between devices: 47.3 us -> 32.6 us  [sum_exchange(): return lax.ppermute(value, axis, [(i, i ^ bit) for i in range(ways)])]
    pallas_call x2, Pallas kernels: 52.1 us -> 64.2 us  [attend_back(): pl.pallas_call(functools.partial(bwd_kernel, utts, chunk), out_shape=jax....]
    pallas_call x2, Pallas kernels: 40.2 us -> 49.8 us  [attend(): pl.pallas_call(functools.partial(fwd_kernel, utts), out_shape=(jax.ShapeD...]
    all_to_all x2, waiting for transfers between devices: 11.8 us -> 5.75 us  [shards(): grad_local.append(exchange(after(grad, *moving)))]
    unnamed x106 -> x108, local copies, waits for them, and re-layouts: 17.1 us -> 16.8 us
  transfers between devices with their start and end apart: 40 -> 40, of which waited for: 18 -> 21; matrix products, arithmetic and copies ran while one was open for 2% -> 2% of each run, Pallas kernels for 30% -> 35%
where the time goes in v2:
time: 538 us; the launch traced here: 528 us
  Pallas kernels  266 us (49%)
  waiting for transfers between devices  156 us (29%)
  starting transfers between devices  69.2 us (13%)
  local copies, waits for them, and re-layouts  25 us (5%)
  matrix products  8.29 us (2%)
    ppermute x32, waiting for transfers between devices, sum_exchange(): return lax.ppermute(value, axis, [(i, i ^ bit) for i in range(ways)])  93.9 us
    pallas_call x2, Pallas kernels, attend_back(): pl.pallas_call(functools.partial(bwd_kernel, utts, chunk), out_shape=jax....  64.2 us
    pallas_call x1, Pallas kernels, mid_block(): pl.pallas_call(functools.partial(mid_kernel, (seq_ways, heads_local, utts...  50.9 us
    pallas_call x2, Pallas kernels, attend(): pl.pallas_call(functools.partial(fwd_kernel, utts), out_shape=(jax.ShapeD...  49.8 us
    ppermute x32, starting transfers between devices, sum_exchange(): return lax.ppermute(value, axis, [(i, i ^ bit) for i in range(ways)])  32.6 us
    all_to_all x2, waiting for transfers between devices, shards(): received.append(exchange(packed))  31 us
    pallas_call x2, Pallas kernels, back_block(): pl.pallas_call(functools.partial(back_kernel, utts, seq_ways, chunk), out...  19.1 us
    unnamed x108, local copies, waits for them, and re-layouts  16.8 us
  transfers between devices with their start and end apart: 40, of which 21 were waited for; matrix products, arithmetic and copies ran while one was open for 2% of the time, Pallas kernels for 35%

profile of v2, /device:TPU:0, one launch (start us, length us, event | category | flops | bytes accessed | tf_op | source)
XLA Modules:
  0.0 528.0 jit_solution(11971721413068266430)
XLA Ops:
  7.3 8.0 %head_block.1 = (f32[512,1024]{1,0:T(8,128)}, bf16[2048,512]{1,0:T(8,128)(2,1)}, bf16[1024,512]{1,0:T(8,128)(2,1)S(1)}, bf16[512,1024]{1,0:T(8,128)(2,1)S(1)}) custom-call(s32[8]{0:T(128)S(1)} %bitcast.67, s32[5]{0:T(128)S(1)} %stack.23.ids_ref, s32[8]{0:T(128)S(1)} %bitcast.57, bf16[512,1024]{1,0:T(8,128)(2,1)S(1)} %bitcast.52, ...), custom_call_target="tpu_custom_call" | custom-call | flops 10000000000 | bytes 10000000 | tf_op jit(solution)/shard_map/head_block/pallas_call | solution.py:676
  17.2 6.8 %qkv_block.2 = bf16[8,192,512]{2,1,0:T(8,128)(2,1)} custom-call(s32[8]{0:T(128)} %bitcast.60, s32[5]{0:T(128)} %copy-done.4, s32[8]{0:T(128)} %bitcast.55, bf16[512,1024]{1,0:T(8,128)(2,1)} %copy-done.28, bf16[1024,3072]{1,0:T(8,128)(2,1)} %w_ref.8, bf16[1,3072]{1,0:T(2,128)(2,1)} %broadcast_in_dim.28.b_ref), custom_call_target="tpu_custom_call" | custom-call | flops 7500000256 | bytes 7500000 | tf_op jit(solution)/shard_map/qkv_block/pallas_call | solution.py:729
  24.0 6.5 %all-to-all-start = ((bf16[8,192,512]{2,1,0:T(8,128)(2,1)}), bf16[8,192,512]{2,1,0:T(8,128)(2,1)S(1)}, u32[]{:S(2)}, u32[]{:S(2)}) async-start(bf16[8,192,512]{2,1,0:T(8,128)(2,1)} %qkv_block.2), calls=%async_computation | async-start | bytes 3145728 | tf_op jit(solution)/shard_map/all_to_all | solution.py:1402
  30.4 5.3 %fusion.2.refs_3_ = f32[16,4096]{1,0:T(8,128)} fusion(bf16[1024,6144]{1,0:T(8,128)(2,1)} %param.32, f32[4096]{0:T(1024)S(1)} %slice_convert_fusion, bf16[8,1024]{1,0:T(8,128)(2,1)S(1)} %fusion.15), kind=kOutput, calls=%fused_computation.2 | convolution fusion | flops 134283264 | bytes 8683520 | tf_op jit(solution)/shard_map/dot_general | solution.py:1388
  35.7 6.8 %qkv_block.3 = bf16[8,192,512]{2,1,0:T(8,128)(2,1)} custom-call(s32[8]{0:T(128)} %bitcast.61, s32[5]{0:T(128)} %copy-done.4, s32[8]{0:T(128)} %bitcast.56, bf16[512,1024]{1,0:T(8,128)(2,1)} %copy-done.28, bf16[1024,3072]{1,0:T(8,128)(2,1)} %w_ref.8, bf16[1,3072]{1,0:T(2,128)(2,1)} %broadcast_in_dim.28.b_ref), custom_call_target="tpu_custom_call" | custom-call | flops 7500000256 | bytes 7500000 | tf_op jit(solution)/shard_map/qkv_block/pallas_call | solution.py:729
  42.5 25.8 %all-to-all-done.qkv_ref = bf16[8,192,512]{2,1,0:T(8,128)(2,1)S(1)} async-done(((bf16[8,192,512]{2,1,0:T(8,128)(2,1)}), bf16[8,192,512]{2,1,0:T(8,128)(2,1)S(1)}, u32[]{:S(2)}, u32[]{:S(2)}) %all-to-all-start) | async-done | bytes 1572896 | tf_op jit(solution)/shard_map/all_to_all | solution.py:1402
  79.6 24.8 %attend.2 = (bf16[8,64,512]{2,1,0:T(8,128)(2,1)}, f32[8,1,512]{2,1,0:T(1,128)}) custom-call(s32[8]{0:T(128)} %bitcast.62, bf16[8,192,512]{2,1,0:T(8,128)(2,1)} %copy-done.34, s32[8,1,512]{2,1,0:T(1,128)} %bitcast.82), custom_call_target="tpu_custom_call" | custom-call | flops 24999999488 | bytes 25000000 | tf_op jit(solution)/shard_map/attend/pallas_call | solution.py:135
  113.8 25.0 %attend.3 = (bf16[8,64,512]{2,1,0:T(8,128)(2,1)}, f32[8,1,512]{2,1,0:T(1,128)}) custom-call(s32[8]{0:T(128)} %bitcast.63, bf16[8,192,512]{2,1,0:T(8,128)(2,1)} %copy-done.33, s32[8,1,512]{2,1,0:T(1,128)} %bitcast.83), custom_call_target="tpu_custom_call" | custom-call | flops 24999999488 | bytes 25000000 | tf_op jit(solution)/shard_map/attend/pallas_call | solution.py:135
  138.8 5.2 all-to-all-start.3
  145.8 13.6 %all-to-all-done.3.refs_1_ = bf16[8,64,512]{2,1,0:T(8,128)(2,1)} async-done(((bf16[8,64,512]{2,1,0:T(8,128)(2,1)}), bf16[8,64,512]{2,1,0:T(8,128)(2,1)}, u32[]{:S(2)}, u32[]{:S(2)}) %all-to-all-start.3) | async-done | bytes 524320 | tf_op jit(solution)/shard_map/all_to_all | solution.py:1415
  159.4 50.9 %mid_block.1 = (bf16[512,1024]{1,0:T(8,128)(2,1)}, f32[512,1024]{1,0:T(8,128)}, f32[40,1024]{1,0:T(8,128)}, bf16[8,128,512]{2,1,0:T(8,128)(2,1)}, bf16[8,4,144,1...) custom-call(s32[8]{0:T(128)} %bitcast.64, s32[5]{0:T(128)} %copy-done.4, bf16[8,64,512]{2,1,0:T(8,128)(2,1)} %copy-done.37, ...), custom_call_target="tpu_custom_call" | custom-call | flops 49999998976 | bytes 50000000 | tf_op jit(solution)/shard_map/mid_block/pallas_call | solution.py:547
  214.9 10.5 %collective-permute-done.3 = bf16[8,4,144,1024]{3,2,1,0:T(8,128)(2,1)} collective-permute-done((bf16[8,4,144,1024]{3,2,1,0:T(8,128)(2,1)}, bf16[8,4,144,1024]{3,2,1,0:T(8,128)(2,1)}, u32[]{:S(2)}, u32[]{:S(2)}) %collective-permute-start.3) | collective-permute-done | bytes 9437216 | tf_op jit(solution)/shard_map/ppermute | solution.py:1265
  225.4 11.3 %first_sum.2 = (bf16[2,4,64,1024]{3,2,1,0:T(8,128)(2,1)}, bf16[2,4,80,1024]{3,2,1,0:T(8,128)(2,1)S(1)}, bf16[2,4,64,1024]{3,2,1,0:T(8,128)(2,1)}, bf16[2,4,80,10...) custom-call(s32[5]{0:T(128)S(1)} %copy-done.5, ...), custom_call_target="tpu_custom_call" | custom-call | flops 6000000000 | bytes 6000000 | tf_op jit(solution)/shard_map/first_sum/pallas_call | solution.py:1039
  241.5 32.2 %attend_back.2 = bf16[8,192,512]{2,1,0:T(8,128)(2,1)} custom-call(s32[8]{0:T(128)} %bitcast.65, bf16[8,192,512]{2,1,0:T(8,128)(2,1)} %copy-done.34, s32[8,1,512]{2,1,0:T(1,128)} %bitcast.84, bf16[8,64,512]{2,1,0:T(8,128)(2,1)} %get-tuple-element.99.o_ref, bf16[8,128,512]{2,1,0:T(8,128)(2,1)} %all-to-all-done.4.do_ref, f32[8,1,512]{2,1,0:T(1,128)} %get-tuple-element.114.lse_ref), custom_call_target="tpu_custom_call" | custom-call | flops 32000000000 | bytes 32000000 | tf_op jit(solution)/shard_map/attend_back/pallas_call | solution.py:257
  279.5 32.1 %attend_back.3 = bf16[8,192,512]{2,1,0:T(8,128)(2,1)} custom-call(s32[8]{0:T(128)} %bitcast.66, bf16[8,192,512]{2,1,0:T(8,128)(2,1)} %copy-done.33, s32[8,1,512]{2,1,0:T(1,128)} %bitcast.85, bf16[8,64,512]{2,1,0:T(8,128)(2,1)} %get-tuple-element.103.o_ref, bf16[8,128,512]{2,1,0:T(8,128)(2,1)} %all-to-all-done.4.do_ref, f32[8,1,512]{2,1,0:T(1,128)} %get-tuple-element.116.lse_ref), custom_call_target="tpu_custom_call" | custom-call | flops 32000000000 | bytes 32000000 | tf_op jit(solution)/shard_map/attend_back/pallas_call | solution.py:257
  311.6 5.7 %all-to-all-done.6.grad_ref = bf16[8,192,512]{2,1,0:T(8,128)(2,1)} async-done(((bf16[8,192,512]{2,1,0:T(8,128)(2,1)}), bf16[8,192,512]{2,1,0:T(8,128)(2,1)}, u32[]{:S(2)}, u32[]{:S(2)}) %all-to-all-start.6) | async-done | bytes 1572896 | tf_op jit(solution)/shard_map/all_to_all | solution.py:1445
  330.2 9.1 %back_block.2 = (f32[1024,512]{1,0:T(8,128)S(1)}, f32[3,8,512]{2,1,0:T(8,128)S(1)}, bf16[8,4,48,1024]{3,2,1,0:T(8,128)(2,1)}, bf16[8,4,48,1024]{3,2,1,0:T(8,128)(2,1)}) custom-call(s32[8]{0:T(128)S(1)} %bitcast.68, s32[5]{0:T(128)S(1)} %copy-done.5, s32[8]{0:T(128)S(1)} %bitcast.58, bf16[8,192,512]{2,1,0:T(8,128)(2,1)} %all-to-all-done.6.grad_ref, ...), custom_call_target="tpu_custom_call" | custom-call | flops 10000000000 | bytes 10000000 | tf_op jit(solution)/shard_map/back_block/pallas_call | solution.py:832
  340.6 15.5 %collective-permute-done.9.got_b = bf16[4,144,1024]{2,1,0:T(8,128)(2,1)S(1)} collective-permute-done((bf16[4,144,1024]{2,1,0:T(8,128)(2,1)S(1)}, bf16[4,144,1024]{2,1,0:T(8,128)(2,1)S(1)}, u32[]{:S(2)}, u32[]{:S(2)}) %collective-permute-start.9) | collective-permute-done | bytes 1179680 | tf_op jit(solution)/shard_map/ppermute | solution.py:1265
  363.1 10.0 %back_block.3 = (f32[1024,512]{1,0:T(8,128)S(1)}, f32[3,8,512]{2,1,0:T(8,128)S(1)}, bf16[8,4,48,1024]{3,2,1,0:T(8,128)(2,1)}, bf16[8,4,48,1024]{3,2,1,0:T(8,128)(2,1)}) custom-call(s32[8]{0:T(128)S(1)} %bitcast.69, s32[5]{0:T(128)S(1)} %copy-done.6, s32[8]{0:T(128)S(1)} %bitcast.59, ...), custom_call_target="tpu_custom_call", output_to_operand_aliasing={{2}: (7, {}), {3}: (8, {})} | custom-call | flops 10000000000 | bytes 10000000 | tf_op jit(solution)/shard_map/back_block/pallas_call | solution.py:832
  394.8 7.2 %collective-permute-done.12 = bf16[64,1024]{1,0:T(8,128)(2,1)S(1)} collective-permute-done((bf16[64,1024]{1,0:T(8,128)(2,1)S(1)}, bf16[64,1024]{1,0:T(8,128)(2,1)S(1)}, u32[]{:S(2)}, u32[]{:S(2)}) %collective-permute-start.12) | collective-permute-done | bytes 131104 | tf_op jit(solution)/shard_map/ppermute | solution.py:1265
  406.8 5.4 %first_sum.3 = (bf16[2,4,80,1024]{3,2,1,0:T(8,128)(2,1)S(1)}, bf16[2,4,80,1024]{3,2,1,0:T(8,128)(2,1)S(1)}, bf16[2,4,80,1024]{3,2,1,0:T(8,128)(2,1)S(1)}, bf16[2,4,80,1024]{3,2,1,0:T(8,128)(2,1)S(1)}) custom-call(s32[5]{0:T(128)S(1)} %copy-done.6, bf16[2,2,2,4,32,1024]{5,4,3,2,1,0:T(8,128)(2,1)} %bitcast.48, ...), custom_call_target="tpu_custom_call" | custom-call | flops 6000000000 | bytes 6000000 | tf_op jit(solution)/shard_map/first_sum/pallas_call | solution.py:1039
  414.5 28.2 %collective-permute-done.16.refs_1_.refs_5_ = bf16[2,4,80,1024]{3,2,1,0:T(8,128)(2,1)S(1)} collective-permute-done((bf16[2,4,80,1024]{3,2,1,0:T(8,128)(2,1)S(1)}, bf16[2,4,80,1024]{3,2,1,0:T(8,128)(2,1)S(1)}, u32[]{:S(2)}, u32[]{:S(2)}) %collective-permute-start.16) | collective-permute-done | bytes 1310752 | tf_op jit(solution)/shard_map/ppermute | solution.py:1265
  450.5 10.2 %all-to-all-done.7.x = bf16[4,2,144,1024]{3,2,1,0:T(8,128)(2,1)} async-done(((bf16[4,2,144,1024]{3,2,1,0:T(8,128)(2,1)}), bf16[4,2,144,1024]{3,2,1,0:T(8,128)(2,1)}, u32[]{:S(2)}, u32[]{:S(2)}) %all-to-all-start.7) | async-done | bytes 2359328 | tf_op jit(solution)/shard_map/all_to_all | solution.py:1297
  490.3 12.0 %collective-permute-done.24.refs_2_ = bf16[2,80,1024]{2,1,0:T(8,128)(2,1)} collective-permute-done((bf16[2,80,1024]{2,1,0:T(8,128)(2,1)S(1)}, bf16[2,80,1024]{2,1,0:T(8,128)(2,1)}, u32[]{:S(2)}, u32[]{:S(2)}) %collective-permute-start.24) | collective-permute-done | bytes 327712 | tf_op jit(solution)/shard_map/ppermute | solution.py:1265
  (214 shorter events, 158.4 us)
Async XLA Ops:
  24.0 44.3 %all-to-all-start = ((bf16[8,192,512]{2,1,0:T(8,128)(2,1)}), bf16[8,192,512]{2,1,0:T(8,128)(2,1)S(1)}, u32[]{:S(2)}, u32[]{:S(2)}) async-start(bf16[8,192,512]{2,1,0:T(8,128)(2,1)} %qkv_block.2), calls=%async_computation | async-start | bytes 3145728 | tf_op jit(solution)/shard_map/all_to_all | solution.py:1402
  68.3 41.3 %all-to-all-start.2 = ((bf16[8,192,512]{2,1,0:T(8,128)(2,1)}), bf16[8,192,512]{2,1,0:T(8,128)(2,1)S(1)}, u32[]{:S(2)}, u32[]{:S(2)}) async-start(bf16[8,192,512]{2,1,0:T(8,128)(2,1)} %qkv_block.3), calls=%async_computation.2 | async-start | bytes 3145728 | tf_op jit(solution)/shard_map/all_to_all | solution.py:1402
  110.2 28.5 %all-to-all-start.1 = ((bf16[8,64,512]{2,1,0:T(8,128)(2,1)}), bf16[8,64,512]{2,1,0:T(8,128)(2,1)S(1)}, u32[]{:S(2)}, u32[]{:S(2)}) async-start(bf16[8,64,512]{2,1,0:T(8,128)(2,1)} %get-tuple-element.99.o_ref), calls=%async_computation.1 | async-start | bytes 1048576 | tf_op jit(solution)/shard_map/all_to_all | solution.py:1415
  138.8 20.7 %all-to-all-start.3 = ((bf16[8,64,512]{2,1,0:T(8,128)(2,1)}), bf16[8,64,512]{2,1,0:T(8,128)(2,1)}, u32[]{:S(2)}, u32[]{:S(2)}) async-start(bf16[8,64,512]{2,1,0:T(8,128)(2,1)} %get-tuple-element.103.o_ref), calls=%async_computation.3 | async-start | bytes 1048576 | tf_op jit(solution)/shard_map/all_to_all | solution.py:1415
  210.3 15.1 %collective-permute-start.3 = (bf16[8,4,144,1024]{3,2,1,0:T(8,128)(2,1)}, bf16[8,4,144,1024]{3,2,1,0:T(8,128)(2,1)}, u32[]{:S(2)}, u32[]{:S(2)}) collective-permute-start(bf16[8,4,144,1024]{3,2,1,0:T(8,128)(2,1)} %get-tuple-element.108), channel_id=1, source_target_pairs={{0,1},{1,0},{2,3},{3,2},{4,5},{5,4},{6,7},{7,6},{8,9},{9,8},{10,11... | collective-permute-start | bytes 28311560 | tf_op jit(solution)/shard_map/ppermute | solution.py:1265
  210.4 31.1 %all-to-all-start.4 = ((bf16[8,128,512]{2,1,0:T(8,128)(2,1)}), bf16[8,128,512]{2,1,0:T(8,128)(2,1)}, u32[]{:S(2)}, u32[]{:S(2)}) async-start(bf16[8,128,512]{2,1,0:T(8,128)(2,1)} %get-tuple-element.106), calls=%async_computation.4 | async-start | bytes 2097152 | tf_op jit(solution)/shard_map/all_to_all | solution.py:1435
  237.8 37.4 %collective-permute-start.6 = (bf16[2,4,64,1024]{3,2,1,0:T(8,128)(2,1)}, bf16[2,4,64,1024]{3,2,1,0:T(8,128)(2,1)S(1)}, u32[]{:S(2)}, u32[]{:S(2)}) collective-permute-start(bf16[2,4,64,1024]{3,2,1,0:T(8,128)(2,1)} %get-tuple-element.109), channel_id=1, source_target_pairs={{0,8},{8,0},{16,24},{24,16},{1,9},{9,1},{17,25},{25,17},{2,10},{10... | collective-permute-start | bytes 3145736 | tf_op jit(solution)/shard_map/ppermute | solution.py:1265
  237.8 37.4 %collective-permute-start.7 = (bf16[2,4,64,1024]{3,2,1,0:T(8,128)(2,1)}, bf16[2,4,64,1024]{3,2,1,0:T(8,128)(2,1)S(1)}, u32[]{:S(2)}, u32[]{:S(2)}) collective-permute-start(bf16[2,4,64,1024]{3,2,1,0:T(8,128)(2,1)} %get-tuple-element.111), channel_id=1, source_target_pairs={{0,16},{8,24},{16,0},{24,8},{1,17},{9,25},{17,1},{25,9},{2,18},{10... | collective-permute-start | bytes 3145736 | tf_op jit(solution)/shard_map/ppermute | solution.py:1265
  273.6 37.9 %collective-permute-start.5 = (bf16[2,4,80,1024]{3,2,1,0:T(8,128)(2,1)}, bf16[2,4,80,1024]{3,2,1,0:T(8,128)(2,1)}, u32[]{:S(2)}, u32[]{:S(2)}) collective-permute-start(bf16[2,4,80,1024]{3,2,1,0:T(8,128)(2,1)} %copy-done.9), channel_id=1, source_target_pairs={{0,16},{8,24},{16,0},{24,8},{1,17},{9,25},{17,1},{25,9},{2,18},{10... | collective-permute-start | bytes 3932168 | tf_op jit(solution)/shard_map/ppermute | solution.py:1265
  275.2 36.4 %collective-permute-start.4 = (bf16[2,4,80,1024]{3,2,1,0:T(8,128)(2,1)S(1)}, bf16[2,4,80,1024]{3,2,1,0:T(8,128)(2,1)}, u32[]{:S(2)}, u32[]{:S(2)}) collective-permute-start(bf16[2,4,80,1024]{3,2,1,0:T(8,128)(2,1)S(1)} %get-tuple-element.117), channel_id=1, source_target_pairs={{0,8},{8,0},{16,24},{24,16},{1,9},{9,1},{17,25},{25,17},{2,10},{10... | collective-permute-start | bytes 3932168 | tf_op jit(solution)/shard_map/ppermute | solution.py:1265
  275.2 42.1 %all-to-all-start.6 = ((bf16[8,192,512]{2,1,0:T(8,128)(2,1)}), bf16[8,192,512]{2,1,0:T(8,128)(2,1)}, u32[]{:S(2)}, u32[]{:S(2)}) async-start(bf16[8,192,512]{2,1,0:T(8,128)(2,1)} %attend_back.2), calls=%async_computation.6 | async-start | bytes 3145728 | tf_op jit(solution)/shard_map/all_to_all | solution.py:1445
  317.3 45.7 %all-to-all-start.5 = ((bf16[8,192,512]{2,1,0:T(8,128)(2,1)}), bf16[8,192,512]{2,1,0:T(8,128)(2,1)}, u32[]{:S(2)}, u32[]{:S(2)}) async-start(bf16[8,192,512]{2,1,0:T(8,128)(2,1)} %attend_back.3), calls=%async_computation.5 | async-start | bytes 3145728 | tf_op jit(solution)/shard_map/all_to_all | solution.py:1445
  327.7 28.5 %collective-permute-start.9 = (bf16[4,144,1024]{2,1,0:T(8,128)(2,1)S(1)}, bf16[4,144,1024]{2,1,0:T(8,128)(2,1)S(1)}, u32[]{:S(2)}, u32[]{:S(2)}) collective-permute-start(bf16[4,144,1024]{2,1,0:T(8,128)(2,1)S(1)} %get-tuple-element.129), channel_id=1, source_target_pairs={{0,8},{8,0},{16,24},{24,16},{1,9},{9,1},{17,25},{25,17},{2,10},{10... | collective-permute-start | bytes 3538952 | tf_op jit(solution)/shard_map/ppermute | solution.py:1265
  329.7 27.9 %collective-permute-start.8 = (bf16[4,144,1024]{2,1,0:T(8,128)(2,1)S(1)}, bf16[4,144,1024]{2,1,0:T(8,128)(2,1)S(1)}, u32[]{:S(2)}, u32[]{:S(2)}) collective-permute-start(bf16[4,144,1024]{2,1,0:T(8,128)(2,1)S(1)} %get-tuple-element.127), channel_id=1, source_target_pairs={{0,16},{8,24},{16,0},{24,8},{1,17},{9,25},{17,1},{25,9},{2,18},{10... | collective-permute-start | bytes 3538952 | tf_op jit(solution)/shard_map/ppermute | solution.py:1265
  373.1 33.7 %collective-permute-start.15 = (bf16[8,4,48,1024]{3,2,1,0:T(8,128)(2,1)}, bf16[8,4,48,1024]{3,2,1,0:T(8,128)(2,1)}, u32[]{:S(2)}, u32[]{:S(2)}) collective-permute-start(bf16[8,4,48,1024]{3,2,1,0:T(8,128)(2,1)} %get-tuple-element.151), channel_id=1, source_target_pairs={{0,1},{1,0},{2,3},{3,2},{4,5},{5,4},{6,7},{7,6},{8,9},{9,8},{10,11... | collective-permute-start | bytes 9437192 | tf_op jit(solution)/shard_map/ppermute | solution.py:1265
  382.7 24.1 %collective-permute-start.14 = (bf16[8,4,32,1024]{3,2,1,0:T(8,128)(2,1)S(1)}, bf16[8,4,32,1024]{3,2,1,0:T(8,128)(2,1)}, u32[]{:S(2)}, u32[]{:S(2)}) collective-permute-start(bf16[8,4,32,1024]{3,2,1,0:T(8,128)(2,1)S(1)} %get-tuple-element.149), channel_id=1, source_target_pairs={{0,1},{1,0},{2,3},{3,2},{4,5},{5,4},{6,7},{7,6},{8,9},{9,8},{10,11... | collective-permute-start | bytes 6291464 | tf_op jit(solution)/shard_map/ppermute | solution.py:1265
  402.0 58.7 %all-to-all-start.7 = ((bf16[4,2,144,1024]{3,2,1,0:T(8,128)(2,1)}), bf16[4,2,144,1024]{3,2,1,0:T(8,128)(2,1)}, u32[]{:S(2)}, u32[]{:S(2)}) async-start(bf16[4,2,144,1024]{3,2,1,0:T(8,128)(2,1)} %third_sum_all.1), calls=%async_computation.7 | async-start | bytes 4718592 | tf_op jit(solution)/shard_map/all_to_all | solution.py:1297
  413.3 29.4 %collective-permute-start.16 = (bf16[2,4,80,1024]{3,2,1,0:T(8,128)(2,1)S(1)}, bf16[2,4,80,1024]{3,2,1,0:T(8,128)(2,1)S(1)}, u32[]{:S(2)}, u32[]{:S(2)}) collective-permute-start(bf16[2,4,80,1024]{3,2,1,0:T(8,128)(2,1)S(1)} %get-tuple-element.153), channel_id=1, source_target_pairs={{0,8},{8,0},{16,24},{24,16},{1,9},{9,1},{17,25},{25,17},{2,10},{10... | collective-permute-start | bytes 3932168 | tf_op jit(solution)/shard_map/ppermute | solution.py:1265
  414.0 29.1 %collective-permute-start.17 = (bf16[2,4,80,1024]{3,2,1,0:T(8,128)(2,1)S(1)}, bf16[2,4,80,1024]{3,2,1,0:T(8,128)(2,1)S(1)}, u32[]{:S(2)}, u32[]{:S(2)}) collective-permute-start(bf16[2,4,80,1024]{3,2,1,0:T(8,128)(2,1)S(1)} %get-tuple-element.155), channel_id=1, source_target_pairs={{0,16},{8,24},{16,0},{24,8},{1,17},{9,25},{17,1},{25,9},{2,18},{10... | collective-permute-start | bytes 3932168 | tf_op jit(solution)/shard_map/ppermute | solution.py:1265
  478.4 23.8 %collective-permute-start.24 = (bf16[2,80,1024]{2,1,0:T(8,128)(2,1)S(1)}, bf16[2,80,1024]{2,1,0:T(8,128)(2,1)}, u32[]{:S(2)}, u32[]{:S(2)}) collective-permute-start(bf16[2,80,1024]{2,1,0:T(8,128)(2,1)S(1)} %copy-done.49), channel_id=1, source_target_pairs={{0,4},{1,5},{2,6},{3,7},{4,0},{5,1},{6,2},{7,3},{8,12},{9,13},{10,... | collective-permute-start | bytes 983048 | tf_op jit(solution)/shard_map/ppermute | solution.py:1265
  479.4 22.9 %collective-permute-start.25 = (bf16[2,80,1024]{2,1,0:T(8,128)(2,1)S(1)}, bf16[2,80,1024]{2,1,0:T(8,128)(2,1)}, u32[]{:S(2)}, u32[]{:S(2)}) collective-permute-start(bf16[2,80,1024]{2,1,0:T(8,128)(2,1)S(1)} %copy-done.48), channel_id=1, source_target_pairs={{0,6},{1,7},{2,4},{3,5},{4,2},{5,3},{6,0},{7,1},{8,14},{9,15},{10,... | collective-permute-start | bytes 983048 | tf_op jit(solution)/shard_map/ppermute | solution.py:1265
  481.0 43.7 %collective-permute-start.29 = (bf16[2,144,1024]{2,1,0:T(8,128)(2,1)}, bf16[2,144,1024]{2,1,0:T(8,128)(2,1)S(1)}, u32[]{:S(2)}, u32[]{:S(2)}) collective-permute-start(bf16[2,144,1024]{2,1,0:T(8,128)(2,1)} %fourth_sum_all.1.refs_0_), channel_id=1, source_target_pairs={{0,8},{8,0},{16,24},{24,16},{1,9},{9,1},{17,25},{25,17},{2,10},{10... | collective-permute-start | bytes 1769480 | tf_op jit(solution)/shard_map/ppermute | solution.py:1265
  481.7 43.0 %collective-permute-start.30 = (bf16[2,144,1024]{2,1,0:T(8,128)(2,1)}, bf16[2,144,1024]{2,1,0:T(8,128)(2,1)S(1)}, u32[]{:S(2)}, u32[]{:S(2)}) collective-permute-start(bf16[2,144,1024]{2,1,0:T(8,128)(2,1)} %fourth_sum_all.1.refs_0_), channel_id=1, source_target_pairs={{0,16},{8,24},{16,0},{24,8},{1,17},{9,25},{17,1},{25,9},{2,18},{10... | collective-permute-start | bytes 1769480 | tf_op jit(solution)/shard_map/ppermute | solution.py:1265
  488.5 36.2 %collective-permute-start.31 = (bf16[2,144,1024]{2,1,0:T(8,128)(2,1)S(1)}, bf16[2,144,1024]{2,1,0:T(8,128)(2,1)S(1)}, u32[]{:S(2)}, u32[]{:S(2)}) collective-permute-start(bf16[2,144,1024]{2,1,0:T(8,128)(2,1)S(1)} %copy-done.14), channel_id=1, source_target_pairs={{0,24},{8,16},{16,8},{24,0},{1,25},{9,17},{17,9},{25,1},{2,26},{10... | collective-permute-start | bytes 1769480 | tf_op jit(solution)/shard_map/ppermute | solution.py:1265
  (69 other events, 636.4 us)

commit v3 on v2

--- a/solution.py
+++ b/solution.py
@@ -1336,10 +1336,10 @@
     return [value] + [sum_exchange(value, "batch", i) for i in range(1, lax.axis_size("batch"))]
 
 
-def sum_z(value):
+def sum_z(value, token):
     away = value.astype(jnp.bfloat16)
     for j in range(1, lax.axis_size("seq") // 2):
-        value = value + sum_exchange(away, "seq", 2 * j).astype(jnp.float32)
+        value = value + after(sum_exchange(away, "seq", 2 * j), token).astype(jnp.float32)
     return value
 
 
@@ -1457,18 +1457,20 @@
         ahead = next(feed) and advance(feed, 1, acc) if c == 0 else []
     gh, small = norm_block(lengths_row, ids, acc, hidden, after_grad, mods_a, loss_mask, mid_small, biases)
     small = small + sum_exchange(small, "seq", 1)
-    small = sum_z(small)
+    skip_keep, skip_send = skip_block(ids, joinedT, gh, seq_ways, PARTS)
+    blocks = [(skip_keep, skip_send), (keep, send)]
+    rest = reduce_stages(ids, blocks, [5 * own // PARTS], False)
+    small = sum_z(small, next(rest)[0])
     moving = feed.send(small)
-    skip_keep, skip_send = skip_block(ids, joinedT, gh, seq_ways, PARTS)
-    blocks = [(after(skip_keep, small), skip_send), (keep, send)]
-    rest = reduce_stages(ids, blocks, [5 * own // PARTS], False)
-    advance(rest, 4)
+    advance(rest, 3)
     groups = gather_groups(after(small, *rest.send(moving[0])))
     numerator = float(group_frames * batch_ways)
     grad_w_ada, vectors, scale = ada_block(time3, groups, utts, numerator)
     grad_tokens, grad_skip = joined_block(gh, w_skip, scale)
     next(feed)
     feed = last_stage(feed, groups[-1])
+    next(rest)
+    rest.send(grad_tokens)
     rest = last_stage(rest)
 
     ff = w_up.shape[1]
@@ -1496,7 +1498,7 @@
     skip_part = 2 * own // PARTS
     grad_w_skip, grad_w_qkv = place_blocks(
         ids,
-        scale,
+        after(scale, grad_w_down),
         [rest],
         [(0, 0, skip_part, 0, width, 0, lambda k: span(k * skip_part, skip_part), whole_lanes)]
         + [

time: 538 us -> 536 us (level)
    all_to_all x1, waiting for transfers between devices: 10.2 us -> 3.8 us  [reduce_stages(): lax.all_to_all(away[0], 'seq', 0, 0, axis_index_groups=groups, tiled=True)]
    ppermute x32, waiting for transfers between devices: 93.9 us -> 99.7 us  [sum_exchange(): return lax.ppermute(value, axis, [(i, i ^ bit) for i in range(ways)])]
    unnamed x108 -> x112, local copies, waits for them, and re-layouts: 16.8 us -> 18.7 us
  transfers between devices with their start and end apart: 40 -> 40, of which waited for: 21 -> 25; matrix products, arithmetic and copies ran while one was open for 2% -> 2% of each run, Pallas kernels for 35% -> 35%
where the time goes in v3:
time: 536 us; the launch traced here: 529 us
  Pallas kernels  266 us (50%)
  waiting for transfers between devices  155 us (29%)
  starting transfers between devices  69.7 us (13%)
  local copies, waits for them, and re-layouts  27 us (5%)
  matrix products  8.29 us (2%)
    ppermute x32, waiting for transfers between devices, sum_exchange(): return lax.ppermute(value, axis, [(i, i ^ bit) for i in range(ways)])  99.7 us
    pallas_call x2, Pallas kernels, attend_back(): pl.pallas_call(functools.partial(bwd_kernel, utts, chunk), out_shape=jax....  64.2 us
    pallas_call x1, Pallas kernels, mid_block(): pl.pallas_call(functools.partial(mid_kernel, (seq_ways, heads_local, utts...  50.9 us
    pallas_call x2, Pallas kernels, attend(): pl.pallas_call(functools.partial(fwd_kernel, utts), out_shape=(jax.ShapeD...  49.8 us
    ppermute x32, starting transfers between devices, sum_exchange(): return lax.ppermute(value, axis, [(i, i ^ bit) for i in range(ways)])  32.9 us
    all_to_all x2, waiting for transfers between devices, shards(): received.append(exchange(packed))  31 us
    pallas_call x2, Pallas kernels, back_block(): pl.pallas_call(functools.partial(back_kernel, utts, seq_ways, chunk), out...  19.1 us
    unnamed x112, local copies, waits for them, and re-layouts  18.7 us
  transfers between devices with their start and end apart: 40, of which 25 were waited for; matrix products, arithmetic and copies ran while one was open for 2% of the time, Pallas kernels for 35%

profile of v3, /device:TPU:0, one launch (start us, length us, event | category | flops | bytes accessed | tf_op | source)
XLA Modules:
  0.0 528.7 jit_solution(3963341643923278729)
XLA Ops:
  7.3 8.0 %head_block.1 = (f32[512,1024]{1,0:T(8,128)}, bf16[2048,512]{1,0:T(8,128)(2,1)}, bf16[1024,512]{1,0:T(8,128)(2,1)S(1)}, bf16[512,1024]{1,0:T(8,128)(2,1)S(1)}) custom-call(s32[8]{0:T(128)S(1)} %bitcast.67, s32[5]{0:T(128)S(1)} %stack.23.ids_ref, s32[8]{0:T(128)S(1)} %bitcast.57, bf16[512,1024]{1,0:T(8,128)(2,1)S(1)} %bitcast.52, ...), custom_call_target="tpu_custom_call" | custom-call | flops 10000000000 | bytes 10000000 | tf_op jit(solution)/shard_map/head_block/pallas_call | solution.py:676
  17.2 6.8 %qkv_block.2 = bf16[8,192,512]{2,1,0:T(8,128)(2,1)} custom-call(s32[8]{0:T(128)} %bitcast.60, s32[5]{0:T(128)} %copy-done.4, s32[8]{0:T(128)} %bitcast.55, bf16[512,1024]{1,0:T(8,128)(2,1)} %copy-done.29, bf16[1024,3072]{1,0:T(8,128)(2,1)} %w_ref.8, bf16[1,3072]{1,0:T(2,128)(2,1)} %broadcast_in_dim.28.b_ref), custom_call_target="tpu_custom_call" | custom-call | flops 7500000256 | bytes 7500000 | tf_op jit(solution)/shard_map/qkv_block/pallas_call | solution.py:729
  24.0 6.5 %all-to-all-start = ((bf16[8,192,512]{2,1,0:T(8,128)(2,1)}), bf16[8,192,512]{2,1,0:T(8,128)(2,1)S(1)}, u32[]{:S(2)}, u32[]{:S(2)}) async-start(bf16[8,192,512]{2,1,0:T(8,128)(2,1)} %qkv_block.2), calls=%async_computation | async-start | bytes 3145728 | tf_op jit(solution)/shard_map/all_to_all | solution.py:1402
  30.4 5.3 %fusion.2.refs_3_ = f32[16,4096]{1,0:T(8,128)} fusion(bf16[1024,6144]{1,0:T(8,128)(2,1)} %param.32, f32[4096]{0:T(1024)S(1)} %slice_convert_fusion, bf16[8,1024]{1,0:T(8,128)(2,1)S(1)} %fusion.15), kind=kOutput, calls=%fused_computation.2 | convolution fusion | flops 134283264 | bytes 8683520 | tf_op jit(solution)/shard_map/dot_general | solution.py:1388
  35.7 6.8 %qkv_block.3 = bf16[8,192,512]{2,1,0:T(8,128)(2,1)} custom-call(s32[8]{0:T(128)} %bitcast.61, s32[5]{0:T(128)} %copy-done.4, s32[8]{0:T(128)} %bitcast.56, bf16[512,1024]{1,0:T(8,128)(2,1)} %copy-done.29, bf16[1024,3072]{1,0:T(8,128)(2,1)} %w_ref.8, bf16[1,3072]{1,0:T(2,128)(2,1)} %broadcast_in_dim.28.b_ref), custom_call_target="tpu_custom_call" | custom-call | flops 7500000256 | bytes 7500000 | tf_op jit(solution)/shard_map/qkv_block/pallas_call | solution.py:729
  42.5 25.8 %all-to-all-done.qkv_ref = bf16[8,192,512]{2,1,0:T(8,128)(2,1)S(1)} async-done(((bf16[8,192,512]{2,1,0:T(8,128)(2,1)}), bf16[8,192,512]{2,1,0:T(8,128)(2,1)S(1)}, u32[]{:S(2)}, u32[]{:S(2)}) %all-to-all-start) | async-done | bytes 1572896 | tf_op jit(solution)/shard_map/all_to_all | solution.py:1402
  79.6 24.8 %attend.2 = (bf16[8,64,512]{2,1,0:T(8,128)(2,1)}, f32[8,1,512]{2,1,0:T(1,128)}) custom-call(s32[8]{0:T(128)} %bitcast.62, bf16[8,192,512]{2,1,0:T(8,128)(2,1)} %copy-done.38, s32[8,1,512]{2,1,0:T(1,128)} %bitcast.90), custom_call_target="tpu_custom_call" | custom-call | flops 24999999488 | bytes 25000000 | tf_op jit(solution)/shard_map/attend/pallas_call | solution.py:135
  104.4 5.2 all-to-all-done.2.qkv_ref
  113.8 25.0 %attend.3 = (bf16[8,64,512]{2,1,0:T(8,128)(2,1)}, f32[8,1,512]{2,1,0:T(1,128)}) custom-call(s32[8]{0:T(128)} %bitcast.63, bf16[8,192,512]{2,1,0:T(8,128)(2,1)} %copy-done.37, s32[8,1,512]{2,1,0:T(1,128)} %bitcast.91), custom_call_target="tpu_custom_call" | custom-call | flops 24999999488 | bytes 25000000 | tf_op jit(solution)/shard_map/attend/pallas_call | solution.py:135
  138.8 5.2 all-to-all-start.3
  145.9 13.6 %all-to-all-done.3.refs_1_ = bf16[8,64,512]{2,1,0:T(8,128)(2,1)} async-done(((bf16[8,64,512]{2,1,0:T(8,128)(2,1)}), bf16[8,64,512]{2,1,0:T(8,128)(2,1)}, u32[]{:S(2)}, u32[]{:S(2)}) %all-to-all-start.3) | async-done | bytes 524320 | tf_op jit(solution)/shard_map/all_to_all | solution.py:1415
  159.4 50.9 %mid_block.1 = (bf16[512,1024]{1,0:T(8,128)(2,1)}, f32[512,1024]{1,0:T(8,128)}, f32[40,1024]{1,0:T(8,128)}, bf16[8,128,512]{2,1,0:T(8,128)(2,1)}, bf16[8,4,144,1...) custom-call(s32[8]{0:T(128)} %bitcast.64, s32[5]{0:T(128)} %copy-done.4, bf16[8,64,512]{2,1,0:T(8,128)(2,1)} %copy-done.41, ...), custom_call_target="tpu_custom_call" | custom-call | flops 49999998976 | bytes 50000000 | tf_op jit(solution)/shard_map/mid_block/pallas_call | solution.py:547
  214.9 10.5 %collective-permute-done.3 = bf16[8,4,144,1024]{3,2,1,0:T(8,128)(2,1)} collective-permute-done((bf16[8,4,144,1024]{3,2,1,0:T(8,128)(2,1)}, bf16[8,4,144,1024]{3,2,1,0:T(8,128)(2,1)}, u32[]{:S(2)}, u32[]{:S(2)}) %collective-permute-start.3) | collective-permute-done | bytes 9437216 | tf_op jit(solution)/shard_map/ppermute | solution.py:1265
  225.4 11.3 %first_sum.2 = (bf16[2,4,64,1024]{3,2,1,0:T(8,128)(2,1)}, bf16[2,4,80,1024]{3,2,1,0:T(8,128)(2,1)S(1)}, bf16[2,4,64,1024]{3,2,1,0:T(8,128)(2,1)}, bf16[2,4,80,10...) custom-call(s32[5]{0:T(128)S(1)} %copy-done.5, ...), custom_call_target="tpu_custom_call" | custom-call | flops 6000000000 | bytes 6000000 | tf_op jit(solution)/shard_map/first_sum/pallas_call | solution.py:1039
  241.5 32.1 %attend_back.2 = bf16[8,192,512]{2,1,0:T(8,128)(2,1)} custom-call(s32[8]{0:T(128)} %bitcast.65, bf16[8,192,512]{2,1,0:T(8,128)(2,1)} %copy-done.38, s32[8,1,512]{2,1,0:T(1,128)} %bitcast.92, bf16[8,64,512]{2,1,0:T(8,128)(2,1)} %get-tuple-element.105.o_ref, bf16[8,128,512]{2,1,0:T(8,128)(2,1)} %all-to-all-done.4.do_ref, f32[8,1,512]{2,1,0:T(1,128)} %get-tuple-element.120.lse_ref), custom_call_target="tpu_custom_call" | custom-call | flops 32000000000 | bytes 32000000 | tf_op jit(solution)/shard_map/attend_back/pallas_call | solution.py:257
  282.1 32.1 %attend_back.3 = bf16[8,192,512]{2,1,0:T(8,128)(2,1)} custom-call(s32[8]{0:T(128)} %bitcast.66, bf16[8,192,512]{2,1,0:T(8,128)(2,1)} %copy-done.37, s32[8,1,512]{2,1,0:T(1,128)} %bitcast.93, bf16[8,64,512]{2,1,0:T(8,128)(2,1)} %get-tuple-element.109.o_ref, bf16[8,128,512]{2,1,0:T(8,128)(2,1)} %all-to-all-done.4.do_ref, f32[8,1,512]{2,1,0:T(1,128)} %get-tuple-element.122.lse_ref), custom_call_target="tpu_custom_call" | custom-call | flops 32000000000 | bytes 32000000 | tf_op jit(solution)/shard_map/attend_back/pallas_call | solution.py:257
  314.2 5.7 %all-to-all-done.6.grad_ref = bf16[8,192,512]{2,1,0:T(8,128)(2,1)} async-done(((bf16[8,192,512]{2,1,0:T(8,128)(2,1)}), bf16[8,192,512]{2,1,0:T(8,128)(2,1)}, u32[]{:S(2)}, u32[]{:S(2)}) %all-to-all-start.6) | async-done | bytes 1572896 | tf_op jit(solution)/shard_map/all_to_all | solution.py:1445
  324.3 5.0 second_sum.2
  332.3 9.1 %back_block.2 = (f32[1024,512]{1,0:T(8,128)S(1)}, f32[3,8,512]{2,1,0:T(8,128)S(1)}, bf16[8,4,48,1024]{3,2,1,0:T(8,128)(2,1)}, bf16[8,4,48,1024]{3,2,1,0:T(8,128)(2,1)}) custom-call(s32[8]{0:T(128)S(1)} %bitcast.68, s32[5]{0:T(128)S(1)} %copy-done.5, s32[8]{0:T(128)S(1)} %bitcast.58, bf16[8,192,512]{2,1,0:T(8,128)(2,1)} %all-to-all-done.6.grad_ref, ...), custom_call_target="tpu_custom_call" | custom-call | flops 10000000000 | bytes 10000000 | tf_op jit(solution)/shard_map/back_block/pallas_call | solution.py:832
  342.7 16.0 %collective-permute-done.9.got_b = bf16[4,144,1024]{2,1,0:T(8,128)(2,1)S(1)} collective-permute-done((bf16[4,144,1024]{2,1,0:T(8,128)(2,1)S(1)}, bf16[4,144,1024]{2,1,0:T(8,128)(2,1)S(1)}, u32[]{:S(2)}, u32[]{:S(2)}) %collective-permute-start.9) | collective-permute-done | bytes 1179680 | tf_op jit(solution)/shard_map/ppermute | solution.py:1265
  365.7 10.0 %back_block.3 = (f32[1024,512]{1,0:T(8,128)S(1)}, f32[3,8,512]{2,1,0:T(8,128)S(1)}, bf16[8,4,48,1024]{3,2,1,0:T(8,128)(2,1)}, bf16[8,4,48,1024]{3,2,1,0:T(8,128)(2,1)}) custom-call(s32[8]{0:T(128)S(1)} %bitcast.69, s32[5]{0:T(128)S(1)} %copy-done.6, s32[8]{0:T(128)S(1)} %bitcast.59, ...), custom_call_target="tpu_custom_call", output_to_operand_aliasing={{2}: (7, {}), {3}: (8, {})} | custom-call | flops 10000000000 | bytes 10000000 | tf_op jit(solution)/shard_map/back_block/pallas_call | solution.py:832
  396.9 5.4 %first_sum.3 = (bf16[2,4,80,1024]{3,2,1,0:T(8,128)(2,1)S(1)}, bf16[2,4,80,1024]{3,2,1,0:T(8,128)(2,1)S(1)}, bf16[2,4,80,1024]{3,2,1,0:T(8,128)(2,1)S(1)}, bf16[2,4,80,1024]{3,2,1,0:T(8,128)(2,1)S(1)}) custom-call(s32[5]{0:T(128)S(1)} %copy-done.6, bf16[2,2,2,4,32,1024]{5,4,3,2,1,0:T(8,128)(2,1)} %bitcast.48, bf16[2,2,2,4,32,1024]{5,4,3,2,1,0:T(8,128)(2,1)} %bitcast.83, ...), custom_call_target="tpu_custom_call" | custom-call | flops 6000000000 | bytes 6000000 | tf_op jit(solution)/shard_map/first_sum/pallas_call | solution.py:1039
  410.5 29.3 %collective-permute-done.16.refs_1_.refs_5_ = bf16[2,4,80,1024]{3,2,1,0:T(8,128)(2,1)S(1)} collective-permute-done((bf16[2,4,80,1024]{3,2,1,0:T(8,128)(2,1)}, bf16[2,4,80,1024]{3,2,1,0:T(8,128)(2,1)S(1)}, u32[]{:S(2)}, u32[]{:S(2)}) %collective-permute-start.16) | collective-permute-done | bytes 1310752 | tf_op jit(solution)/shard_map/ppermute | solution.py:1265
  447.2 13.0 %collective-permute-done.19.got_b = bf16[4,80,1024]{2,1,0:T(8,128)(2,1)S(1)} collective-permute-done((bf16[4,80,1024]{2,1,0:T(8,128)(2,1)S(1)}, bf16[4,80,1024]{2,1,0:T(8,128)(2,1)S(1)}, u32[]{:S(2)}, u32[]{:S(2)}) %collective-permute-start.19) | collective-permute-done | bytes 655392 | tf_op jit(solution)/shard_map/ppermute | solution.py:1265
  (218 shorter events, 163.7 us)
Async XLA Ops:
  24.0 44.3 %all-to-all-start = ((bf16[8,192,512]{2,1,0:T(8,128)(2,1)}), bf16[8,192,512]{2,1,0:T(8,128)(2,1)S(1)}, u32[]{:S(2)}, u32[]{:S(2)}) async-start(bf16[8,192,512]{2,1,0:T(8,128)(2,1)} %qkv_block.2), calls=%async_computation | async-start | bytes 3145728 | tf_op jit(solution)/shard_map/all_to_all | solution.py:1402
  68.3 41.3 %all-to-all-start.2 = ((bf16[8,192,512]{2,1,0:T(8,128)(2,1)}), bf16[8,192,512]{2,1,0:T(8,128)(2,1)S(1)}, u32[]{:S(2)}, u32[]{:S(2)}) async-start(bf16[8,192,512]{2,1,0:T(8,128)(2,1)} %qkv_block.3), calls=%async_computation.2 | async-start | bytes 3145728 | tf_op jit(solution)/shard_map/all_to_all | solution.py:1402
  110.2 28.5 %all-to-all-start.1 = ((bf16[8,64,512]{2,1,0:T(8,128)(2,1)}), bf16[8,64,512]{2,1,0:T(8,128)(2,1)S(1)}, u32[]{:S(2)}, u32[]{:S(2)}) async-start(bf16[8,64,512]{2,1,0:T(8,128)(2,1)} %get-tuple-element.105.o_ref), calls=%async_computation.1 | async-start | bytes 1048576 | tf_op jit(solution)/shard_map/all_to_all | solution.py:1415
  138.8 20.7 %all-to-all-start.3 = ((bf16[8,64,512]{2,1,0:T(8,128)(2,1)}), bf16[8,64,512]{2,1,0:T(8,128)(2,1)}, u32[]{:S(2)}, u32[]{:S(2)}) async-start(bf16[8,64,512]{2,1,0:T(8,128)(2,1)} %get-tuple-element.109.o_ref), calls=%async_computation.3 | async-start | bytes 1048576 | tf_op jit(solution)/shard_map/all_to_all | solution.py:1415
  210.4 31.1 %all-to-all-start.4 = ((bf16[8,128,512]{2,1,0:T(8,128)(2,1)}), bf16[8,128,512]{2,1,0:T(8,128)(2,1)}, u32[]{:S(2)}, u32[]{:S(2)}) async-start(bf16[8,128,512]{2,1,0:T(8,128)(2,1)} %get-tuple-element.112), calls=%async_computation.4 | async-start | bytes 2097152 | tf_op jit(solution)/shard_map/all_to_all | solution.py:1435
  237.8 40.0 %collective-permute-start.6 = (bf16[2,4,64,1024]{3,2,1,0:T(8,128)(2,1)}, bf16[2,4,64,1024]{3,2,1,0:T(8,128)(2,1)S(1)}, u32[]{:S(2)}, u32[]{:S(2)}) collective-permute-start(bf16[2,4,64,1024]{3,2,1,0:T(8,128)(2,1)} %get-tuple-element.115), channel_id=1, source_target_pairs={{0,8},{8,0},{16,24},{24,16},{1,9},{9,1},{17,25},{25,17},{2,10},{10... | collective-permute-start | bytes 3145736 | tf_op jit(solution)/shard_map/ppermute | solution.py:1265
  237.8 40.0 %collective-permute-start.7 = (bf16[2,4,64,1024]{3,2,1,0:T(8,128)(2,1)}, bf16[2,4,64,1024]{3,2,1,0:T(8,128)(2,1)S(1)}, u32[]{:S(2)}, u32[]{:S(2)}) collective-permute-start(bf16[2,4,64,1024]{3,2,1,0:T(8,128)(2,1)} %get-tuple-element.117), channel_id=1, source_target_pairs={{0,16},{8,24},{16,0},{24,8},{1,17},{9,25},{17,1},{25,9},{2,18},{10... | collective-permute-start | bytes 3145736 | tf_op jit(solution)/shard_map/ppermute | solution.py:1265
  273.5 40.6 %collective-permute-start.5 = (bf16[2,4,80,1024]{3,2,1,0:T(8,128)(2,1)}, bf16[2,4,80,1024]{3,2,1,0:T(8,128)(2,1)}, u32[]{:S(2)}, u32[]{:S(2)}) collective-permute-start(bf16[2,4,80,1024]{3,2,1,0:T(8,128)(2,1)} %copy-done.9), channel_id=1, source_target_pairs={{0,16},{8,24},{16,0},{24,8},{1,17},{9,25},{17,1},{25,9},{2,18},{10... | collective-permute-start | bytes 3932168 | tf_op jit(solution)/shard_map/ppermute | solution.py:1265
  277.8 36.4 %collective-permute-start.4 = (bf16[2,4,80,1024]{3,2,1,0:T(8,128)(2,1)S(1)}, bf16[2,4,80,1024]{3,2,1,0:T(8,128)(2,1)}, u32[]{:S(2)}, u32[]{:S(2)}) collective-permute-start(bf16[2,4,80,1024]{3,2,1,0:T(8,128)(2,1)S(1)} %get-tuple-element.123), channel_id=1, source_target_pairs={{0,8},{8,0},{16,24},{24,16},{1,9},{9,1},{17,25},{25,17},{2,10},{10... | collective-permute-start | bytes 3932168 | tf_op jit(solution)/shard_map/ppermute | solution.py:1265
  277.8 42.2 %all-to-all-start.6 = ((bf16[8,192,512]{2,1,0:T(8,128)(2,1)}), bf16[8,192,512]{2,1,0:T(8,128)(2,1)}, u32[]{:S(2)}, u32[]{:S(2)}) async-start(bf16[8,192,512]{2,1,0:T(8,128)(2,1)} %attend_back.2), calls=%async_computation.6 | async-start | bytes 3145728 | tf_op jit(solution)/shard_map/all_to_all | solution.py:1445
  319.9 45.8 %all-to-all-start.5 = ((bf16[8,192,512]{2,1,0:T(8,128)(2,1)}), bf16[8,192,512]{2,1,0:T(8,128)(2,1)}, u32[]{:S(2)}, u32[]{:S(2)}) async-start(bf16[8,192,512]{2,1,0:T(8,128)(2,1)} %attend_back.3), calls=%async_computation.5 | async-start | bytes 3145728 | tf_op jit(solution)/shard_map/all_to_all | solution.py:1445
  330.3 28.5 %collective-permute-start.9 = (bf16[4,144,1024]{2,1,0:T(8,128)(2,1)S(1)}, bf16[4,144,1024]{2,1,0:T(8,128)(2,1)S(1)}, u32[]{:S(2)}, u32[]{:S(2)}) collective-permute-start(bf16[4,144,1024]{2,1,0:T(8,128)(2,1)S(1)} %get-tuple-element.135), channel_id=1, source_target_pairs={{0,8},{8,0},{16,24},{24,16},{1,9},{9,1},{17,25},{25,17},{2,10},{10... | collective-permute-start | bytes 3538952 | tf_op jit(solution)/shard_map/ppermute | solution.py:1265
  332.3 27.9 %collective-permute-start.8 = (bf16[4,144,1024]{2,1,0:T(8,128)(2,1)S(1)}, bf16[4,144,1024]{2,1,0:T(8,128)(2,1)S(1)}, u32[]{:S(2)}, u32[]{:S(2)}) collective-permute-start(bf16[4,144,1024]{2,1,0:T(8,128)(2,1)S(1)} %get-tuple-element.133), channel_id=1, source_target_pairs={{0,16},{8,24},{16,0},{24,8},{1,17},{9,25},{17,1},{25,9},{2,18},{10... | collective-permute-start | bytes 3538952 | tf_op jit(solution)/shard_map/ppermute | solution.py:1265
  375.8 18.8 %collective-permute-start.13 = (bf16[8,4,48,1024]{3,2,1,0:T(8,128)(2,1)}, bf16[8,4,48,1024]{3,2,1,0:T(8,128)(2,1)S(1)}, u32[]{:S(2)}, u32[]{:S(2)}) collective-permute-start(bf16[8,4,48,1024]{3,2,1,0:T(8,128)(2,1)} %get-tuple-element.156), channel_id=1, source_target_pairs={{0,1},{1,0},{2,3},{3,2},{4,5},{5,4},{6,7},{7,6},{8,9},{9,8},{10,11... | collective-permute-start | bytes 9437192 | tf_op jit(solution)/shard_map/ppermute | solution.py:1265
  404.8 59.1 %all-to-all-start.7 = ((bf16[4,2,144,1024]{3,2,1,0:T(8,128)(2,1)}), bf16[4,2,144,1024]{3,2,1,0:T(8,128)(2,1)}, u32[]{:S(2)}, u32[]{:S(2)}) async-start(bf16[4,2,144,1024]{3,2,1,0:T(8,128)(2,1)} %third_sum_all.1), calls=%async_computation.7 | async-start | bytes 4718592 | tf_op jit(solution)/shard_map/all_to_all | solution.py:1297
  409.8 30.0 %collective-permute-start.16 = (bf16[2,4,80,1024]{3,2,1,0:T(8,128)(2,1)}, bf16[2,4,80,1024]{3,2,1,0:T(8,128)(2,1)S(1)}, u32[]{:S(2)}, u32[]{:S(2)}) collective-permute-start(bf16[2,4,80,1024]{3,2,1,0:T(8,128)(2,1)} %copy-done.11), channel_id=1, source_target_pairs={{0,8},{8,0},{16,24},{24,16},{1,9},{9,1},{17,25},{25,17},{2,10},{10... | collective-permute-start | bytes 3932168 | tf_op jit(solution)/shard_map/ppermute | solution.py:1265
  410.5 29.5 %collective-permute-start.17 = (bf16[2,4,80,1024]{3,2,1,0:T(8,128)(2,1)S(1)}, bf16[2,4,80,1024]{3,2,1,0:T(8,128)(2,1)S(1)}, u32[]{:S(2)}, u32[]{:S(2)}) collective-permute-start(bf16[2,4,80,1024]{3,2,1,0:T(8,128)(2,1)S(1)} %get-tuple-element.163), channel_id=1, source_target_pairs={{0,16},{8,24},{16,0},{24,8},{1,17},{9,25},{17,1},{25,9},{2,18},{10... | collective-permute-start | bytes 3932168 | tf_op jit(solution)/shard_map/ppermute | solution.py:1265
  472.6 24.3 %collective-permute-start.28 = (bf16[2,80,1024]{2,1,0:T(8,128)(2,1)}, bf16[2,80,1024]{2,1,0:T(8,128)(2,1)S(1)}, u32[]{:S(2)}, u32[]{:S(2)}) collective-permute-start(bf16[2,80,1024]{2,1,0:T(8,128)(2,1)} %get-tuple-element.173), channel_id=1, source_target_pairs={{0,6},{1,7},{2,4},{3,5},{4,2},{5,3},{6,0},{7,1},{8,14},{9,15},{10,... | collective-permute-start | bytes 983048 | tf_op jit(solution)/shard_map/ppermute | solution.py:1265
  474.0 26.4 %collective-permute-start.27 = (bf16[2,80,1024]{2,1,0:T(8,128)(2,1)}, bf16[2,80,1024]{2,1,0:T(8,128)(2,1)}, u32[]{:S(2)}, u32[]{:S(2)}) collective-permute-start(bf16[2,80,1024]{2,1,0:T(8,128)(2,1)} %get-tuple-element.172), channel_id=1, source_target_pairs={{0,4},{1,5},{2,6},{3,7},{4,0},{5,1},{6,2},{7,3},{8,12},{9,13},{10,... | collective-permute-start | bytes 983048 | tf_op jit(solution)/shard_map/ppermute | solution.py:1265
  478.5 22.0 %collective-permute-start.26 = (bf16[2,80,1024]{2,1,0:T(8,128)(2,1)}, bf16[2,80,1024]{2,1,0:T(8,128)(2,1)}, u32[]{:S(2)}, u32[]{:S(2)}) collective-permute-start(bf16[2,80,1024]{2,1,0:T(8,128)(2,1)} %get-tuple-element.171), channel_id=1, source_target_pairs={{0,2},{1,3},{2,0},{3,1},{4,6},{5,7},{6,4},{7,5},{8,10},{9,11},{10,... | collective-permute-start | bytes 983048 | tf_op jit(solution)/shard_map/ppermute | solution.py:1265
  481.8 21.7 %collective-permute-start.23 = (bf16[2,144,1024]{2,1,0:T(8,128)(2,1)}, bf16[2,144,1024]{2,1,0:T(8,128)(2,1)S(1)}, u32[]{:S(2)}, u32[]{:S(2)}) collective-permute-start(bf16[2,144,1024]{2,1,0:T(8,128)(2,1)} %fourth_sum_all.1.refs_0_), channel_id=1, source_target_pairs={{0,8},{8,0},{16,24},{24,16},{1,9},{9,1},{17,25},{25,17},{2,10},{10... | collective-permute-start | bytes 1769480 | tf_op jit(solution)/shard_map/ppermute | solution.py:1265
  483.1 26.1 %collective-permute-start.24 = (bf16[2,144,1024]{2,1,0:T(8,128)(2,1)}, bf16[2,144,1024]{2,1,0:T(8,128)(2,1)S(1)}, u32[]{:S(2)}, u32[]{:S(2)}) collective-permute-start(bf16[2,144,1024]{2,1,0:T(8,128)(2,1)} %fourth_sum_all.1.refs_0_), channel_id=1, source_target_pairs={{0,16},{8,24},{16,0},{24,8},{1,17},{9,25},{17,1},{25,9},{2,18},{10... | collective-permute-start | bytes 1769480 | tf_op jit(solution)/shard_map/ppermute | solution.py:1265
  502.6 17.9 %collective-permute-start.29 = (bf16[2,80,1024]{2,1,0:T(8,128)(2,1)}, bf16[2,80,1024]{2,1,0:T(8,128)(2,1)S(1)}, u32[]{:S(2)}, u32[]{:S(2)}) collective-permute-start(bf16[2,80,1024]{2,1,0:T(8,128)(2,1)} %fourth_sum.1.refs_0_), channel_id=1, source_target_pairs={{0,8},{8,0},{16,24},{24,16},{1,9},{9,1},{17,25},{25,17},{2,10},{10... | collective-permute-start | bytes 983048 | tf_op jit(solution)/shard_map/ppermute | solution.py:1265
  503.6 22.5 %collective-permute-start.31 = (bf16[2,80,1024]{2,1,0:T(8,128)(2,1)}, bf16[2,80,1024]{2,1,0:T(8,128)(2,1)S(1)}, u32[]{:S(2)}, u32[]{:S(2)}) collective-permute-start(bf16[2,80,1024]{2,1,0:T(8,128)(2,1)} %fourth_sum.1.refs_0_), channel_id=1, source_target_pairs={{0,24},{8,16},{16,8},{24,0},{1,25},{9,17},{17,9},{25,1},{2,26},{10... | collective-permute-start | bytes 983048 | tf_op jit(solution)/shard_map/ppermute | solution.py:1265
  (71 other events, 642.0 us)

commit v4 on v3

--- a/solution.py
+++ b/solution.py
@@ -1333,13 +1333,15 @@
 
 
 def gather_groups(value):
-    return [value] + [sum_exchange(value, "batch", i) for i in range(1, lax.axis_size("batch"))]
-
-
-def sum_z(value, token):
     away = value.astype(jnp.bfloat16)
+    others = [sum_exchange(away, "batch", i) for i in range(1, lax.axis_size("batch"))]
+    return [value] + [other.astype(value.dtype) for other in others]
+
+
+def sum_z(value, tokens):
+    away = after(value.astype(jnp.bfloat16), *tokens)
     for j in range(1, lax.axis_size("seq") // 2):
-        value = value + after(sum_exchange(away, "seq", 2 * j), token).astype(jnp.float32)
+        value = value + sum_exchange(away, "seq", 2 * j).astype(jnp.float32)
     return value
 
 
@@ -1460,10 +1462,10 @@
     skip_keep, skip_send = skip_block(ids, joinedT, gh, seq_ways, PARTS)
     blocks = [(skip_keep, skip_send), (keep, send)]
     rest = reduce_stages(ids, blocks, [5 * own // PARTS], False)
-    small = sum_z(small, next(rest)[0])
-    moving = feed.send(small)
-    advance(rest, 3)
-    groups = gather_groups(after(small, *rest.send(moving[0])))
+    moving = next(feed)
+    small = sum_z(small, moving + advance(rest, 3))
+    next(rest)
+    groups = gather_groups(after(small, *next(rest)))
     numerator = float(group_frames * batch_ways)
     grad_w_ada, vectors, scale = ada_block(time3, groups, utts, numerator)
     grad_tokens, grad_skip = joined_block(gh, w_skip, scale)

time: 536 us -> 526 us (0.981)
  the two profiles are of different devices: /device:TPU:0 before, /device:TPU:8 now
where the time goes in v4:
time: 526 us; the launch traced here: 517 us
  Pallas kernels  266 us (51%)
  waiting for transfers between devices  128 us (24%)
  starting transfers between devices  85.9 us (16%)
  local copies, waits for them, and re-layouts  22.7 us (4%)
  matrix products  8.32 us (2%)
    ppermute x32, waiting for transfers between devices, sum_exchange(): return lax.ppermute(value, axis, [(i, i ^ bit) for i in range(ways)])  83.7 us
    pallas_call x2, Pallas kernels, attend_back(): pl.pallas_call(functools.partial(bwd_kernel, utts, chunk), out_shape=jax....  64.2 us
    pallas_call x1, Pallas kernels, mid_block(): pl.pallas_call(functools.partial(mid_kernel, (seq_ways, heads_local, utts...  50.8 us
    pallas_call x2, Pallas kernels, attend(): pl.pallas_call(functools.partial(fwd_kernel, utts), out_shape=(jax.ShapeD...  49.8 us
    ppermute x32, starting transfers between devices, sum_exchange(): return lax.ppermute(value, axis, [(i, i ^ bit) for i in range(ways)])  32.6 us
    all_to_all x2, waiting for transfers between devices, shards(): received.append(exchange(packed))  24.1 us
    pallas_call x2, Pallas kernels, back_block(): pl.pallas_call(functools.partial(back_kernel, utts, seq_ways, chunk), out...  19.1 us
    pallas_call x2, Pallas kernels, first_sum(): pl.pallas_call(functools.partial(first_kernel, len(pairs), len(splits)),...  16.8 us
  transfers between devices with their start and end apart: 40, of which 22 were waited for; matrix products, arithmetic and copies ran while one was open for 3% of the time, Pallas kernels for 36%

profile of v4, /device:TPU:8, one launch (start us, length us, event | category | flops | bytes accessed | tf_op | source)
XLA Modules:
  0.0 516.6 jit_solution(15791861306912458353)
XLA Ops:
  7.3 8.0 %head_block.1 = (f32[512,1024]{1,0:T(8,128)}, bf16[2048,512]{1,0:T(8,128)(2,1)}, bf16[1024,512]{1,0:T(8,128)(2,1)S(1)}, bf16[512,1024]{1,0:T(8,128)(2,1)S(1)}) custom-call(s32[8]{0:T(128)S(1)} %bitcast.67, s32[5]{0:T(128)S(1)} %stack.23.ids_ref, s32[8]{0:T(128)S(1)} %bitcast.57, bf16[512,1024]{1,0:T(8,128)(2,1)S(1)} %bitcast.52, ...), custom_call_target="tpu_custom_call" | custom-call | flops 10000000000 | bytes 10000000 | tf_op jit(solution)/shard_map/head_block/pallas_call | solution.py:676
  17.2 6.8 %qkv_block.2 = bf16[8,192,512]{2,1,0:T(8,128)(2,1)} custom-call(s32[8]{0:T(128)} %bitcast.60, s32[5]{0:T(128)} %copy-done.4, s32[8]{0:T(128)} %bitcast.55, bf16[512,1024]{1,0:T(8,128)(2,1)} %copy-done.26, bf16[1024,3072]{1,0:T(8,128)(2,1)} %w_ref.8, bf16[1,3072]{1,0:T(2,128)(2,1)} %broadcast_in_dim.28.b_ref), custom_call_target="tpu_custom_call" | custom-call | flops 7500000256 | bytes 7500000 | tf_op jit(solution)/shard_map/qkv_block/pallas_call | solution.py:729
  24.0 5.4 %all-to-all-start = ((bf16[8,192,512]{2,1,0:T(8,128)(2,1)}), bf16[8,192,512]{2,1,0:T(8,128)(2,1)S(1)}, u32[]{:S(2)}, u32[]{:S(2)}) async-start(bf16[8,192,512]{2,1,0:T(8,128)(2,1)} %qkv_block.2), calls=%async_computation | async-start | bytes 3145728 | tf_op jit(solution)/shard_map/all_to_all | solution.py:1404
  34.7 6.8 %qkv_block.3 = bf16[8,192,512]{2,1,0:T(8,128)(2,1)} custom-call(s32[8]{0:T(128)} %bitcast.61, s32[5]{0:T(128)} %copy-done.4, s32[8]{0:T(128)} %bitcast.56, bf16[512,1024]{1,0:T(8,128)(2,1)} %copy-done.26, bf16[1024,3072]{1,0:T(8,128)(2,1)} %w_ref.8, bf16[1,3072]{1,0:T(2,128)(2,1)} %broadcast_in_dim.28.b_ref), custom_call_target="tpu_custom_call" | custom-call | flops 7500000256 | bytes 7500000 | tf_op jit(solution)/shard_map/qkv_block/pallas_call | solution.py:729
  41.5 22.3 %all-to-all-done.qkv_ref = bf16[8,192,512]{2,1,0:T(8,128)(2,1)S(1)} async-done(((bf16[8,192,512]{2,1,0:T(8,128)(2,1)}), bf16[8,192,512]{2,1,0:T(8,128)(2,1)S(1)}, u32[]{:S(2)}, u32[]{:S(2)}) %all-to-all-start) | async-done | bytes 1572896 | tf_op jit(solution)/shard_map/all_to_all | solution.py:1404
  63.8 7.0 %all-to-all-start.2 = ((bf16[8,192,512]{2,1,0:T(8,128)(2,1)}), bf16[8,192,512]{2,1,0:T(8,128)(2,1)S(1)}, u32[]{:S(2)}, u32[]{:S(2)}) async-start(bf16[8,192,512]{2,1,0:T(8,128)(2,1)} %qkv_block.3), calls=%async_computation.2 | async-start | bytes 3145728 | tf_op jit(solution)/shard_map/all_to_all | solution.py:1404
  78.4 24.8 %attend.2 = (bf16[8,64,512]{2,1,0:T(8,128)(2,1)}, f32[8,1,512]{2,1,0:T(1,128)}) custom-call(s32[8]{0:T(128)} %bitcast.62, bf16[8,192,512]{2,1,0:T(8,128)(2,1)} %copy-done.33, s32[8,1,512]{2,1,0:T(1,128)} %bitcast.82), custom_call_target="tpu_custom_call" | custom-call | flops 24999999488 | bytes 25000000 | tf_op jit(solution)/shard_map/attend/pallas_call | solution.py:135
  105.7 6.9 %all-to-all-start.1 = ((bf16[8,64,512]{2,1,0:T(8,128)(2,1)}), bf16[8,64,512]{2,1,0:T(8,128)(2,1)S(1)}, u32[]{:S(2)}, u32[]{:S(2)}) async-start(bf16[8,64,512]{2,1,0:T(8,128)(2,1)} %get-tuple-element.100.o_ref), calls=%async_computation.1 | async-start | bytes 1048576 | tf_op jit(solution)/shard_map/all_to_all | solution.py:1417
  112.6 25.0 %attend.3 = (bf16[8,64,512]{2,1,0:T(8,128)(2,1)}, f32[8,1,512]{2,1,0:T(1,128)}) custom-call(s32[8]{0:T(128)} %bitcast.63, bf16[8,192,512]{2,1,0:T(8,128)(2,1)} %copy-done.32, s32[8,1,512]{2,1,0:T(1,128)} %bitcast.83), custom_call_target="tpu_custom_call" | custom-call | flops 24999999488 | bytes 25000000 | tf_op jit(solution)/shard_map/attend/pallas_call | solution.py:135
  144.8 10.3 %all-to-all-done.3.refs_1_ = bf16[8,64,512]{2,1,0:T(8,128)(2,1)} async-done(((bf16[8,64,512]{2,1,0:T(8,128)(2,1)}), bf16[8,64,512]{2,1,0:T(8,128)(2,1)}, u32[]{:S(2)}, u32[]{:S(2)}) %all-to-all-start.3) | async-done | bytes 524320 | tf_op jit(solution)/shard_map/all_to_all | solution.py:1417
  155.1 50.8 %mid_block.1 = (bf16[512,1024]{1,0:T(8,128)(2,1)}, f32[512,1024]{1,0:T(8,128)}, f32[40,1024]{1,0:T(8,128)}, bf16[8,128,512]{2,1,0:T(8,128)(2,1)}, bf16[8,4,144,1...) custom-call(s32[8]{0:T(128)} %bitcast.64, s32[5]{0:T(128)} %copy-done.4, bf16[8,64,512]{2,1,0:T(8,128)(2,1)} %copy-done.37, ...), custom_call_target="tpu_custom_call" | custom-call | flops 49999998976 | bytes 50000000 | tf_op jit(solution)/shard_map/mid_block/pallas_call | solution.py:547
  206.1 7.7 %all-to-all-start.4 = ((bf16[8,128,512]{2,1,0:T(8,128)(2,1)}), bf16[8,128,512]{2,1,0:T(8,128)(2,1)}, u32[]{:S(2)}, u32[]{:S(2)}) async-start(bf16[8,128,512]{2,1,0:T(8,128)(2,1)} %get-tuple-element.107), calls=%async_computation.4 | async-start | bytes 2097152 | tf_op jit(solution)/shard_map/all_to_all | solution.py:1437
  213.8 7.3 %collective-permute-done.3 = bf16[8,4,144,1024]{3,2,1,0:T(8,128)(2,1)} collective-permute-done((bf16[8,4,144,1024]{3,2,1,0:T(8,128)(2,1)}, bf16[8,4,144,1024]{3,2,1,0:T(8,128)(2,1)}, u32[]{:S(2)}, u32[]{:S(2)}) %collective-permute-start.3) | collective-permute-done | bytes 9437216 | tf_op jit(solution)/shard_map/ppermute | solution.py:1265
  221.1 11.3 %first_sum.2 = (bf16[2,4,64,1024]{3,2,1,0:T(8,128)(2,1)}, bf16[2,4,80,1024]{3,2,1,0:T(8,128)(2,1)S(1)}, bf16[2,4,64,1024]{3,2,1,0:T(8,128)(2,1)}, bf16[2,4,80,10...) custom-call(s32[5]{0:T(128)S(1)} %copy-done.5, ...), custom_call_target="tpu_custom_call" | custom-call | flops 6000000000 | bytes 6000000 | tf_op jit(solution)/shard_map/first_sum/pallas_call | solution.py:1039
  236.8 32.2 %attend_back.2 = bf16[8,192,512]{2,1,0:T(8,128)(2,1)} custom-call(s32[8]{0:T(128)} %bitcast.65, bf16[8,192,512]{2,1,0:T(8,128)(2,1)} %copy-done.33, s32[8,1,512]{2,1,0:T(1,128)} %bitcast.84, bf16[8,64,512]{2,1,0:T(8,128)(2,1)} %get-tuple-element.100.o_ref, bf16[8,128,512]{2,1,0:T(8,128)(2,1)} %all-to-all-done.4.do_ref, f32[8,1,512]{2,1,0:T(1,128)} %get-tuple-element.115.lse_ref), custom_call_target="tpu_custom_call" | custom-call | flops 32000000000 | bytes 32000000 | tf_op jit(solution)/shard_map/attend_back/pallas_call | solution.py:257
  270.5 7.8 %all-to-all-start.6 = ((bf16[8,192,512]{2,1,0:T(8,128)(2,1)}), bf16[8,192,512]{2,1,0:T(8,128)(2,1)}, u32[]{:S(2)}, u32[]{:S(2)}) async-start(bf16[8,192,512]{2,1,0:T(8,128)(2,1)} %attend_back.2), calls=%async_computation.6 | async-start | bytes 3145728 | tf_op jit(solution)/shard_map/all_to_all | solution.py:1447
  278.3 32.1 %attend_back.3 = bf16[8,192,512]{2,1,0:T(8,128)(2,1)} custom-call(s32[8]{0:T(128)} %bitcast.66, bf16[8,192,512]{2,1,0:T(8,128)(2,1)} %copy-done.32, s32[8,1,512]{2,1,0:T(1,128)} %bitcast.85, bf16[8,64,512]{2,1,0:T(8,128)(2,1)} %get-tuple-element.104.o_ref, bf16[8,128,512]{2,1,0:T(8,128)(2,1)} %all-to-all-done.4.do_ref, f32[8,1,512]{2,1,0:T(1,128)} %get-tuple-element.117.lse_ref), custom_call_target="tpu_custom_call" | custom-call | flops 32000000000 | bytes 32000000 | tf_op jit(solution)/shard_map/attend_back/pallas_call | solution.py:257
  312.7 7.8 %all-to-all-start.5 = ((bf16[8,192,512]{2,1,0:T(8,128)(2,1)}), bf16[8,192,512]{2,1,0:T(8,128)(2,1)}, u32[]{:S(2)}, u32[]{:S(2)}) async-start(bf16[8,192,512]{2,1,0:T(8,128)(2,1)} %attend_back.3), calls=%async_computation.5 | async-start | bytes 3145728 | tf_op jit(solution)/shard_map/all_to_all | solution.py:1447
  329.0 9.1 %back_block.2 = (f32[1024,512]{1,0:T(8,128)S(1)}, f32[3,8,512]{2,1,0:T(8,128)S(1)}, bf16[8,4,48,1024]{3,2,1,0:T(8,128)(2,1)}, bf16[8,4,48,1024]{3,2,1,0:T(8,128)(2,1)}) custom-call(s32[8]{0:T(128)S(1)} %bitcast.68, s32[5]{0:T(128)S(1)} %copy-done.5, s32[8]{0:T(128)S(1)} %bitcast.58, bf16[8,192,512]{2,1,0:T(8,128)(2,1)} %all-to-all-done.6.grad_ref, ...), custom_call_target="tpu_custom_call" | custom-call | flops 10000000000 | bytes 10000000 | tf_op jit(solution)/shard_map/back_block/pallas_call | solution.py:832
  339.4 15.3 %collective-permute-done.9.got_b = bf16[4,144,1024]{2,1,0:T(8,128)(2,1)S(1)} collective-permute-done((bf16[4,144,1024]{2,1,0:T(8,128)(2,1)S(1)}, bf16[4,144,1024]{2,1,0:T(8,128)(2,1)S(1)}, u32[]{:S(2)}, u32[]{:S(2)}) %collective-permute-start.9) | collective-permute-done | bytes 1179680 | tf_op jit(solution)/shard_map/ppermute | solution.py:1265
  361.7 10.0 %back_block.3 = (f32[1024,512]{1,0:T(8,128)S(1)}, f32[3,8,512]{2,1,0:T(8,128)S(1)}, bf16[8,4,48,1024]{3,2,1,0:T(8,128)(2,1)}, bf16[8,4,48,1024]{3,2,1,0:T(8,128)(2,1)}) custom-call(s32[8]{0:T(128)S(1)} %bitcast.69, s32[5]{0:T(128)S(1)} %copy-done.6, s32[8]{0:T(128)S(1)} %bitcast.59, ...), custom_call_target="tpu_custom_call", output_to_operand_aliasing={{2}: (7, {}), {3}: (8, {})} | custom-call | flops 10000000000 | bytes 10000000 | tf_op jit(solution)/shard_map/back_block/pallas_call | solution.py:832
  387.2 5.4 %first_sum.3 = (bf16[2,4,80,1024]{3,2,1,0:T(8,128)(2,1)S(1)}, bf16[2,4,80,1024]{3,2,1,0:T(8,128)(2,1)S(1)}, bf16[2,4,80,1024]{3,2,1,0:T(8,128)(2,1)S(1)}, bf16[2,4,80,1024]{3,2,1,0:T(8,128)(2,1)S(1)}) custom-call(s32[5]{0:T(128)S(1)} %copy-done.6, bf16[2,2,2,4,32,1024]{5,4,3,2,1,0:T(8,128)(2,1)} %bitcast.48, ...), custom_call_target="tpu_custom_call" | custom-call | flops 6000000000 | bytes 6000000 | tf_op jit(solution)/shard_map/first_sum/pallas_call | solution.py:1039
  395.8 28.2 %collective-permute-done.13.refs_1_.refs_5_ = bf16[2,4,80,1024]{3,2,1,0:T(8,128)(2,1)S(1)} collective-permute-done((bf16[2,4,80,1024]{3,2,1,0:T(8,128)(2,1)S(1)}, bf16[2,4,80,1024]{3,2,1,0:T(8,128)(2,1)S(1)}, u32[]{:S(2)}, u32[]{:S(2)}) %collective-permute-start.13) | collective-permute-done | bytes 1310752 | tf_op jit(solution)/shard_map/ppermute | solution.py:1265
  431.9 6.0 %all-to-all-done.7.x = bf16[4,2,144,1024]{3,2,1,0:T(8,128)(2,1)} async-done(((bf16[4,2,144,1024]{3,2,1,0:T(8,128)(2,1)}), bf16[4,2,144,1024]{3,2,1,0:T(8,128)(2,1)}, u32[]{:S(2)}, u32[]{:S(2)}) %all-to-all-start.7) | async-done | bytes 2359328 | tf_op jit(solution)/shard_map/all_to_all | solution.py:1297
  (202 shorter events, 160.7 us)
Async XLA Ops:
  24.0 39.8 %all-to-all-start = ((bf16[8,192,512]{2,1,0:T(8,128)(2,1)}), bf16[8,192,512]{2,1,0:T(8,128)(2,1)S(1)}, u32[]{:S(2)}, u32[]{:S(2)}) async-start(bf16[8,192,512]{2,1,0:T(8,128)(2,1)} %qkv_block.2), calls=%async_computation | async-start | bytes 3145728 | tf_op jit(solution)/shard_map/all_to_all | solution.py:1404
  63.8 41.3 %all-to-all-start.2 = ((bf16[8,192,512]{2,1,0:T(8,128)(2,1)}), bf16[8,192,512]{2,1,0:T(8,128)(2,1)S(1)}, u32[]{:S(2)}, u32[]{:S(2)}) async-start(bf16[8,192,512]{2,1,0:T(8,128)(2,1)} %qkv_block.3), calls=%async_computation.2 | async-start | bytes 3145728 | tf_op jit(solution)/shard_map/all_to_all | solution.py:1404
  105.7 31.9 %all-to-all-start.1 = ((bf16[8,64,512]{2,1,0:T(8,128)(2,1)}), bf16[8,64,512]{2,1,0:T(8,128)(2,1)S(1)}, u32[]{:S(2)}, u32[]{:S(2)}) async-start(bf16[8,64,512]{2,1,0:T(8,128)(2,1)} %get-tuple-element.100.o_ref), calls=%async_computation.1 | async-start | bytes 1048576 | tf_op jit(solution)/shard_map/all_to_all | solution.py:1417
  206.1 30.7 %all-to-all-start.4 = ((bf16[8,128,512]{2,1,0:T(8,128)(2,1)}), bf16[8,128,512]{2,1,0:T(8,128)(2,1)}, u32[]{:S(2)}, u32[]{:S(2)}) async-start(bf16[8,128,512]{2,1,0:T(8,128)(2,1)} %get-tuple-element.107), calls=%async_computation.4 | async-start | bytes 2097152 | tf_op jit(solution)/shard_map/all_to_all | solution.py:1437
  233.5 37.0 %collective-permute-start.6 = (bf16[2,4,64,1024]{3,2,1,0:T(8,128)(2,1)}, bf16[2,4,64,1024]{3,2,1,0:T(8,128)(2,1)S(1)}, u32[]{:S(2)}, u32[]{:S(2)}) collective-permute-start(bf16[2,4,64,1024]{3,2,1,0:T(8,128)(2,1)} %get-tuple-element.110), channel_id=1, source_target_pairs={{0,8},{8,0},{16,24},{24,16},{1,9},{9,1},{17,25},{25,17},{2,10},{10... | collective-permute-start | bytes 3145736 | tf_op jit(solution)/shard_map/ppermute | solution.py:1265
  235.0 35.5 %collective-permute-start.7 = (bf16[2,4,64,1024]{3,2,1,0:T(8,128)(2,1)}, bf16[2,4,64,1024]{3,2,1,0:T(8,128)(2,1)S(1)}, u32[]{:S(2)}, u32[]{:S(2)}) collective-permute-start(bf16[2,4,64,1024]{3,2,1,0:T(8,128)(2,1)} %get-tuple-element.112), channel_id=1, source_target_pairs={{0,16},{8,24},{16,0},{24,8},{1,17},{9,25},{17,1},{25,9},{2,18},{10... | collective-permute-start | bytes 3145736 | tf_op jit(solution)/shard_map/ppermute | solution.py:1265
  269.0 41.4 %collective-permute-start.5 = (bf16[2,4,80,1024]{3,2,1,0:T(8,128)(2,1)}, bf16[2,4,80,1024]{3,2,1,0:T(8,128)(2,1)}, u32[]{:S(2)}, u32[]{:S(2)}) collective-permute-start(bf16[2,4,80,1024]{3,2,1,0:T(8,128)(2,1)} %copy-done.9), channel_id=1, source_target_pairs={{0,16},{8,24},{16,0},{24,8},{1,17},{9,25},{17,1},{25,9},{2,18},{10... | collective-permute-start | bytes 3932168 | tf_op jit(solution)/shard_map/ppermute | solution.py:1265
  270.5 39.9 %collective-permute-start.4 = (bf16[2,4,80,1024]{3,2,1,0:T(8,128)(2,1)S(1)}, bf16[2,4,80,1024]{3,2,1,0:T(8,128)(2,1)}, u32[]{:S(2)}, u32[]{:S(2)}) collective-permute-start(bf16[2,4,80,1024]{3,2,1,0:T(8,128)(2,1)S(1)} %get-tuple-element.118), channel_id=1, source_target_pairs={{0,8},{8,0},{16,24},{24,16},{1,9},{9,1},{17,25},{25,17},{2,10},{10... | collective-permute-start | bytes 3932168 | tf_op jit(solution)/shard_map/ppermute | solution.py:1265
  270.5 42.2 %all-to-all-start.6 = ((bf16[8,192,512]{2,1,0:T(8,128)(2,1)}), bf16[8,192,512]{2,1,0:T(8,128)(2,1)}, u32[]{:S(2)}, u32[]{:S(2)}) async-start(bf16[8,192,512]{2,1,0:T(8,128)(2,1)} %attend_back.2), calls=%async_computation.6 | async-start | bytes 3145728 | tf_op jit(solution)/shard_map/all_to_all | solution.py:1447
  312.7 49.0 %all-to-all-start.5 = ((bf16[8,192,512]{2,1,0:T(8,128)(2,1)}), bf16[8,192,512]{2,1,0:T(8,128)(2,1)}, u32[]{:S(2)}, u32[]{:S(2)}) async-start(bf16[8,192,512]{2,1,0:T(8,128)(2,1)} %attend_back.3), calls=%async_computation.5 | async-start | bytes 3145728 | tf_op jit(solution)/shard_map/all_to_all | solution.py:1447
  326.5 28.3 %collective-permute-start.9 = (bf16[4,144,1024]{2,1,0:T(8,128)(2,1)S(1)}, bf16[4,144,1024]{2,1,0:T(8,128)(2,1)S(1)}, u32[]{:S(2)}, u32[]{:S(2)}) collective-permute-start(bf16[4,144,1024]{2,1,0:T(8,128)(2,1)S(1)} %get-tuple-element.130), channel_id=1, source_target_pairs={{0,8},{8,0},{16,24},{24,16},{1,9},{9,1},{17,25},{25,17},{2,10},{10... | collective-permute-start | bytes 3538952 | tf_op jit(solution)/shard_map/ppermute | solution.py:1265
  328.5 27.7 %collective-permute-start.8 = (bf16[4,144,1024]{2,1,0:T(8,128)(2,1)S(1)}, bf16[4,144,1024]{2,1,0:T(8,128)(2,1)S(1)}, u32[]{:S(2)}, u32[]{:S(2)}) collective-permute-start(bf16[4,144,1024]{2,1,0:T(8,128)(2,1)S(1)} %get-tuple-element.128), channel_id=1, source_target_pairs={{0,16},{8,24},{16,0},{24,8},{1,17},{9,25},{17,1},{25,9},{2,18},{10... | collective-permute-start | bytes 3538952 | tf_op jit(solution)/shard_map/ppermute | solution.py:1265
  381.8 56.1 %all-to-all-start.7 = ((bf16[4,2,144,1024]{3,2,1,0:T(8,128)(2,1)}), bf16[4,2,144,1024]{3,2,1,0:T(8,128)(2,1)}, u32[]{:S(2)}, u32[]{:S(2)}) async-start(bf16[4,2,144,1024]{3,2,1,0:T(8,128)(2,1)} %third_sum_all.1), calls=%async_computation.7 | async-start | bytes 4718592 | tf_op jit(solution)/shard_map/all_to_all | solution.py:1297
  393.8 30.2 %collective-permute-start.13 = (bf16[2,4,80,1024]{3,2,1,0:T(8,128)(2,1)S(1)}, bf16[2,4,80,1024]{3,2,1,0:T(8,128)(2,1)S(1)}, u32[]{:S(2)}, u32[]{:S(2)}) collective-permute-start(bf16[2,4,80,1024]{3,2,1,0:T(8,128)(2,1)S(1)} %get-tuple-element.153), channel_id=1, source_target_pairs={{0,8},{8,0},{16,24},{24,16},{1,9},{9,1},{17,25},{25,17},{2,10},{10... | collective-permute-start | bytes 3932168 | tf_op jit(solution)/shard_map/ppermute | solution.py:1265
  394.5 29.9 %collective-permute-start.14 = (bf16[2,4,80,1024]{3,2,1,0:T(8,128)(2,1)S(1)}, bf16[2,4,80,1024]{3,2,1,0:T(8,128)(2,1)S(1)}, u32[]{:S(2)}, u32[]{:S(2)}) collective-permute-start(bf16[2,4,80,1024]{3,2,1,0:T(8,128)(2,1)S(1)} %get-tuple-element.155), channel_id=1, source_target_pairs={{0,16},{8,24},{16,0},{24,8},{1,17},{9,25},{17,1},{25,9},{2,18},{10... | collective-permute-start | bytes 3932168 | tf_op jit(solution)/shard_map/ppermute | solution.py:1265
  395.8 36.1 %collective-permute-start.10 = (f32[64,1024]{1,0:T(8,128)S(1)}, f32[64,1024]{1,0:T(8,128)S(1)}, u32[]{:S(2)}, u32[]{:S(2)}) collective-permute-start(f32[64,1024]{1,0:T(8,128)S(1)} %get-tuple-element.146), channel_id=1, source_target_pairs={{0,1},{1,0},{2,3},{3,2},{4,5},{5,4},{6,7},{7,6},{8,9},{9,8},{10,11... | collective-permute-start | bytes 786440 | tf_op jit(solution)/shard_map/ppermute | solution.py:1265
  429.9 24.0 %collective-permute-start.18 = (bf16[4,80,1024]{2,1,0:T(8,128)(2,1)S(1)}, bf16[4,80,1024]{2,1,0:T(8,128)(2,1)}, u32[]{:S(2)}, u32[]{:S(2)}) collective-permute-start(bf16[4,80,1024]{2,1,0:T(8,128)(2,1)S(1)} %get-tuple-element.156), channel_id=1, source_target_pairs={{0,16},{8,24},{16,0},{24,8},{1,17},{9,25},{17,1},{25,9},{2,18},{10... | collective-permute-start | bytes 1966088 | tf_op jit(solution)/shard_map/ppermute | solution.py:1265
  431.2 22.7 %collective-permute-start.19 = (bf16[4,80,1024]{2,1,0:T(8,128)(2,1)S(1)}, bf16[4,80,1024]{2,1,0:T(8,128)(2,1)}, u32[]{:S(2)}, u32[]{:S(2)}) collective-permute-start(bf16[4,80,1024]{2,1,0:T(8,128)(2,1)S(1)} %get-tuple-element.157), channel_id=1, source_target_pairs={{0,8},{8,0},{16,24},{24,16},{1,9},{9,1},{17,25},{25,17},{2,10},{10... | collective-permute-start | bytes 1966088 | tf_op jit(solution)/shard_map/ppermute | solution.py:1265
  464.7 20.3 %collective-permute-start.28 = (bf16[2,80,1024]{2,1,0:T(8,128)(2,1)}, bf16[2,80,1024]{2,1,0:T(8,128)(2,1)}, u32[]{:S(2)}, u32[]{:S(2)}) collective-permute-start(bf16[2,80,1024]{2,1,0:T(8,128)(2,1)} %get-tuple-element.163), channel_id=1, source_target_pairs={{0,6},{1,7},{2,4},{3,5},{4,2},{5,3},{6,0},{7,1},{8,14},{9,15},{10,... | collective-permute-start | bytes 983048 | tf_op jit(solution)/shard_map/ppermute | solution.py:1265
  465.2 24.5 %collective-permute-start.27 = (bf16[2,80,1024]{2,1,0:T(8,128)(2,1)}, bf16[2,80,1024]{2,1,0:T(8,128)(2,1)}, u32[]{:S(2)}, u32[]{:S(2)}) collective-permute-start(bf16[2,80,1024]{2,1,0:T(8,128)(2,1)} %get-tuple-element.162), channel_id=1, source_target_pairs={{0,4},{1,5},{2,6},{3,7},{4,0},{5,1},{6,2},{7,3},{8,12},{9,13},{10,... | collective-permute-start | bytes 983048 | tf_op jit(solution)/shard_map/ppermute | solution.py:1265
  467.1 22.6 %collective-permute-start.26 = (bf16[2,80,1024]{2,1,0:T(8,128)(2,1)}, bf16[2,80,1024]{2,1,0:T(8,128)(2,1)}, u32[]{:S(2)}, u32[]{:S(2)}) collective-permute-start(bf16[2,80,1024]{2,1,0:T(8,128)(2,1)} %get-tuple-element.161), channel_id=1, source_target_pairs={{0,2},{1,3},{2,0},{3,1},{4,6},{5,7},{6,4},{7,5},{8,10},{9,11},{10,... | collective-permute-start | bytes 983048 | tf_op jit(solution)/shard_map/ppermute | solution.py:1265
  468.9 25.0 %collective-permute-start.23 = (bf16[2,144,1024]{2,1,0:T(8,128)(2,1)}, bf16[2,144,1024]{2,1,0:T(8,128)(2,1)S(1)}, u32[]{:S(2)}, u32[]{:S(2)}) collective-permute-start(bf16[2,144,1024]{2,1,0:T(8,128)(2,1)} %fourth_sum_all.1.refs_0_), channel_id=1, source_target_pairs={{0,8},{8,0},{16,24},{24,16},{1,9},{9,1},{17,25},{25,17},{2,10},{10... | collective-permute-start | bytes 1769480 | tf_op jit(solution)/shard_map/ppermute | solution.py:1265
  470.3 28.1 %collective-permute-start.24 = (bf16[2,144,1024]{2,1,0:T(8,128)(2,1)}, bf16[2,144,1024]{2,1,0:T(8,128)(2,1)S(1)}, u32[]{:S(2)}, u32[]{:S(2)}) collective-permute-start(bf16[2,144,1024]{2,1,0:T(8,128)(2,1)} %fourth_sum_all.1.refs_0_), channel_id=1, source_target_pairs={{0,16},{8,24},{16,0},{24,8},{1,17},{9,25},{17,1},{25,9},{2,18},{10... | collective-permute-start | bytes 1769480 | tf_op jit(solution)/shard_map/ppermute | solution.py:1265
  493.9 20.1 %collective-permute-start.31 = (bf16[2,80,1024]{2,1,0:T(8,128)(2,1)}, bf16[2,80,1024]{2,1,0:T(8,128)(2,1)S(1)}, u32[]{:S(2)}, u32[]{:S(2)}) collective-permute-start(bf16[2,80,1024]{2,1,0:T(8,128)(2,1)} %fourth_sum.1.refs_0_), channel_id=1, source_target_pairs={{0,24},{8,16},{16,8},{24,0},{1,25},{9,17},{17,9},{25,1},{2,26},{10... | collective-permute-start | bytes 983048 | tf_op jit(solution)/shard_map/ppermute | solution.py:1265
  (61 other events, 532.3 us)

commit v5 on v4

--- a/solution.py
+++ b/solution.py
@@ -1465,11 +1465,11 @@
     moving = next(feed)
     small = sum_z(small, moving + advance(rest, 3))
     next(rest)
-    groups = gather_groups(after(small, *next(rest)))
+    moving = next(rest)
+    groups = gather_groups(after(small, *moving, *next(feed)))
     numerator = float(group_frames * batch_ways)
     grad_w_ada, vectors, scale = ada_block(time3, groups, utts, numerator)
     grad_tokens, grad_skip = joined_block(gh, w_skip, scale)
-    next(feed)
     feed = last_stage(feed, groups[-1])
     next(rest)
     rest.send(grad_tokens)

time: 526 us -> 523 us (level)
  the two profiles are of different devices: /device:TPU:8 before, /device:TPU:0 now
where the time goes in v5:
time: 523 us; the launch traced here: 515 us
  Pallas kernels  266 us (51%)
  waiting for transfers between devices  137 us (26%)
  starting transfers between devices  75.6 us (14%)
  local copies, waits for them, and re-layouts  22.9 us (4%)
  matrix products  8.32 us (2%)
    ppermute x32, waiting for transfers between devices, sum_exchange(): return lax.ppermute(value, axis, [(i, i ^ bit) for i in range(ways)])  78.5 us
    pallas_call x2, Pallas kernels, attend_back(): pl.pallas_call(functools.partial(bwd_kernel, utts, chunk), out_shape=jax....  64.3 us
    pallas_call x1, Pallas kernels, mid_block(): pl.pallas_call(functools.partial(mid_kernel, (seq_ways, heads_local, utts...  50.8 us
    pallas_call x2, Pallas kernels, attend(): pl.pallas_call(functools.partial(fwd_kernel, utts), out_shape=(jax.ShapeD...  49.8 us
    ppermute x32, starting transfers between devices, sum_exchange(): return lax.ppermute(value, axis, [(i, i ^ bit) for i in range(ways)])  38.7 us
    all_to_all x2, waiting for transfers between devices, shards(): received.append(exchange(packed))  30.9 us
    pallas_call x2, Pallas kernels, back_block(): pl.pallas_call(functools.partial(back_kernel, utts, seq_ways, chunk), out...  19.1 us
    pallas_call x2, Pallas kernels, first_sum(): pl.pallas_call(functools.partial(first_kernel, len(pairs), len(splits)),...  16.8 us
  transfers between devices with their start and end apart: 40, of which 19 were waited for; matrix products, arithmetic and copies ran while one was open for 3% of the time, Pallas kernels for 36%

profile of v5, /device:TPU:0, one launch (start us, length us, event | category | flops | bytes accessed | tf_op | source)
XLA Modules:
  0.0 515.4 jit_solution(7282014734939039207)
XLA Ops:
  7.3 8.0 %head_block.1 = (f32[512,1024]{1,0:T(8,128)}, bf16[2048,512]{1,0:T(8,128)(2,1)}, bf16[1024,512]{1,0:T(8,128)(2,1)S(1)}, bf16[512,1024]{1,0:T(8,128)(2,1)S(1)}) custom-call(s32[8]{0:T(128)S(1)} %bitcast.67, s32[5]{0:T(128)S(1)} %stack.23.ids_ref, s32[8]{0:T(128)S(1)} %bitcast.57, bf16[512,1024]{1,0:T(8,128)(2,1)S(1)} %bitcast.52, ...), custom_call_target="tpu_custom_call" | custom-call | flops 10000000000 | bytes 10000000 | tf_op jit(solution)/shard_map/head_block/pallas_call | solution.py:676
  17.2 6.7 %qkv_block.2 = bf16[8,192,512]{2,1,0:T(8,128)(2,1)} custom-call(s32[8]{0:T(128)} %bitcast.60, s32[5]{0:T(128)} %copy-done.4, s32[8]{0:T(128)} %bitcast.55, bf16[512,1024]{1,0:T(8,128)(2,1)} %copy-done.26, bf16[1024,3072]{1,0:T(8,128)(2,1)} %w_ref.8, bf16[1,3072]{1,0:T(2,128)(2,1)} %broadcast_in_dim.28.b_ref), custom_call_target="tpu_custom_call" | custom-call | flops 7500000256 | bytes 7500000 | tf_op jit(solution)/shard_map/qkv_block/pallas_call | solution.py:729
  23.9 6.5 %all-to-all-start = ((bf16[8,192,512]{2,1,0:T(8,128)(2,1)}), bf16[8,192,512]{2,1,0:T(8,128)(2,1)S(1)}, u32[]{:S(2)}, u32[]{:S(2)}) async-start(bf16[8,192,512]{2,1,0:T(8,128)(2,1)} %qkv_block.2), calls=%async_computation | async-start | bytes 3145728 | tf_op jit(solution)/shard_map/all_to_all | solution.py:1404
  30.4 5.3 %fusion.2.refs_3_ = f32[16,4096]{1,0:T(8,128)} fusion(bf16[1024,6144]{1,0:T(8,128)(2,1)} %param.32, f32[4096]{0:T(1024)S(1)} %slice_convert_fusion, bf16[8,1024]{1,0:T(8,128)(2,1)S(1)} %fusion.15), kind=kOutput, calls=%fused_computation.2 | convolution fusion | flops 134283264 | bytes 8683520 | tf_op jit(solution)/shard_map/dot_general | solution.py:1390
  35.7 6.8 %qkv_block.3 = bf16[8,192,512]{2,1,0:T(8,128)(2,1)} custom-call(s32[8]{0:T(128)} %bitcast.61, s32[5]{0:T(128)} %copy-done.4, s32[8]{0:T(128)} %bitcast.56, bf16[512,1024]{1,0:T(8,128)(2,1)} %copy-done.26, bf16[1024,3072]{1,0:T(8,128)(2,1)} %w_ref.8, bf16[1,3072]{1,0:T(2,128)(2,1)} %broadcast_in_dim.28.b_ref), custom_call_target="tpu_custom_call" | custom-call | flops 7500000256 | bytes 7500000 | tf_op jit(solution)/shard_map/qkv_block/pallas_call | solution.py:729
  42.5 25.7 %all-to-all-done.qkv_ref = bf16[8,192,512]{2,1,0:T(8,128)(2,1)S(1)} async-done(((bf16[8,192,512]{2,1,0:T(8,128)(2,1)}), bf16[8,192,512]{2,1,0:T(8,128)(2,1)S(1)}, u32[]{:S(2)}, u32[]{:S(2)}) %all-to-all-start) | async-done | bytes 1572896 | tf_op jit(solution)/shard_map/all_to_all | solution.py:1404
  79.6 24.8 %attend.2 = (bf16[8,64,512]{2,1,0:T(8,128)(2,1)}, f32[8,1,512]{2,1,0:T(1,128)}) custom-call(s32[8]{0:T(128)} %bitcast.62, bf16[8,192,512]{2,1,0:T(8,128)(2,1)} %copy-done.33, s32[8,1,512]{2,1,0:T(1,128)} %bitcast.82), custom_call_target="tpu_custom_call" | custom-call | flops 24999999488 | bytes 25000000 | tf_op jit(solution)/shard_map/attend/pallas_call | solution.py:135
  113.8 25.0 %attend.3 = (bf16[8,64,512]{2,1,0:T(8,128)(2,1)}, f32[8,1,512]{2,1,0:T(1,128)}) custom-call(s32[8]{0:T(128)} %bitcast.63, bf16[8,192,512]{2,1,0:T(8,128)(2,1)} %copy-done.32, s32[8,1,512]{2,1,0:T(1,128)} %bitcast.83), custom_call_target="tpu_custom_call" | custom-call | flops 24999999488 | bytes 25000000 | tf_op jit(solution)/shard_map/attend/pallas_call | solution.py:135
  138.7 5.2 %all-to-all-start.3 = ((bf16[8,64,512]{2,1,0:T(8,128)(2,1)}), bf16[8,64,512]{2,1,0:T(8,128)(2,1)}, u32[]{:S(2)}, u32[]{:S(2)}) async-start(bf16[8,64,512]{2,1,0:T(8,128)(2,1)} %get-tuple-element.104.o_ref), calls=%async_computation.3 | async-start | bytes 1048576 | tf_op jit(solution)/shard_map/all_to_all | solution.py:1417
  145.8 13.6 %all-to-all-done.3.refs_1_ = bf16[8,64,512]{2,1,0:T(8,128)(2,1)} async-done(((bf16[8,64,512]{2,1,0:T(8,128)(2,1)}), bf16[8,64,512]{2,1,0:T(8,128)(2,1)}, u32[]{:S(2)}, u32[]{:S(2)}) %all-to-all-start.3) | async-done | bytes 524320 | tf_op jit(solution)/shard_map/all_to_all | solution.py:1417
  159.4 50.8 %mid_block.1 = (bf16[512,1024]{1,0:T(8,128)(2,1)}, f32[512,1024]{1,0:T(8,128)}, f32[40,1024]{1,0:T(8,128)}, bf16[8,128,512]{2,1,0:T(8,128)(2,1)}, bf16[8,4,144,1...) custom-call(s32[8]{0:T(128)} %bitcast.64, s32[5]{0:T(128)} %copy-done.4, bf16[8,64,512]{2,1,0:T(8,128)(2,1)} %copy-done.37, ...), custom_call_target="tpu_custom_call" | custom-call | flops 49999998976 | bytes 50000000 | tf_op jit(solution)/shard_map/mid_block/pallas_call | solution.py:547
  214.8 10.5 %collective-permute-done.3 = bf16[8,4,144,1024]{3,2,1,0:T(8,128)(2,1)} collective-permute-done((bf16[8,4,144,1024]{3,2,1,0:T(8,128)(2,1)}, bf16[8,4,144,1024]{3,2,1,0:T(8,128)(2,1)}, u32[]{:S(2)}, u32[]{:S(2)}) %collective-permute-start.3) | collective-permute-done | bytes 9437216 | tf_op jit(solution)/shard_map/ppermute | solution.py:1265
  225.3 11.3 %first_sum.2 = (bf16[2,4,64,1024]{3,2,1,0:T(8,128)(2,1)}, bf16[2,4,80,1024]{3,2,1,0:T(8,128)(2,1)S(1)}, bf16[2,4,64,1024]{3,2,1,0:T(8,128)(2,1)}, bf16[2,4,80,10...) custom-call(s32[5]{0:T(128)S(1)} %copy-done.5, ...), custom_call_target="tpu_custom_call" | custom-call | flops 6000000000 | bytes 6000000 | tf_op jit(solution)/shard_map/first_sum/pallas_call | solution.py:1039
  241.4 32.2 %attend_back.2 = bf16[8,192,512]{2,1,0:T(8,128)(2,1)} custom-call(s32[8]{0:T(128)} %bitcast.65, bf16[8,192,512]{2,1,0:T(8,128)(2,1)} %copy-done.33, s32[8,1,512]{2,1,0:T(1,128)} %bitcast.84, bf16[8,64,512]{2,1,0:T(8,128)(2,1)} %get-tuple-element.100.o_ref, bf16[8,128,512]{2,1,0:T(8,128)(2,1)} %all-to-all-done.4.do_ref, f32[8,1,512]{2,1,0:T(1,128)} %get-tuple-element.115.lse_ref), custom_call_target="tpu_custom_call" | custom-call | flops 32000000000 | bytes 32000000 | tf_op jit(solution)/shard_map/attend_back/pallas_call | solution.py:257
  282.1 32.1 %attend_back.3 = bf16[8,192,512]{2,1,0:T(8,128)(2,1)} custom-call(s32[8]{0:T(128)} %bitcast.66, bf16[8,192,512]{2,1,0:T(8,128)(2,1)} %copy-done.32, s32[8,1,512]{2,1,0:T(1,128)} %bitcast.85, bf16[8,64,512]{2,1,0:T(8,128)(2,1)} %get-tuple-element.104.o_ref, bf16[8,128,512]{2,1,0:T(8,128)(2,1)} %all-to-all-done.4.do_ref, f32[8,1,512]{2,1,0:T(1,128)} %get-tuple-element.117.lse_ref), custom_call_target="tpu_custom_call" | custom-call | flops 32000000000 | bytes 32000000 | tf_op jit(solution)/shard_map/attend_back/pallas_call | solution.py:257
  314.2 5.7 %all-to-all-done.6.grad_ref = bf16[8,192,512]{2,1,0:T(8,128)(2,1)} async-done(((bf16[8,192,512]{2,1,0:T(8,128)(2,1)}), bf16[8,192,512]{2,1,0:T(8,128)(2,1)}, u32[]{:S(2)}, u32[]{:S(2)}) %all-to-all-start.6) | async-done | bytes 1572896 | tf_op jit(solution)/shard_map/all_to_all | solution.py:1447
  332.3 9.1 %back_block.2 = (f32[1024,512]{1,0:T(8,128)S(1)}, f32[3,8,512]{2,1,0:T(8,128)S(1)}, bf16[8,4,48,1024]{3,2,1,0:T(8,128)(2,1)}, bf16[8,4,48,1024]{3,2,1,0:T(8,128)(2,1)}) custom-call(s32[8]{0:T(128)S(1)} %bitcast.68, s32[5]{0:T(128)S(1)} %copy-done.5, s32[8]{0:T(128)S(1)} %bitcast.58, bf16[8,192,512]{2,1,0:T(8,128)(2,1)} %all-to-all-done.6.grad_ref, ...), custom_call_target="tpu_custom_call" | custom-call | flops 10000000000 | bytes 10000000 | tf_op jit(solution)/shard_map/back_block/pallas_call | solution.py:832
  342.8 15.7 %collective-permute-done.9.got_b = bf16[4,144,1024]{2,1,0:T(8,128)(2,1)S(1)} collective-permute-done((bf16[4,144,1024]{2,1,0:T(8,128)(2,1)S(1)}, bf16[4,144,1024]{2,1,0:T(8,128)(2,1)S(1)}, u32[]{:S(2)}, u32[]{:S(2)}) %collective-permute-start.9) | collective-permute-done | bytes 1179680 | tf_op jit(solution)/shard_map/ppermute | solution.py:1265
  364.4 10.0 %back_block.3 = (f32[1024,512]{1,0:T(8,128)S(1)}, f32[3,8,512]{2,1,0:T(8,128)S(1)}, bf16[8,4,48,1024]{3,2,1,0:T(8,128)(2,1)}, bf16[8,4,48,1024]{3,2,1,0:T(8,128)(2,1)}) custom-call(s32[8]{0:T(128)S(1)} %bitcast.69, s32[5]{0:T(128)S(1)} %copy-done.6, s32[8]{0:T(128)S(1)} %bitcast.59, ...), custom_call_target="tpu_custom_call", output_to_operand_aliasing={{2}: (7, {}), {3}: (8, {})} | custom-call | flops 10000000000 | bytes 10000000 | tf_op jit(solution)/shard_map/back_block/pallas_call | solution.py:832
  389.6 5.4 %first_sum.3 = (bf16[2,4,80,1024]{3,2,1,0:T(8,128)(2,1)S(1)}, bf16[2,4,80,1024]{3,2,1,0:T(8,128)(2,1)S(1)}, bf16[2,4,80,1024]{3,2,1,0:T(8,128)(2,1)S(1)}, bf16[2,4,80,1024]{3,2,1,0:T(8,128)(2,1)S(1)}) custom-call(s32[5]{0:T(128)S(1)} %copy-done.6, bf16[2,2,2,4,32,1024]{5,4,3,2,1,0:T(8,128)(2,1)} %bitcast.48, ...), custom_call_target="tpu_custom_call" | custom-call | flops 6000000000 | bytes 6000000 | tf_op jit(solution)/shard_map/first_sum/pallas_call | solution.py:1039
  399.5 27.1 %collective-permute-done.13.refs_1_.refs_5_ = bf16[2,4,80,1024]{3,2,1,0:T(8,128)(2,1)S(1)} collective-permute-done((bf16[2,4,80,1024]{3,2,1,0:T(8,128)(2,1)S(1)}, bf16[2,4,80,1024]{3,2,1,0:T(8,128)(2,1)S(1)}, u32[]{:S(2)}, u32[]{:S(2)}) %collective-permute-start.13) | collective-permute-done | bytes 1310752 | tf_op jit(solution)/shard_map/ppermute | solution.py:1265
  435.9 7.7 %all-to-all-done.7.x = bf16[4,2,144,1024]{3,2,1,0:T(8,128)(2,1)} async-done(((bf16[4,2,144,1024]{3,2,1,0:T(8,128)(2,1)}), bf16[4,2,144,1024]{3,2,1,0:T(8,128)(2,1)}, u32[]{:S(2)}, u32[]{:S(2)}) %all-to-all-start.7) | async-done | bytes 2359328 | tf_op jit(solution)/shard_map/all_to_all | solution.py:1297
  450.8 5.3 %collective-permute-done.16 = bf16[64,1024]{1,0:T(8,128)(2,1)S(1)} collective-permute-done((bf16[64,1024]{1,0:T(8,128)(2,1)S(1)}, bf16[64,1024]{1,0:T(8,128)(2,1)S(1)}, u32[]{:S(2)}, u32[]{:S(2)}) %collective-permute-start.16) | collective-permute-done | bytes 131104 | tf_op jit(solution)/shard_map/ppermute | solution.py:1265
  505.3 6.3 %collective-permute-done.30.refs_2_ = bf16[2,80,1024]{2,1,0:T(8,128)(2,1)S(1)} collective-permute-done((bf16[2,80,1024]{2,1,0:T(8,128)(2,1)}, bf16[2,80,1024]{2,1,0:T(8,128)(2,1)S(1)}, u32[]{:S(2)}, u32[]{:S(2)}) %collective-permute-start.30) | collective-permute-done | bytes 327712 | tf_op jit(solution)/shard_map/ppermute | solution.py:1265
  (202 shorter events, 156.8 us)
Async XLA Ops:
  23.9 44.3 %all-to-all-start = ((bf16[8,192,512]{2,1,0:T(8,128)(2,1)}), bf16[8,192,512]{2,1,0:T(8,128)(2,1)S(1)}, u32[]{:S(2)}, u32[]{:S(2)}) async-start(bf16[8,192,512]{2,1,0:T(8,128)(2,1)} %qkv_block.2), calls=%async_computation | async-start | bytes 3145728 | tf_op jit(solution)/shard_map/all_to_all | solution.py:1404
  68.2 41.3 %all-to-all-start.2 = ((bf16[8,192,512]{2,1,0:T(8,128)(2,1)}), bf16[8,192,512]{2,1,0:T(8,128)(2,1)S(1)}, u32[]{:S(2)}, u32[]{:S(2)}) async-start(bf16[8,192,512]{2,1,0:T(8,128)(2,1)} %qkv_block.3), calls=%async_computation.2 | async-start | bytes 3145728 | tf_op jit(solution)/shard_map/all_to_all | solution.py:1404
  110.2 28.5 %all-to-all-start.1 = ((bf16[8,64,512]{2,1,0:T(8,128)(2,1)}), bf16[8,64,512]{2,1,0:T(8,128)(2,1)S(1)}, u32[]{:S(2)}, u32[]{:S(2)}) async-start(bf16[8,64,512]{2,1,0:T(8,128)(2,1)} %get-tuple-element.100.o_ref), calls=%async_computation.1 | async-start | bytes 1048576 | tf_op jit(solution)/shard_map/all_to_all | solution.py:1417
  138.7 20.7 %all-to-all-start.3 = ((bf16[8,64,512]{2,1,0:T(8,128)(2,1)}), bf16[8,64,512]{2,1,0:T(8,128)(2,1)}, u32[]{:S(2)}, u32[]{:S(2)}) async-start(bf16[8,64,512]{2,1,0:T(8,128)(2,1)} %get-tuple-element.104.o_ref), calls=%async_computation.3 | async-start | bytes 1048576 | tf_op jit(solution)/shard_map/all_to_all | solution.py:1417
  210.3 31.1 %all-to-all-start.4 = ((bf16[8,128,512]{2,1,0:T(8,128)(2,1)}), bf16[8,128,512]{2,1,0:T(8,128)(2,1)}, u32[]{:S(2)}, u32[]{:S(2)}) async-start(bf16[8,128,512]{2,1,0:T(8,128)(2,1)} %get-tuple-element.107), calls=%async_computation.4 | async-start | bytes 2097152 | tf_op jit(solution)/shard_map/all_to_all | solution.py:1437
  237.7 40.1 %collective-permute-start.6 = (bf16[2,4,64,1024]{3,2,1,0:T(8,128)(2,1)}, bf16[2,4,64,1024]{3,2,1,0:T(8,128)(2,1)S(1)}, u32[]{:S(2)}, u32[]{:S(2)}) collective-permute-start(bf16[2,4,64,1024]{3,2,1,0:T(8,128)(2,1)} %get-tuple-element.110), channel_id=1, source_target_pairs={{0,8},{8,0},{16,24},{24,16},{1,9},{9,1},{17,25},{25,17},{2,10},{10... | collective-permute-start | bytes 3145736 | tf_op jit(solution)/shard_map/ppermute | solution.py:1265
  240.4 37.4 %collective-permute-start.7 = (bf16[2,4,64,1024]{3,2,1,0:T(8,128)(2,1)}, bf16[2,4,64,1024]{3,2,1,0:T(8,128)(2,1)S(1)}, u32[]{:S(2)}, u32[]{:S(2)}) collective-permute-start(bf16[2,4,64,1024]{3,2,1,0:T(8,128)(2,1)} %get-tuple-element.112), channel_id=1, source_target_pairs={{0,16},{8,24},{16,0},{24,8},{1,17},{9,25},{17,1},{25,9},{2,18},{10... | collective-permute-start | bytes 3145736 | tf_op jit(solution)/shard_map/ppermute | solution.py:1265
  273.6 40.6 %collective-permute-start.5 = (bf16[2,4,80,1024]{3,2,1,0:T(8,128)(2,1)}, bf16[2,4,80,1024]{3,2,1,0:T(8,128)(2,1)}, u32[]{:S(2)}, u32[]{:S(2)}) collective-permute-start(bf16[2,4,80,1024]{3,2,1,0:T(8,128)(2,1)} %copy-done.9), channel_id=1, source_target_pairs={{0,16},{8,24},{16,0},{24,8},{1,17},{9,25},{17,1},{25,9},{2,18},{10... | collective-permute-start | bytes 3932168 | tf_op jit(solution)/shard_map/ppermute | solution.py:1265
  273.6 40.6 %collective-permute-start.4 = (bf16[2,4,80,1024]{3,2,1,0:T(8,128)(2,1)S(1)}, bf16[2,4,80,1024]{3,2,1,0:T(8,128)(2,1)}, u32[]{:S(2)}, u32[]{:S(2)}) collective-permute-start(bf16[2,4,80,1024]{3,2,1,0:T(8,128)(2,1)S(1)} %get-tuple-element.118), channel_id=1, source_target_pairs={{0,8},{8,0},{16,24},{24,16},{1,9},{9,1},{17,25},{25,17},{2,10},{10... | collective-permute-start | bytes 3932168 | tf_op jit(solution)/shard_map/ppermute | solution.py:1265
  277.8 42.1 %all-to-all-start.6 = ((bf16[8,192,512]{2,1,0:T(8,128)(2,1)}), bf16[8,192,512]{2,1,0:T(8,128)(2,1)}, u32[]{:S(2)}, u32[]{:S(2)}) async-start(bf16[8,192,512]{2,1,0:T(8,128)(2,1)} %attend_back.2), calls=%async_computation.6 | async-start | bytes 3145728 | tf_op jit(solution)/shard_map/all_to_all | solution.py:1447
  319.9 44.4 %all-to-all-start.5 = ((bf16[8,192,512]{2,1,0:T(8,128)(2,1)}), bf16[8,192,512]{2,1,0:T(8,128)(2,1)}, u32[]{:S(2)}, u32[]{:S(2)}) async-start(bf16[8,192,512]{2,1,0:T(8,128)(2,1)} %attend_back.3), calls=%async_computation.5 | async-start | bytes 3145728 | tf_op jit(solution)/shard_map/all_to_all | solution.py:1447
  330.3 28.2 %collective-permute-start.9 = (bf16[4,144,1024]{2,1,0:T(8,128)(2,1)S(1)}, bf16[4,144,1024]{2,1,0:T(8,128)(2,1)S(1)}, u32[]{:S(2)}, u32[]{:S(2)}) collective-permute-start(bf16[4,144,1024]{2,1,0:T(8,128)(2,1)S(1)} %get-tuple-element.130), channel_id=1, source_target_pairs={{0,8},{8,0},{16,24},{24,16},{1,9},{9,1},{17,25},{25,17},{2,10},{10... | collective-permute-start | bytes 3538952 | tf_op jit(solution)/shard_map/ppermute | solution.py:1265
  330.3 28.5 %collective-permute-start.8 = (bf16[4,144,1024]{2,1,0:T(8,128)(2,1)S(1)}, bf16[4,144,1024]{2,1,0:T(8,128)(2,1)S(1)}, u32[]{:S(2)}, u32[]{:S(2)}) collective-permute-start(bf16[4,144,1024]{2,1,0:T(8,128)(2,1)S(1)} %get-tuple-element.128), channel_id=1, source_target_pairs={{0,16},{8,24},{16,0},{24,8},{1,17},{9,25},{17,1},{25,9},{2,18},{10... | collective-permute-start | bytes 3538952 | tf_op jit(solution)/shard_map/ppermute | solution.py:1265
  384.5 59.1 %all-to-all-start.7 = ((bf16[4,2,144,1024]{3,2,1,0:T(8,128)(2,1)}), bf16[4,2,144,1024]{3,2,1,0:T(8,128)(2,1)}, u32[]{:S(2)}, u32[]{:S(2)}) async-start(bf16[4,2,144,1024]{3,2,1,0:T(8,128)(2,1)} %third_sum_all.1), calls=%async_computation.7 | async-start | bytes 4718592 | tf_op jit(solution)/shard_map/all_to_all | solution.py:1297
  396.1 30.5 %collective-permute-start.13 = (bf16[2,4,80,1024]{3,2,1,0:T(8,128)(2,1)S(1)}, bf16[2,4,80,1024]{3,2,1,0:T(8,128)(2,1)S(1)}, u32[]{:S(2)}, u32[]{:S(2)}) collective-permute-start(bf16[2,4,80,1024]{3,2,1,0:T(8,128)(2,1)S(1)} %get-tuple-element.153), channel_id=1, source_target_pairs={{0,8},{8,0},{16,24},{24,16},{1,9},{9,1},{17,25},{25,17},{2,10},{10... | collective-permute-start | bytes 3932168 | tf_op jit(solution)/shard_map/ppermute | solution.py:1265
  397.7 30.2 %collective-permute-start.14 = (bf16[2,4,80,1024]{3,2,1,0:T(8,128)(2,1)S(1)}, bf16[2,4,80,1024]{3,2,1,0:T(8,128)(2,1)S(1)}, u32[]{:S(2)}, u32[]{:S(2)}) collective-permute-start(bf16[2,4,80,1024]{3,2,1,0:T(8,128)(2,1)S(1)} %get-tuple-element.155), channel_id=1, source_target_pairs={{0,16},{8,24},{16,0},{24,8},{1,17},{9,25},{17,1},{25,9},{2,18},{10... | collective-permute-start | bytes 3932168 | tf_op jit(solution)/shard_map/ppermute | solution.py:1265
  399.5 36.4 %collective-permute-start.10 = (f32[64,1024]{1,0:T(8,128)S(1)}, f32[64,1024]{1,0:T(8,128)S(1)}, u32[]{:S(2)}, u32[]{:S(2)}) collective-permute-start(f32[64,1024]{1,0:T(8,128)S(1)} %get-tuple-element.146), channel_id=1, source_target_pairs={{0,1},{1,0},{2,3},{3,2},{4,5},{5,4},{6,7},{7,6},{8,9},{9,8},{10,11... | collective-permute-start | bytes 786440 | tf_op jit(solution)/shard_map/ppermute | solution.py:1265
  433.5 22.8 %collective-permute-start.18 = (bf16[4,80,1024]{2,1,0:T(8,128)(2,1)S(1)}, bf16[4,80,1024]{2,1,0:T(8,128)(2,1)}, u32[]{:S(2)}, u32[]{:S(2)}) collective-permute-start(bf16[4,80,1024]{2,1,0:T(8,128)(2,1)S(1)} %get-tuple-element.156), channel_id=1, source_target_pairs={{0,16},{8,24},{16,0},{24,8},{1,17},{9,25},{17,1},{25,9},{2,18},{10... | collective-permute-start | bytes 1966088 | tf_op jit(solution)/shard_map/ppermute | solution.py:1265
  435.2 21.0 %collective-permute-start.19 = (bf16[4,80,1024]{2,1,0:T(8,128)(2,1)S(1)}, bf16[4,80,1024]{2,1,0:T(8,128)(2,1)}, u32[]{:S(2)}, u32[]{:S(2)}) collective-permute-start(bf16[4,80,1024]{2,1,0:T(8,128)(2,1)S(1)} %get-tuple-element.157), channel_id=1, source_target_pairs={{0,8},{8,0},{16,24},{24,16},{1,9},{9,1},{17,25},{25,17},{2,10},{10... | collective-permute-start | bytes 1966088 | tf_op jit(solution)/shard_map/ppermute | solution.py:1265
  464.4 22.6 %collective-permute-start.28 = (bf16[2,80,1024]{2,1,0:T(8,128)(2,1)}, bf16[2,80,1024]{2,1,0:T(8,128)(2,1)}, u32[]{:S(2)}, u32[]{:S(2)}) collective-permute-start(bf16[2,80,1024]{2,1,0:T(8,128)(2,1)} %get-tuple-element.163), channel_id=1, source_target_pairs={{0,6},{1,7},{2,4},{3,5},{4,2},{5,3},{6,0},{7,1},{8,14},{9,15},{10,... | collective-permute-start | bytes 983048 | tf_op jit(solution)/shard_map/ppermute | solution.py:1265
  465.8 26.6 %collective-permute-start.27 = (bf16[2,80,1024]{2,1,0:T(8,128)(2,1)}, bf16[2,80,1024]{2,1,0:T(8,128)(2,1)}, u32[]{:S(2)}, u32[]{:S(2)}) collective-permute-start(bf16[2,80,1024]{2,1,0:T(8,128)(2,1)} %get-tuple-element.162), channel_id=1, source_target_pairs={{0,4},{1,5},{2,6},{3,7},{4,0},{5,1},{6,2},{7,3},{8,12},{9,13},{10,... | collective-permute-start | bytes 983048 | tf_op jit(solution)/shard_map/ppermute | solution.py:1265
  467.8 24.6 %collective-permute-start.26 = (bf16[2,80,1024]{2,1,0:T(8,128)(2,1)}, bf16[2,80,1024]{2,1,0:T(8,128)(2,1)}, u32[]{:S(2)}, u32[]{:S(2)}) collective-permute-start(bf16[2,80,1024]{2,1,0:T(8,128)(2,1)} %get-tuple-element.161), channel_id=1, source_target_pairs={{0,2},{1,3},{2,0},{3,1},{4,6},{5,7},{6,4},{7,5},{8,10},{9,11},{10,... | collective-permute-start | bytes 983048 | tf_op jit(solution)/shard_map/ppermute | solution.py:1265
  469.5 28.1 %collective-permute-start.23 = (bf16[2,144,1024]{2,1,0:T(8,128)(2,1)S(1)}, bf16[2,144,1024]{2,1,0:T(8,128)(2,1)S(1)}, u32[]{:S(2)}, u32[]{:S(2)}) collective-permute-start(bf16[2,144,1024]{2,1,0:T(8,128)(2,1)S(1)} %copy-done.14), channel_id=1, source_target_pairs={{0,8},{8,0},{16,24},{24,16},{1,9},{9,1},{17,25},{25,17},{2,10},{10... | collective-permute-start | bytes 1769480 | tf_op jit(solution)/shard_map/ppermute | solution.py:1265
  471.9 29.2 %collective-permute-start.24 = (bf16[2,144,1024]{2,1,0:T(8,128)(2,1)S(1)}, bf16[2,144,1024]{2,1,0:T(8,128)(2,1)S(1)}, u32[]{:S(2)}, u32[]{:S(2)}) collective-permute-start(bf16[2,144,1024]{2,1,0:T(8,128)(2,1)S(1)} %copy-done.14), channel_id=1, source_target_pairs={{0,16},{8,24},{16,0},{24,8},{1,17},{9,25},{17,1},{25,9},{2,18},{10... | collective-permute-start | bytes 1769480 | tf_op jit(solution)/shard_map/ppermute | solution.py:1265
  (61 other events, 507.2 us)

commit v6 on v5

--- a/solution.py
+++ b/solution.py
@@ -1051,19 +1051,22 @@
     )(ids, *([a for pair in pairs for a in pair] * 4))
 
 
-def second_kernel(pieces, ids_ref, *refs):
+def second_kernel(keeps, pieces, ids_ref, *refs):
     for i in range(4):
-        keep, *got = refs[(pieces + 1) * i : (pieces + 1) * (i + 1)]
-        out = refs[4 * (pieces + 1) + i]
+        own = refs[(keeps + pieces) * i : (keeps + pieces) * (i + 1)]
+        out = refs[4 * (keeps + pieces) + i]
         at = 0
-        for g in got:
-            rows = g.shape[2]
-            out[:, at : at + rows, :] = add_bf16(keep[0, :, at : at + rows, :], g[0])
+        for p in range(pieces):
+            got = own[keeps + p]
+            rows = got.shape[2]
+            left = own[p][0] if keeps > 1 else own[0][0, :, at : at + rows, :]
+            out[:, at : at + rows, :] = add_bf16(left, got[0])
             at += rows
 
 
 def second_sum(ids, keep_a, got_a, keep_b, got_b):
-    _, z_ways, rows, width = keep_a.shape
+    _, z_ways, _, width = keep_a[0].shape
+    rows = sum(g.shape[2] for g in got_a)
     step = z_ways // 2 if rows > 100 else z_ways
 
     def source(axis, mine, value):
@@ -1074,10 +1077,10 @@
         return pl.BlockSpec((1, step, *value.shape[2:]), at)
 
     order = [(3, False), (2, False), (3, True), (2, True)]
-    sides = [[keep_a, *got_a], [keep_b, *got_b]]
+    sides = [[*keep_a, *got_a], [*keep_b, *got_b]]
     out = jax.ShapeDtypeStruct((z_ways, rows, width), jnp.bfloat16)
     return pl.pallas_call(
-        functools.partial(second_kernel, len(got_a)),
+        functools.partial(second_kernel, len(keep_a), len(got_a)),
         out_shape=[out] * 4,
         grid_spec=pltpu.PrefetchScalarGridSpec(
             num_scalar_prefetch=1,
@@ -1116,14 +1119,15 @@
 
 
 def third_all_kernel(ids_ref, keep_a, got_a, keep_b, got_b, out):
+    rows = keep_a.shape[1]
     for z in range(keep_a.shape[0]):
-        out[z, 0] = add_bf16(keep_a[z], got_a[z])
-        out[z, 1] = add_bf16(keep_b[z], got_b[z])
-
-
-def third_sum_all(ids, keep_a, got_a, keep_b, got_b):
+        out[z, 0, :rows, :] = add_bf16(keep_a[z], got_a[z])
+        out[z, 1, :rows, :] = add_bf16(keep_b[z], got_b[z])
+
+
+def third_sum_all(ids, keep_a, got_a, keep_b, got_b, room):
     z_ways, rows, width = keep_a.shape
-    out = jax.ShapeDtypeStruct((z_ways, 2, rows, width), jnp.bfloat16)
+    out = jax.ShapeDtypeStruct((z_ways, 2, rows + room, width), jnp.bfloat16)
     step = max(1, z_ways // 2)
     return pl.pallas_call(
         third_all_kernel,
@@ -1132,27 +1136,69 @@
             num_scalar_prefetch=1,
             grid=(z_ways // step,),
             in_specs=[pl.BlockSpec((step, rows, width), lambda i, *_: (i, 0, 0))] * 4,
-            out_specs=pl.BlockSpec((step, 2, rows, width), lambda i, *_: (i, 0, 0, 0)),
+            out_specs=pl.BlockSpec((step, 2, rows + room, width), lambda i, *_: (i, 0, 0, 0)),
         ),
         cost_estimate=cost(10),
         name="third_sum_all",
     )(ids, keep_a, got_a, keep_b, got_b)
 
 
-def fourth_all_kernel(x, out):
+def put_kernel(small_ref, big_ref, out_ref, held, sems):
+    room = held.shape[1]
+    z_ways, rows = out_ref.shape[0], out_ref.shape[2] - room
+    for half in range(2):
+        held[half] = small_ref[half * room : (half + 1) * room, :].astype(jnp.bfloat16)
+    copies = [
+        pltpu.make_async_copy(held, out_ref.at[z, :, pl.ds(rows, room), :], sems.at[z]) for z in range(z_ways)
+    ]
+    for copy in copies:
+        copy.start()
+    for copy in copies:
+        copy.wait()
+
+
+def put_rows(big, small):
+    room = small.shape[0] // 2
+    hbm = pl.BlockSpec(memory_space=pl.ANY)
+    return pl.pallas_call(
+        put_kernel,
+        out_shape=jax.ShapeDtypeStruct(big.shape, big.dtype),
+        grid=(1,),
+        in_specs=[whole_block(small.shape), hbm],
+        out_specs=hbm,
+        scratch_shapes=[
+            pltpu.VMEM((2, room, big.shape[3]), jnp.bfloat16),
+            pltpu.SemaphoreType.DMA((big.shape[0],)),
+        ],
+        input_output_aliases={1: 0},
+        cost_estimate=cost(10),
+        name="put_rows",
+    )(small, big)
+
+
+def fourth_all_kernel(x, out, small):
+    rows = out.shape[1]
+    room = small.shape[0] // 2
     total = x[0].astype(jnp.float32)
     for z in range(1, x.shape[0]):
         total = total + x[z].astype(jnp.float32)
-    out[...] = total.astype(jnp.bfloat16)
-
-
-def fourth_sum_all(terms):
+    out[...] = total[:, :rows].astype(jnp.bfloat16)
+    for half in range(2):
+        small[half * room : (half + 1) * room, :] = total[half, rows:]
+
+
+def fourth_sum_all(terms, room):
+    _, _, rows, width = terms.shape
+    outs = [
+        jax.ShapeDtypeStruct((2, rows - room, width), jnp.bfloat16),
+        jax.ShapeDtypeStruct((2 * room, width), jnp.float32),
+    ]
     return pl.pallas_call(
         fourth_all_kernel,
-        out_shape=jax.ShapeDtypeStruct(terms.shape[1:], jnp.bfloat16),
+        out_shape=outs,
         grid=(1,),
         in_specs=[whole_block(terms.shape)],
-        out_specs=whole_block(terms.shape[1:]),
+        out_specs=[whole_block(o.shape) for o in outs],
         cost_estimate=cost(10),
         name="fourth_sum_all",
     )(terms)
@@ -1269,34 +1315,41 @@
     return [1 << i for i in range(ways.bit_length() - 1)]
 
 
-def reduce_stages(ids, blocks, splits, whole_z):
+def reduce_stages(ids, blocks, splits, room=0):
     batch_ways = lax.axis_size("batch")
     x_bit, y_bit = 1, 1 << ((batch_ways.bit_length() - 1) // 2)
-    pairs = []
-    for keep, send in blocks:
+    side_a, side_b, keeps_a, keeps_b = [], [], [], []
+    for block, split in zip(blocks, splits):
+        keep, send = block(side_a + side_b) if callable(block) else block
         shape = (2, 2, 2) + keep.shape[1:]
-        pairs.append((keep.reshape(shape), sum_exchange(send, "seq", 1).reshape(shape)))
-    *sends, keep_a, keep_b = first_sum(ids, pairs, splits)
-    sends = follow(sends, (yield sends))
+        pair = (keep.reshape(shape), sum_exchange(send, "seq", 1).reshape(shape))
+        *sends, keep_a, keep_b = first_sum(ids, [pair], split)
+        side_a += sends[: len(split)]
+        side_b += sends[len(split) :]
+        keeps_a.append(keep_a)
+        keeps_b.append(keep_b)
+    pieces = len(side_a)
+    sends = follow(side_a + side_b, (yield side_a + side_b))
     got, token = [[], []], None
-    for i in range(len(splits)):
-        pieces = follow([sends[i], sends[len(splits) + i]], token)
+    for i in range(pieces):
+        moved = follow([sends[i], sends[pieces + i]], token)
         for side, bit in enumerate((x_bit, y_bit)):
-            got[side].append(sum_exchange(pieces[side], "batch", bit))
+            got[side].append(sum_exchange(moved[side], "batch", bit))
         token = yield [got[0][i], got[1][i]]
     got_a, got_b = (follow(g, token) for g in got)
-    send_a, send_b, keep_a, keep_b = second_sum(ids, keep_a, got_a, keep_b, got_b)
+    send_a, send_b, keep_a, keep_b = second_sum(ids, keeps_a, got_a, keeps_b, got_b)
     send_a, send_b = follow([send_a, send_b], (yield [send_a, send_b]))
     got = [sum_exchange(send_a, "batch", y_bit), sum_exchange(send_b, "batch", x_bit)]
     got_a, got_b = follow(got, (yield got))
-    if whole_z:
+    extra = []
+    if room:
         ways = lax.axis_size("seq")
         groups = [list(range(c, ways, 2)) for c in range(2)]
-        away = [third_sum_all(ids, keep_a, got_a, keep_b, got_b)]
-        away = follow(away, (yield away))
-        got = [lax.all_to_all(away[0], "seq", 0, 0, axis_index_groups=groups, tiled=True)]
+        away = third_sum_all(ids, keep_a, got_a, keep_b, got_b, room)
+        away = put_rows(away, (yield [away]))
+        got = [lax.all_to_all(away, "seq", 0, 0, axis_index_groups=groups, tiled=True)]
         got = follow(got, (yield got))
-        block = fourth_sum_all(got[0])
+        block, *extra = fourth_sum_all(got[0], room)
     else:
         own, *away = third_sum(ids, keep_a, got_a, keep_b, got_b)
         away = follow(away, (yield away))
@@ -1306,7 +1359,7 @@
     for bit in axis_bits(batch_ways):
         if bit not in (x_bit, y_bit):
             block = add_bf16(block, sum_exchange(block, "batch", bit))
-    (block,) = follow([block], (yield [block]))
+    (block,) = follow([block], (yield [block, *extra]))
     yield [block] + [sum_exchange(block, "batch", bit) for bit in (x_bit, y_bit, x_bit | y_bit)]
 
 
@@ -1336,13 +1389,6 @@
     away = value.astype(jnp.bfloat16)
     others = [sum_exchange(away, "batch", i) for i in range(1, lax.axis_size("batch"))]
     return [value] + [other.astype(value.dtype) for other in others]
-
-
-def sum_z(value, tokens):
-    away = after(value.astype(jnp.bfloat16), *tokens)
-    for j in range(1, lax.axis_size("seq") // 2):
-        value = value + sum_exchange(away, "seq", 2 * j).astype(jnp.float32)
-    return value
 
 
 def shards(
@@ -1436,7 +1482,7 @@
     output, after_grad, mid_small, grad_att, keep, send = mid
     grad_heads = exchange(grad_att)
     front = keep.shape[2] * 4 // 9 // 16 * 16
-    feed = reduce_stages(ids, [(keep, send)], [front, keep.shape[2] - front], True)
+    feed = reduce_stages(ids, [(keep, send)], [[front, keep.shape[2] - front]], 3 * pad_u + 8)
 
     ahead = next(feed)
     grad_local = []
@@ -1459,20 +1505,18 @@
         ahead = next(feed) and advance(feed, 1, acc) if c == 0 else []
     gh, small = norm_block(lengths_row, ids, acc, hidden, after_grad, mods_a, loss_mask, mid_small, biases)
     small = small + sum_exchange(small, "seq", 1)
-    skip_keep, skip_send = skip_block(ids, joinedT, gh, seq_ways, PARTS)
-    blocks = [(skip_keep, skip_send), (keep, send)]
-    rest = reduce_stages(ids, blocks, [5 * own // PARTS], False)
-    moving = next(feed)
-    small = sum_z(small, moving + advance(rest, 3))
-    next(rest)
-    moving = next(rest)
-    groups = gather_groups(after(small, *moving, *next(feed)))
+    blocks = [(keep, send), lambda sends: skip_block(ids, joinedT, after(gh, *sends), seq_ways, PARTS)]
+    rest = reduce_stages(ids, blocks, [[3 * own // PARTS], [2 * own // PARTS]])
+    feed.send(small)
+    third = advance(rest, 6)
+    brought = next(rest)
+    _, small = feed.send(third[0])
+    feed = last_stage(feed, third[0])
+    groups = gather_groups(after(small, *brought, *feed[1:]))
     numerator = float(group_frames * batch_ways)
     grad_w_ada, vectors, scale = ada_block(time3, groups, utts, numerator)
     grad_tokens, grad_skip = joined_block(gh, w_skip, scale)
-    feed = last_stage(feed, groups[-1])
     next(rest)
-    rest.send(grad_tokens)
     rest = last_stage(rest)
 
     ff = w_up.shape[1]
@@ -1502,10 +1546,10 @@
         ids,
         after(scale, grad_w_down),
         [rest],
-        [(0, 0, skip_part, 0, width, 0, lambda k: span(k * skip_part, skip_part), whole_lanes)]
+        [(0, 3 * out_part, skip_part, 0, width, 0, lambda k: span(k * skip_part, skip_part), whole_lanes)]
         + [
             (
-                *(0, skip_part + p * out_part, out_part, 0, width, 1),
+                *(0, p * out_part, out_part, 0, width, 1),
                 lambda k: span(k * out_part, out_part),
                 lambda k, at=p * width: span(at, width),
             )

time: 523 us -> 537 us (1.027)
  waiting for transfers between devices: 137 us -> 143 us
    ppermute x32 -> x31, waiting for transfers between devices: 78.5 us -> 92.9 us  [sum_exchange(): return lax.ppermute(value, axis, [(i, i ^ bit) for i in range(ways)])]
    all_to_all x1, waiting for transfers between devices: 7.72 us -> 0.01 us  [reduce_stages(): lax.all_to_all(away, 'seq', 0, 0, axis_index_groups=groups, tiled=True)]
    ppermute x32 -> x31, starting transfers between devices: 38.7 us -> 35.4 us  [sum_exchange(): return lax.ppermute(value, axis, [(i, i ^ bit) for i in range(ways)])]
    pallas_call x3 -> x4, Pallas kernels: 10.6 us -> 12.5 us  [the longest x2 7.69 us: second_sum(): pl.pallas_call(functools.partial(second_kernel, len(keep_a), len(got_a)),...]
    unnamed x92 -> x108, local copies, waits for them, and re-layouts: 14.6 us -> 16.5 us
    pallas_call x2 -> x3, Pallas kernels: 16.8 us -> 17.5 us  [first_sum(): pl.pallas_call(functools.partial(first_kernel, len(pairs), len(splits)),...]
  transfers between devices with their start and end apart: 40 -> 39, of which waited for: 19 -> 18; matrix products, arithmetic and copies ran while one was open for 3% -> 3% of each run, Pallas kernels for 36% -> 36%
where the time goes in v6:
time: 537 us; the launch traced here: 527 us
  Pallas kernels  269 us (50%)
  waiting for transfers between devices  143 us (27%)
  starting transfers between devices  72.4 us (13%)
  local copies, waits for them, and re-layouts  27.1 us (5%)
  matrix products  8.29 us (2%)
    ppermute x31, waiting for transfers between devices, sum_exchange(): return lax.ppermute(value, axis, [(i, i ^ bit) for i in range(ways)])  92.9 us
    pallas_call x2, Pallas kernels, attend_back(): pl.pallas_call(functools.partial(bwd_kernel, utts, chunk), out_shape=jax....  64.2 us
    pallas_call x1, Pallas kernels, mid_block(): pl.pallas_call(functools.partial(mid_kernel, (seq_ways, heads_local, utts...  50.9 us
    pallas_call x2, Pallas kernels, attend(): pl.pallas_call(functools.partial(fwd_kernel, utts), out_shape=(jax.ShapeD...  49.8 us
    ppermute x31, starting transfers between devices, sum_exchange(): return lax.ppermute(value, axis, [(i, i ^ bit) for i in range(ways)])  35.4 us
    all_to_all x2, waiting for transfers between devices, shards(): received.append(exchange(packed))  31 us
    pallas_call x2, Pallas kernels, back_block(): pl.pallas_call(functools.partial(back_kernel, utts, seq_ways, chunk), out...  19.1 us
    pallas_call x3, Pallas kernels, first_sum(): pl.pallas_call(functools.partial(first_kernel, len(pairs), len(splits)),...  17.5 us
  transfers between devices with their start and end apart: 39, of which 18 were waited for; matrix products, arithmetic and copies ran while one was open for 3% of the time, Pallas kernels for 36%

profile of v6, /device:TPU:0, one launch (start us, length us, event | category | flops | bytes accessed | tf_op | source)
XLA Modules:
  0.0 526.7 jit_solution(336223140296524837)
XLA Ops:
  7.3 8.0 %head_block.1 = (f32[512,1024]{1,0:T(8,128)}, bf16[2048,512]{1,0:T(8,128)(2,1)}, bf16[1024,512]{1,0:T(8,128)(2,1)S(1)}, bf16[512,1024]{1,0:T(8,128)(2,1)S(1)}) custom-call(s32[8]{0:T(128)S(1)} %bitcast.63, s32[5]{0:T(128)S(1)} %stack.23.ids_ref, s32[8]{0:T(128)S(1)} %bitcast.53, bf16[512,1024]{1,0:T(8,128)(2,1)S(1)} %bitcast.48, ...), custom_call_target="tpu_custom_call" | custom-call | flops 10000000000 | bytes 10000000 | tf_op jit(solution)/shard_map/head_block/pallas_call | solution.py:676
  17.2 6.8 %qkv_block.2 = bf16[8,192,512]{2,1,0:T(8,128)(2,1)} custom-call(s32[8]{0:T(128)} %bitcast.56, s32[5]{0:T(128)} %copy-done.3, s32[8]{0:T(128)} %bitcast.51, bf16[512,1024]{1,0:T(8,128)(2,1)} %copy-done.27, bf16[1024,3072]{1,0:T(8,128)(2,1)} %w_ref.8, bf16[1,3072]{1,0:T(2,128)(2,1)} %broadcast_in_dim.28.b_ref), custom_call_target="tpu_custom_call" | custom-call | flops 7500000256 | bytes 7500000 | tf_op jit(solution)/shard_map/qkv_block/pallas_call | solution.py:729
  24.0 6.5 %all-to-all-start = ((bf16[8,192,512]{2,1,0:T(8,128)(2,1)}), bf16[8,192,512]{2,1,0:T(8,128)(2,1)S(1)}, u32[]{:S(2)}, u32[]{:S(2)}) async-start(bf16[8,192,512]{2,1,0:T(8,128)(2,1)} %qkv_block.2), calls=%async_computation | async-start | bytes 3145728 | tf_op jit(solution)/shard_map/all_to_all | solution.py:1450
  30.4 5.3 %fusion.2.refs_3_ = f32[16,4096]{1,0:T(8,128)} fusion(bf16[1024,6144]{1,0:T(8,128)(2,1)} %param.32, f32[4096]{0:T(1024)S(1)} %slice_convert_fusion, bf16[8,1024]{1,0:T(8,128)(2,1)S(1)} %fusion.15), kind=kOutput, calls=%fused_computation.2 | convolution fusion | flops 134283264 | bytes 8683520 | tf_op jit(solution)/shard_map/dot_general | solution.py:1436
  35.7 6.8 %qkv_block.3 = bf16[8,192,512]{2,1,0:T(8,128)(2,1)} custom-call(s32[8]{0:T(128)} %bitcast.57, s32[5]{0:T(128)} %copy-done.3, s32[8]{0:T(128)} %bitcast.52, bf16[512,1024]{1,0:T(8,128)(2,1)} %copy-done.27, bf16[1024,3072]{1,0:T(8,128)(2,1)} %w_ref.8, bf16[1,3072]{1,0:T(2,128)(2,1)} %broadcast_in_dim.28.b_ref), custom_call_target="tpu_custom_call" | custom-call | flops 7500000256 | bytes 7500000 | tf_op jit(solution)/shard_map/qkv_block/pallas_call | solution.py:729
  42.5 25.8 %all-to-all-done.qkv_ref = bf16[8,192,512]{2,1,0:T(8,128)(2,1)S(1)} async-done(((bf16[8,192,512]{2,1,0:T(8,128)(2,1)}), bf16[8,192,512]{2,1,0:T(8,128)(2,1)S(1)}, u32[]{:S(2)}, u32[]{:S(2)}) %all-to-all-start) | async-done | bytes 1572896 | tf_op jit(solution)/shard_map/all_to_all | solution.py:1450
  79.6 24.8 %attend.2 = (bf16[8,64,512]{2,1,0:T(8,128)(2,1)}, f32[8,1,512]{2,1,0:T(1,128)}) custom-call(s32[8]{0:T(128)} %bitcast.58, bf16[8,192,512]{2,1,0:T(8,128)(2,1)} %copy-done.34, s32[8,1,512]{2,1,0:T(1,128)} %bitcast.86), custom_call_target="tpu_custom_call" | custom-call | flops 24999999488 | bytes 25000000 | tf_op jit(solution)/shard_map/attend/pallas_call | solution.py:135
  104.4 5.2 all-to-all-done.2.qkv_ref
  113.8 25.0 %attend.3 = (bf16[8,64,512]{2,1,0:T(8,128)(2,1)}, f32[8,1,512]{2,1,0:T(1,128)}) custom-call(s32[8]{0:T(128)} %bitcast.59, bf16[8,192,512]{2,1,0:T(8,128)(2,1)} %copy-done.33, s32[8,1,512]{2,1,0:T(1,128)} %bitcast.87), custom_call_target="tpu_custom_call" | custom-call | flops 24999999488 | bytes 25000000 | tf_op jit(solution)/shard_map/attend/pallas_call | solution.py:135
  138.8 5.2 all-to-all-start.3
  145.8 13.6 %all-to-all-done.3.refs_1_ = bf16[8,64,512]{2,1,0:T(8,128)(2,1)} async-done(((bf16[8,64,512]{2,1,0:T(8,128)(2,1)}), bf16[8,64,512]{2,1,0:T(8,128)(2,1)}, u32[]{:S(2)}, u32[]{:S(2)}) %all-to-all-start.3) | async-done | bytes 524320 | tf_op jit(solution)/shard_map/all_to_all | solution.py:1463
  159.4 50.9 %mid_block.1 = (bf16[512,1024]{1,0:T(8,128)(2,1)}, f32[512,1024]{1,0:T(8,128)}, f32[40,1024]{1,0:T(8,128)}, bf16[8,128,512]{2,1,0:T(8,128)(2,1)}, bf16[8,4,144,1...) custom-call(s32[8]{0:T(128)} %bitcast.60, s32[5]{0:T(128)} %copy-done.3, bf16[8,64,512]{2,1,0:T(8,128)(2,1)} %copy-done.37, ...), custom_call_target="tpu_custom_call" | custom-call | flops 49999998976 | bytes 50000000 | tf_op jit(solution)/shard_map/mid_block/pallas_call | solution.py:547
  214.9 10.5 %collective-permute-done.3 = bf16[8,4,144,1024]{3,2,1,0:T(8,128)(2,1)} collective-permute-done((bf16[8,4,144,1024]{3,2,1,0:T(8,128)(2,1)}, bf16[8,4,144,1024]{3,2,1,0:T(8,128)(2,1)}, u32[]{:S(2)}, u32[]{:S(2)}) %collective-permute-start.3) | collective-permute-done | bytes 9437216 | tf_op jit(solution)/shard_map/ppermute | solution.py:1311
  225.4 11.3 %first_sum.3 = (bf16[2,4,64,1024]{3,2,1,0:T(8,128)(2,1)}, bf16[2,4,80,1024]{3,2,1,0:T(8,128)(2,1)S(1)}, bf16[2,4,64,1024]{3,2,1,0:T(8,128)(2,1)}, bf16[2,4,80,10...) custom-call(s32[5]{0:T(128)S(1)} %copy-done.4, ...), custom_call_target="tpu_custom_call" | custom-call | flops 6000000000 | bytes 6000000 | tf_op jit(solution)/shard_map/first_sum/pallas_call | solution.py:1039
  242.0 32.2 %attend_back.2 = bf16[8,192,512]{2,1,0:T(8,128)(2,1)} custom-call(s32[8]{0:T(128)} %bitcast.61, bf16[8,192,512]{2,1,0:T(8,128)(2,1)} %copy-done.34, s32[8,1,512]{2,1,0:T(1,128)} %bitcast.88, bf16[8,64,512]{2,1,0:T(8,128)(2,1)} %get-tuple-element.104.o_ref, bf16[8,128,512]{2,1,0:T(8,128)(2,1)} %all-to-all-done.4.do_ref, f32[8,1,512]{2,1,0:T(1,128)} %get-tuple-element.119.lse_ref), custom_call_target="tpu_custom_call" | custom-call | flops 32000000000 | bytes 32000000 | tf_op jit(solution)/shard_map/attend_back/pallas_call | solution.py:257
  283.7 32.1 %attend_back.3 = bf16[8,192,512]{2,1,0:T(8,128)(2,1)} custom-call(s32[8]{0:T(128)} %bitcast.62, bf16[8,192,512]{2,1,0:T(8,128)(2,1)} %copy-done.33, s32[8,1,512]{2,1,0:T(1,128)} %bitcast.89, bf16[8,64,512]{2,1,0:T(8,128)(2,1)} %get-tuple-element.108.o_ref, bf16[8,128,512]{2,1,0:T(8,128)(2,1)} %all-to-all-done.4.do_ref, f32[8,1,512]{2,1,0:T(1,128)} %get-tuple-element.121.lse_ref), custom_call_target="tpu_custom_call" | custom-call | flops 32000000000 | bytes 32000000 | tf_op jit(solution)/shard_map/attend_back/pallas_call | solution.py:257
  315.8 5.7 %all-to-all-done.6.grad_ref = bf16[8,192,512]{2,1,0:T(8,128)(2,1)} async-done(((bf16[8,192,512]{2,1,0:T(8,128)(2,1)}), bf16[8,192,512]{2,1,0:T(8,128)(2,1)}, u32[]{:S(2)}, u32[]{:S(2)}) %all-to-all-start.6) | async-done | bytes 1572896 | tf_op jit(solution)/shard_map/all_to_all | solution.py:1493
  331.9 9.1 %back_block.2 = (f32[1024,512]{1,0:T(8,128)S(1)}, f32[3,8,512]{2,1,0:T(8,128)S(1)}, bf16[8,4,48,1024]{3,2,1,0:T(8,128)(2,1)}, bf16[8,4,48,1024]{3,2,1,0:T(8,128)(2,1)}) custom-call(s32[8]{0:T(128)S(1)} %bitcast.64, s32[5]{0:T(128)S(1)} %copy-done.4, s32[8]{0:T(128)S(1)} %bitcast.54, bf16[8,192,512]{2,1,0:T(8,128)(2,1)} %all-to-all-done.6.grad_ref, ...), custom_call_target="tpu_custom_call" | custom-call | flops 10000000000 | bytes 10000000 | tf_op jit(solution)/shard_map/back_block/pallas_call | solution.py:832
  342.3 17.8 %collective-permute-done.9.got_b = bf16[4,144,1024]{2,1,0:T(8,128)(2,1)S(1)} collective-permute-done((bf16[4,144,1024]{2,1,0:T(8,128)(2,1)S(1)}, bf16[4,144,1024]{2,1,0:T(8,128)(2,1)S(1)}, u32[]{:S(2)}, u32[]{:S(2)}) %collective-permute-start.9) | collective-permute-done | bytes 1179680 | tf_op jit(solution)/shard_map/ppermute | solution.py:1311
  366.1 10.0 %back_block.3 = (f32[1024,512]{1,0:T(8,128)S(1)}, f32[3,8,512]{2,1,0:T(8,128)S(1)}, bf16[8,4,48,1024]{3,2,1,0:T(8,128)(2,1)}, bf16[8,4,48,1024]{3,2,1,0:T(8,128)(2,1)}) custom-call(s32[8]{0:T(128)S(1)} %bitcast.65, s32[5]{0:T(128)S(1)} %copy-done.5, s32[8]{0:T(128)S(1)} %bitcast.55, ...), custom_call_target="tpu_custom_call", output_to_operand_aliasing={{2}: (7, {}), {3}: (8, {})} | custom-call | flops 10000000000 | bytes 10000000 | tf_op jit(solution)/shard_map/back_block/pallas_call | solution.py:832
  407.2 11.0 %collective-permute-done.13.refs_2_.refs_10_ = bf16[2,4,48,1024]{3,2,1,0:T(8,128)(2,1)S(1)} collective-permute-done((bf16[2,4,48,1024]{3,2,1,0:T(8,128)(2,1)S(1)}, bf16[2,4,48,1024]{3,2,1,0:T(8,128)(2,1)S(1)}, u32[]{:S(2)}, u32[]{:S(2)}) %collective-permute-start.13) | collective-permute-done | bytes 786464 | tf_op jit(solution)/shard_map/ppermute | solution.py:1311
  419.6 9.2 %collective-permute-done.14.refs_3_.refs_11_ = bf16[2,4,32,1024]{3,2,1,0:T(8,128)(2,1)S(1)} collective-permute-done((bf16[2,4,32,1024]{3,2,1,0:T(8,128)(2,1)S(1)}, bf16[2,4,32,1024]{3,2,1,0:T(8,128)(2,1)S(1)}, u32[]{:S(2)}, u32[]{:S(2)}) %collective-permute-start.14) | collective-permute-done | bytes 524320 | tf_op jit(solution)/shard_map/ppermute | solution.py:1311
  435.3 15.0 %collective-permute-done.17.got_a = bf16[4,80,1024]{2,1,0:T(8,128)(2,1)S(1)} collective-permute-done((bf16[4,80,1024]{2,1,0:T(8,128)(2,1)S(1)}, bf16[4,80,1024]{2,1,0:T(8,128)(2,1)S(1)}, u32[]{:S(2)}, u32[]{:S(2)}) %collective-permute-start.17) | collective-permute-done | bytes 655392 | tf_op jit(solution)/shard_map/ppermute | solution.py:1311
  468.2 19.0 %collective-permute-done.20.refs_2_ = bf16[2,80,1024]{2,1,0:T(8,128)(2,1)S(1)} collective-permute-done((bf16[2,80,1024]{2,1,0:T(8,128)(2,1)S(1)}, bf16[2,80,1024]{2,1,0:T(8,128)(2,1)S(1)}, u32[]{:S(2)}, u32[]{:S(2)}) %collective-permute-start.20) | collective-permute-done | bytes 327712 | tf_op jit(solution)/shard_map/ppermute | solution.py:1311
  (217 shorter events, 158.5 us)
Async XLA Ops:
  24.0 44.3 %all-to-all-start = ((bf16[8,192,512]{2,1,0:T(8,128)(2,1)}), bf16[8,192,512]{2,1,0:T(8,128)(2,1)S(1)}, u32[]{:S(2)}, u32[]{:S(2)}) async-start(bf16[8,192,512]{2,1,0:T(8,128)(2,1)} %qkv_block.2), calls=%async_computation | async-start | bytes 3145728 | tf_op jit(solution)/shard_map/all_to_all | solution.py:1450
  68.3 41.3 %all-to-all-start.2 = ((bf16[8,192,512]{2,1,0:T(8,128)(2,1)}), bf16[8,192,512]{2,1,0:T(8,128)(2,1)S(1)}, u32[]{:S(2)}, u32[]{:S(2)}) async-start(bf16[8,192,512]{2,1,0:T(8,128)(2,1)} %qkv_block.3), calls=%async_computation.2 | async-start | bytes 3145728 | tf_op jit(solution)/shard_map/all_to_all | solution.py:1450
  110.2 28.5 %all-to-all-start.1 = ((bf16[8,64,512]{2,1,0:T(8,128)(2,1)}), bf16[8,64,512]{2,1,0:T(8,128)(2,1)S(1)}, u32[]{:S(2)}, u32[]{:S(2)}) async-start(bf16[8,64,512]{2,1,0:T(8,128)(2,1)} %get-tuple-element.104.o_ref), calls=%async_computation.1 | async-start | bytes 1048576 | tf_op jit(solution)/shard_map/all_to_all | solution.py:1463
  138.8 20.7 %all-to-all-start.3 = ((bf16[8,64,512]{2,1,0:T(8,128)(2,1)}), bf16[8,64,512]{2,1,0:T(8,128)(2,1)}, u32[]{:S(2)}, u32[]{:S(2)}) async-start(bf16[8,64,512]{2,1,0:T(8,128)(2,1)} %get-tuple-element.108.o_ref), calls=%async_computation.3 | async-start | bytes 1048576 | tf_op jit(solution)/shard_map/all_to_all | solution.py:1463
  210.4 31.6 %all-to-all-start.4 = ((bf16[8,128,512]{2,1,0:T(8,128)(2,1)}), bf16[8,128,512]{2,1,0:T(8,128)(2,1)}, u32[]{:S(2)}, u32[]{:S(2)}) async-start(bf16[8,128,512]{2,1,0:T(8,128)(2,1)} %get-tuple-element.111), calls=%async_computation.4 | async-start | bytes 2097152 | tf_op jit(solution)/shard_map/all_to_all | solution.py:1483
  237.8 41.6 %collective-permute-start.6 = (bf16[2,4,64,1024]{3,2,1,0:T(8,128)(2,1)}, bf16[2,4,64,1024]{3,2,1,0:T(8,128)(2,1)S(1)}, u32[]{:S(2)}, u32[]{:S(2)}) collective-permute-start(bf16[2,4,64,1024]{3,2,1,0:T(8,128)(2,1)} %get-tuple-element.114), channel_id=1, source_target_pairs={{0,8},{8,0},{16,24},{24,16},{1,9},{9,1},{17,25},{25,17},{2,10},{10... | collective-permute-start | bytes 3145736 | tf_op jit(solution)/shard_map/ppermute | solution.py:1311
  237.8 41.6 %collective-permute-start.7 = (bf16[2,4,64,1024]{3,2,1,0:T(8,128)(2,1)}, bf16[2,4,64,1024]{3,2,1,0:T(8,128)(2,1)S(1)}, u32[]{:S(2)}, u32[]{:S(2)}) collective-permute-start(bf16[2,4,64,1024]{3,2,1,0:T(8,128)(2,1)} %get-tuple-element.116), channel_id=1, source_target_pairs={{0,16},{8,24},{16,0},{24,8},{1,17},{9,25},{17,1},{25,9},{2,18},{10... | collective-permute-start | bytes 3145736 | tf_op jit(solution)/shard_map/ppermute | solution.py:1311
  274.2 41.6 %collective-permute-start.5 = (bf16[2,4,80,1024]{3,2,1,0:T(8,128)(2,1)}, bf16[2,4,80,1024]{3,2,1,0:T(8,128)(2,1)}, u32[]{:S(2)}, u32[]{:S(2)}) collective-permute-start(bf16[2,4,80,1024]{3,2,1,0:T(8,128)(2,1)} %copy-done.8), channel_id=1, source_target_pairs={{0,16},{8,24},{16,0},{24,8},{1,17},{9,25},{17,1},{25,9},{2,18},{10... | collective-permute-start | bytes 3932168 | tf_op jit(solution)/shard_map/ppermute | solution.py:1311
  275.1 40.6 %collective-permute-start.4 = (bf16[2,4,80,1024]{3,2,1,0:T(8,128)(2,1)S(1)}, bf16[2,4,80,1024]{3,2,1,0:T(8,128)(2,1)}, u32[]{:S(2)}, u32[]{:S(2)}) collective-permute-start(bf16[2,4,80,1024]{3,2,1,0:T(8,128)(2,1)S(1)} %get-tuple-element.122), channel_id=1, source_target_pairs={{0,8},{8,0},{16,24},{24,16},{1,9},{9,1},{17,25},{25,17},{2,10},{10... | collective-permute-start | bytes 3932168 | tf_op jit(solution)/shard_map/ppermute | solution.py:1311
  279.4 42.1 %all-to-all-start.6 = ((bf16[8,192,512]{2,1,0:T(8,128)(2,1)}), bf16[8,192,512]{2,1,0:T(8,128)(2,1)}, u32[]{:S(2)}, u32[]{:S(2)}) async-start(bf16[8,192,512]{2,1,0:T(8,128)(2,1)} %attend_back.2), calls=%async_computation.6 | async-start | bytes 3145728 | tf_op jit(solution)/shard_map/all_to_all | solution.py:1493
  321.5 44.5 %all-to-all-start.5 = ((bf16[8,192,512]{2,1,0:T(8,128)(2,1)}), bf16[8,192,512]{2,1,0:T(8,128)(2,1)}, u32[]{:S(2)}, u32[]{:S(2)}) async-start(bf16[8,192,512]{2,1,0:T(8,128)(2,1)} %attend_back.3), calls=%async_computation.5 | async-start | bytes 3145728 | tf_op jit(solution)/shard_map/all_to_all | solution.py:1493
  331.8 28.2 %collective-permute-start.9 = (bf16[4,144,1024]{2,1,0:T(8,128)(2,1)S(1)}, bf16[4,144,1024]{2,1,0:T(8,128)(2,1)S(1)}, u32[]{:S(2)}, u32[]{:S(2)}) collective-permute-start(bf16[4,144,1024]{2,1,0:T(8,128)(2,1)S(1)} %get-tuple-element.134), channel_id=1, source_target_pairs={{0,8},{8,0},{16,24},{24,16},{1,9},{9,1},{17,25},{25,17},{2,10},{10... | collective-permute-start | bytes 3538952 | tf_op jit(solution)/shard_map/ppermute | solution.py:1311
  331.8 28.2 %collective-permute-start.8 = (bf16[4,144,1024]{2,1,0:T(8,128)(2,1)S(1)}, bf16[4,144,1024]{2,1,0:T(8,128)(2,1)S(1)}, u32[]{:S(2)}, u32[]{:S(2)}) collective-permute-start(bf16[4,144,1024]{2,1,0:T(8,128)(2,1)S(1)} %get-tuple-element.132), channel_id=1, source_target_pairs={{0,16},{8,24},{16,0},{24,8},{1,17},{9,25},{17,1},{25,9},{2,18},{10... | collective-permute-start | bytes 3538952 | tf_op jit(solution)/shard_map/ppermute | solution.py:1311
  385.1 72.1 %all-to-all-start.7 = ((bf16[4,2,176,1024]{3,2,1,0:T(8,128)(2,1)}), bf16[4,2,176,1024]{3,2,1,0:T(8,128)(2,1)}, u32[]{:S(2)}, u32[]{:S(2)}) async-start(bf16[4,2,176,1024]{3,2,1,0:T(8,128)(2,1)} %put_rows.1), calls=%async_computation.7 | async-start | bytes 5767168 | tf_op jit(solution)/shard_map/all_to_all | solution.py:1350
  405.5 23.4 %collective-permute-start.14 = (bf16[2,4,32,1024]{3,2,1,0:T(8,128)(2,1)S(1)}, bf16[2,4,32,1024]{3,2,1,0:T(8,128)(2,1)S(1)}, u32[]{:S(2)}, u32[]{:S(2)}) collective-permute-start(bf16[2,4,32,1024]{3,2,1,0:T(8,128)(2,1)S(1)} %get-tuple-element.161), channel_id=1, source_target_pairs={{0,8},{8,0},{16,24},{24,16},{1,9},{9,1},{17,25},{25,17},{2,10},{10... | collective-permute-start | bytes 1572872 | tf_op jit(solution)/shard_map/ppermute | solution.py:1311
  406.9 23.0 %collective-permute-start.16 = (bf16[2,4,32,1024]{3,2,1,0:T(8,128)(2,1)S(1)}, bf16[2,4,32,1024]{3,2,1,0:T(8,128)(2,1)S(1)}, u32[]{:S(2)}, u32[]{:S(2)}) collective-permute-start(bf16[2,4,32,1024]{3,2,1,0:T(8,128)(2,1)S(1)} %get-tuple-element.164), channel_id=1, source_target_pairs={{0,16},{8,24},{16,0},{24,8},{1,17},{9,25},{17,1},{25,9},{2,18},{10... | collective-permute-start | bytes 1572872 | tf_op jit(solution)/shard_map/ppermute | solution.py:1311
  460.2 26.9 %collective-permute-start.22 = (bf16[2,144,1024]{2,1,0:T(8,128)(2,1)}, bf16[2,144,1024]{2,1,0:T(8,128)(2,1)S(1)}, u32[]{:S(2)}, u32[]{:S(2)}) collective-permute-start(bf16[2,144,1024]{2,1,0:T(8,128)(2,1)} %get-tuple-element.175.refs_0_), channel_id=1, source_target_pairs={{0,8},{8,0},{16,24},{24,16},{1,9},{9,1},{17,25},{25,17},{2,10},{10... | collective-permute-start | bytes 1769480 | tf_op jit(solution)/shard_map/ppermute | solution.py:1311
  461.0 26.4 %collective-permute-start.23 = (bf16[2,144,1024]{2,1,0:T(8,128)(2,1)}, bf16[2,144,1024]{2,1,0:T(8,128)(2,1)S(1)}, u32[]{:S(2)}, u32[]{:S(2)}) collective-permute-start(bf16[2,144,1024]{2,1,0:T(8,128)(2,1)} %get-tuple-element.175.refs_0_), channel_id=1, source_target_pairs={{0,16},{8,24},{16,0},{24,8},{1,17},{9,25},{17,1},{25,9},{2,18},{10... | collective-permute-start | bytes 1769480 | tf_op jit(solution)/shard_map/ppermute | solution.py:1311
  462.4 25.0 %collective-permute-start.24 = (bf16[2,144,1024]{2,1,0:T(8,128)(2,1)}, bf16[2,144,1024]{2,1,0:T(8,128)(2,1)S(1)}, u32[]{:S(2)}, u32[]{:S(2)}) collective-permute-start(bf16[2,144,1024]{2,1,0:T(8,128)(2,1)} %get-tuple-element.175.refs_0_), channel_id=1, source_target_pairs={{0,24},{8,16},{16,8},{24,0},{1,25},{9,17},{17,9},{25,1},{2,26},{10... | collective-permute-start | bytes 1769480 | tf_op jit(solution)/shard_map/ppermute | solution.py:1311
  463.7 23.4 %collective-permute-start.20 = (bf16[2,80,1024]{2,1,0:T(8,128)(2,1)S(1)}, bf16[2,80,1024]{2,1,0:T(8,128)(2,1)S(1)}, u32[]{:S(2)}, u32[]{:S(2)}) collective-permute-start(bf16[2,80,1024]{2,1,0:T(8,128)(2,1)S(1)} %copy-done.52), channel_id=1, source_target_pairs={{0,4},{1,5},{2,6},{3,7},{4,0},{5,1},{6,2},{7,3},{8,12},{9,13},{10,... | collective-permute-start | bytes 983048 | tf_op jit(solution)/shard_map/ppermute | solution.py:1311
  466.0 21.2 %collective-permute-start.21 = (bf16[2,80,1024]{2,1,0:T(8,128)(2,1)S(1)}, bf16[2,80,1024]{2,1,0:T(8,128)(2,1)S(1)}, u32[]{:S(2)}, u32[]{:S(2)}) collective-permute-start(bf16[2,80,1024]{2,1,0:T(8,128)(2,1)S(1)} %copy-done.51), channel_id=1, source_target_pairs={{0,6},{1,7},{2,4},{3,5},{4,2},{5,3},{6,0},{7,1},{8,14},{9,15},{10,... | collective-permute-start | bytes 983048 | tf_op jit(solution)/shard_map/ppermute | solution.py:1311
  495.3 28.8 %collective-permute-start.28 = (bf16[2,80,1024]{2,1,0:T(8,128)(2,1)}, bf16[2,80,1024]{2,1,0:T(8,128)(2,1)S(1)}, u32[]{:S(2)}, u32[]{:S(2)}) collective-permute-start(bf16[2,80,1024]{2,1,0:T(8,128)(2,1)} %fourth_sum.1.refs_0_), channel_id=1, source_target_pairs={{0,8},{8,0},{16,24},{24,16},{1,9},{9,1},{17,25},{25,17},{2,10},{10... | collective-permute-start | bytes 983048 | tf_op jit(solution)/shard_map/ppermute | solution.py:1311
  496.1 27.9 %collective-permute-start.29 = (bf16[2,80,1024]{2,1,0:T(8,128)(2,1)}, bf16[2,80,1024]{2,1,0:T(8,128)(2,1)S(1)}, u32[]{:S(2)}, u32[]{:S(2)}) collective-permute-start(bf16[2,80,1024]{2,1,0:T(8,128)(2,1)} %fourth_sum.1.refs_0_), channel_id=1, source_target_pairs={{0,16},{8,24},{16,0},{24,8},{1,17},{9,25},{17,1},{25,9},{2,18},{10... | collective-permute-start | bytes 983048 | tf_op jit(solution)/shard_map/ppermute | solution.py:1311
  497.2 26.9 %collective-permute-start.30 = (bf16[2,80,1024]{2,1,0:T(8,128)(2,1)}, bf16[2,80,1024]{2,1,0:T(8,128)(2,1)S(1)}, u32[]{:S(2)}, u32[]{:S(2)}) collective-permute-start(bf16[2,80,1024]{2,1,0:T(8,128)(2,1)} %fourth_sum.1.refs_0_), channel_id=1, source_target_pairs={{0,24},{8,16},{16,8},{24,0},{1,25},{9,17},{17,9},{25,1},{2,26},{10... | collective-permute-start | bytes 983048 | tf_op jit(solution)/shard_map/ppermute | solution.py:1311
  (68 other events, 581.3 us)

commit v7 on v5

--- a/solution.py
+++ b/solution.py
@@ -1025,7 +1025,7 @@
 def first_sum(ids, pairs, splits):
     _, _, _, z_ways, _, width = pairs[0][0].shape
     total = sum(k.shape[4] for k, _ in pairs)
-    step = 1 if total > 100 else z_ways
+    step = z_ways // 2 if total > 100 else z_ways
 
     def source(half, axis, mine, rows):
         def at(g, z, ids):

time: 523 us -> 523 us (level)
  transfers between devices with their start and end apart: 40 -> 40, of which waited for: 19 -> 17; matrix products, arithmetic and copies ran while one was open for 3% -> 3% of each run, Pallas kernels for 36% -> 36%
where the time goes in v7:
time: 523 us; the launch traced here: 513 us
  Pallas kernels  265 us (51%)
  waiting for transfers between devices  141 us (27%)
  starting transfers between devices  70.5 us (13%)
  local copies, waits for them, and re-layouts  23.2 us (4%)
  matrix products  8.32 us (2%)
    ppermute x32, waiting for transfers between devices, sum_exchange(): return lax.ppermute(value, axis, [(i, i ^ bit) for i in range(ways)])  79.6 us
    pallas_call x2, Pallas kernels, attend_back(): pl.pallas_call(functools.partial(bwd_kernel, utts, chunk), out_shape=jax....  64.3 us
    pallas_call x1, Pallas kernels, mid_block(): pl.pallas_call(functools.partial(mid_kernel, (seq_ways, heads_local, utts...  50.8 us
    pallas_call x2, Pallas kernels, attend(): pl.pallas_call(functools.partial(fwd_kernel, utts), out_shape=(jax.ShapeD...  49.8 us
    ppermute x32, starting transfers between devices, sum_exchange(): return lax.ppermute(value, axis, [(i, i ^ bit) for i in range(ways)])  33.7 us
    all_to_all x2, waiting for transfers between devices, shards(): received.append(exchange(packed))  30.9 us
    pallas_call x2, Pallas kernels, back_block(): pl.pallas_call(functools.partial(back_kernel, utts, seq_ways, chunk), out...  19.1 us
    pallas_call x2, Pallas kernels, first_sum(): pl.pallas_call(functools.partial(first_kernel, len(pairs), len(splits)),...  15.5 us
  transfers between devices with their start and end apart: 40, of which 17 were waited for; matrix products, arithmetic and copies ran while one was open for 3% of the time, Pallas kernels for 36%

profile of v7, /device:TPU:0, one launch (start us, length us, event | category | flops | bytes accessed | tf_op | source)
XLA Modules:
  0.0 513.4 jit_solution(15512502271826791100)
XLA Ops:
  7.3 8.0 %head_block.1 = (f32[512,1024]{1,0:T(8,128)}, bf16[2048,512]{1,0:T(8,128)(2,1)}, bf16[1024,512]{1,0:T(8,128)(2,1)S(1)}, bf16[512,1024]{1,0:T(8,128)(2,1)S(1)}) custom-call(s32[8]{0:T(128)S(1)} %bitcast.67, s32[5]{0:T(128)S(1)} %stack.23.ids_ref, s32[8]{0:T(128)S(1)} %bitcast.57, bf16[512,1024]{1,0:T(8,128)(2,1)S(1)} %bitcast.52, ...), custom_call_target="tpu_custom_call" | custom-call | flops 10000000000 | bytes 10000000 | tf_op jit(solution)/shard_map/head_block/pallas_call | solution.py:676
  17.2 6.7 %qkv_block.2 = bf16[8,192,512]{2,1,0:T(8,128)(2,1)} custom-call(s32[8]{0:T(128)} %bitcast.60, s32[5]{0:T(128)} %copy-done.4, s32[8]{0:T(128)} %bitcast.55, bf16[512,1024]{1,0:T(8,128)(2,1)} %copy-done.26, bf16[1024,3072]{1,0:T(8,128)(2,1)} %w_ref.8, bf16[1,3072]{1,0:T(2,128)(2,1)} %broadcast_in_dim.28.b_ref), custom_call_target="tpu_custom_call" | custom-call | flops 7500000256 | bytes 7500000 | tf_op jit(solution)/shard_map/qkv_block/pallas_call | solution.py:729
  23.9 6.5 %all-to-all-start = ((bf16[8,192,512]{2,1,0:T(8,128)(2,1)}), bf16[8,192,512]{2,1,0:T(8,128)(2,1)S(1)}, u32[]{:S(2)}, u32[]{:S(2)}) async-start(bf16[8,192,512]{2,1,0:T(8,128)(2,1)} %qkv_block.2), calls=%async_computation | async-start | bytes 3145728 | tf_op jit(solution)/shard_map/all_to_all | solution.py:1404
  30.4 5.3 %fusion.2.refs_3_ = f32[16,4096]{1,0:T(8,128)} fusion(bf16[1024,6144]{1,0:T(8,128)(2,1)} %param.32, f32[4096]{0:T(1024)S(1)} %slice_convert_fusion, bf16[8,1024]{1,0:T(8,128)(2,1)S(1)} %fusion.15), kind=kOutput, calls=%fused_computation.2 | convolution fusion | flops 134283264 | bytes 8683520 | tf_op jit(solution)/shard_map/dot_general | solution.py:1390
  35.7 6.8 %qkv_block.3 = bf16[8,192,512]{2,1,0:T(8,128)(2,1)} custom-call(s32[8]{0:T(128)} %bitcast.61, s32[5]{0:T(128)} %copy-done.4, s32[8]{0:T(128)} %bitcast.56, bf16[512,1024]{1,0:T(8,128)(2,1)} %copy-done.26, bf16[1024,3072]{1,0:T(8,128)(2,1)} %w_ref.8, bf16[1,3072]{1,0:T(2,128)(2,1)} %broadcast_in_dim.28.b_ref), custom_call_target="tpu_custom_call" | custom-call | flops 7500000256 | bytes 7500000 | tf_op jit(solution)/shard_map/qkv_block/pallas_call | solution.py:729
  42.5 25.7 %all-to-all-done.qkv_ref = bf16[8,192,512]{2,1,0:T(8,128)(2,1)S(1)} async-done(((bf16[8,192,512]{2,1,0:T(8,128)(2,1)}), bf16[8,192,512]{2,1,0:T(8,128)(2,1)S(1)}, u32[]{:S(2)}, u32[]{:S(2)}) %all-to-all-start) | async-done | bytes 1572896 | tf_op jit(solution)/shard_map/all_to_all | solution.py:1404
  79.6 24.8 %attend.2 = (bf16[8,64,512]{2,1,0:T(8,128)(2,1)}, f32[8,1,512]{2,1,0:T(1,128)}) custom-call(s32[8]{0:T(128)} %bitcast.62, bf16[8,192,512]{2,1,0:T(8,128)(2,1)} %copy-done.33, s32[8,1,512]{2,1,0:T(1,128)} %bitcast.82), custom_call_target="tpu_custom_call" | custom-call | flops 24999999488 | bytes 25000000 | tf_op jit(solution)/shard_map/attend/pallas_call | solution.py:135
  113.8 25.0 %attend.3 = (bf16[8,64,512]{2,1,0:T(8,128)(2,1)}, f32[8,1,512]{2,1,0:T(1,128)}) custom-call(s32[8]{0:T(128)} %bitcast.63, bf16[8,192,512]{2,1,0:T(8,128)(2,1)} %copy-done.32, s32[8,1,512]{2,1,0:T(1,128)} %bitcast.83), custom_call_target="tpu_custom_call" | custom-call | flops 24999999488 | bytes 25000000 | tf_op jit(solution)/shard_map/attend/pallas_call | solution.py:135
  138.7 5.2 %all-to-all-start.3 = ((bf16[8,64,512]{2,1,0:T(8,128)(2,1)}), bf16[8,64,512]{2,1,0:T(8,128)(2,1)}, u32[]{:S(2)}, u32[]{:S(2)}) async-start(bf16[8,64,512]{2,1,0:T(8,128)(2,1)} %get-tuple-element.104.o_ref), calls=%async_computation.3 | async-start | bytes 1048576 | tf_op jit(solution)/shard_map/all_to_all | solution.py:1417
  145.8 13.6 %all-to-all-done.3.refs_1_ = bf16[8,64,512]{2,1,0:T(8,128)(2,1)} async-done(((bf16[8,64,512]{2,1,0:T(8,128)(2,1)}), bf16[8,64,512]{2,1,0:T(8,128)(2,1)}, u32[]{:S(2)}, u32[]{:S(2)}) %all-to-all-start.3) | async-done | bytes 524320 | tf_op jit(solution)/shard_map/all_to_all | solution.py:1417
  159.4 50.8 %mid_block.1 = (bf16[512,1024]{1,0:T(8,128)(2,1)}, f32[512,1024]{1,0:T(8,128)}, f32[40,1024]{1,0:T(8,128)}, bf16[8,128,512]{2,1,0:T(8,128)(2,1)}, bf16[8,4,144,1...) custom-call(s32[8]{0:T(128)} %bitcast.64, s32[5]{0:T(128)} %copy-done.4, bf16[8,64,512]{2,1,0:T(8,128)(2,1)} %copy-done.37, ...), custom_call_target="tpu_custom_call" | custom-call | flops 49999998976 | bytes 50000000 | tf_op jit(solution)/shard_map/mid_block/pallas_call | solution.py:547
  214.8 10.5 %collective-permute-done.3 = bf16[8,4,144,1024]{3,2,1,0:T(8,128)(2,1)} collective-permute-done((bf16[8,4,144,1024]{3,2,1,0:T(8,128)(2,1)}, bf16[8,4,144,1024]{3,2,1,0:T(8,128)(2,1)}, u32[]{:S(2)}, u32[]{:S(2)}) %collective-permute-start.3) | collective-permute-done | bytes 9437216 | tf_op jit(solution)/shard_map/ppermute | solution.py:1265
  225.3 10.0 %first_sum.2 = (bf16[2,4,64,1024]{3,2,1,0:T(8,128)(2,1)}, bf16[2,4,80,1024]{3,2,1,0:T(8,128)(2,1)S(1)}, bf16[2,4,64,1024]{3,2,1,0:T(8,128)(2,1)}, bf16[2,4,80,10...) custom-call(s32[5]{0:T(128)S(1)} %copy-done.5, ...), custom_call_target="tpu_custom_call" | custom-call | flops 6000000000 | bytes 6000000 | tf_op jit(solution)/shard_map/first_sum/pallas_call | solution.py:1039
  241.4 32.2 %attend_back.2 = bf16[8,192,512]{2,1,0:T(8,128)(2,1)} custom-call(s32[8]{0:T(128)} %bitcast.65, bf16[8,192,512]{2,1,0:T(8,128)(2,1)} %copy-done.33, s32[8,1,512]{2,1,0:T(1,128)} %bitcast.84, bf16[8,64,512]{2,1,0:T(8,128)(2,1)} %get-tuple-element.100.o_ref, bf16[8,128,512]{2,1,0:T(8,128)(2,1)} %all-to-all-done.4.do_ref, f32[8,1,512]{2,1,0:T(1,128)} %get-tuple-element.115.lse_ref), custom_call_target="tpu_custom_call" | custom-call | flops 32000000000 | bytes 32000000 | tf_op jit(solution)/shard_map/attend_back/pallas_call | solution.py:257
  280.9 32.1 %attend_back.3 = bf16[8,192,512]{2,1,0:T(8,128)(2,1)} custom-call(s32[8]{0:T(128)} %bitcast.66, bf16[8,192,512]{2,1,0:T(8,128)(2,1)} %copy-done.32, s32[8,1,512]{2,1,0:T(1,128)} %bitcast.85, bf16[8,64,512]{2,1,0:T(8,128)(2,1)} %get-tuple-element.104.o_ref, bf16[8,128,512]{2,1,0:T(8,128)(2,1)} %all-to-all-done.4.do_ref, f32[8,1,512]{2,1,0:T(1,128)} %get-tuple-element.117.lse_ref), custom_call_target="tpu_custom_call" | custom-call | flops 32000000000 | bytes 32000000 | tf_op jit(solution)/shard_map/attend_back/pallas_call | solution.py:257
  313.0 5.7 %all-to-all-done.6.grad_ref = bf16[8,192,512]{2,1,0:T(8,128)(2,1)} async-done(((bf16[8,192,512]{2,1,0:T(8,128)(2,1)}), bf16[8,192,512]{2,1,0:T(8,128)(2,1)}, u32[]{:S(2)}, u32[]{:S(2)}) %all-to-all-start.6) | async-done | bytes 1572896 | tf_op jit(solution)/shard_map/all_to_all | solution.py:1447
  330.1 9.1 %back_block.2 = (f32[1024,512]{1,0:T(8,128)S(1)}, f32[3,8,512]{2,1,0:T(8,128)S(1)}, bf16[8,4,48,1024]{3,2,1,0:T(8,128)(2,1)}, bf16[8,4,48,1024]{3,2,1,0:T(8,128)(2,1)}) custom-call(s32[8]{0:T(128)S(1)} %bitcast.68, s32[5]{0:T(128)S(1)} %copy-done.5, s32[8]{0:T(128)S(1)} %bitcast.58, bf16[8,192,512]{2,1,0:T(8,128)(2,1)} %all-to-all-done.6.grad_ref, ...), custom_call_target="tpu_custom_call" | custom-call | flops 10000000000 | bytes 10000000 | tf_op jit(solution)/shard_map/back_block/pallas_call | solution.py:832
  340.6 16.8 %collective-permute-done.9.got_b = bf16[4,144,1024]{2,1,0:T(8,128)(2,1)S(1)} collective-permute-done((bf16[4,144,1024]{2,1,0:T(8,128)(2,1)S(1)}, bf16[4,144,1024]{2,1,0:T(8,128)(2,1)S(1)}, u32[]{:S(2)}, u32[]{:S(2)}) %collective-permute-start.9) | collective-permute-done | bytes 1179680 | tf_op jit(solution)/shard_map/ppermute | solution.py:1265
  363.2 10.0 %back_block.3 = (f32[1024,512]{1,0:T(8,128)S(1)}, f32[3,8,512]{2,1,0:T(8,128)S(1)}, bf16[8,4,48,1024]{3,2,1,0:T(8,128)(2,1)}, bf16[8,4,48,1024]{3,2,1,0:T(8,128)(2,1)}) custom-call(s32[8]{0:T(128)S(1)} %bitcast.69, s32[5]{0:T(128)S(1)} %copy-done.6, s32[8]{0:T(128)S(1)} %bitcast.59, ...), custom_call_target="tpu_custom_call", output_to_operand_aliasing={{2}: (7, {}), {3}: (8, {})} | custom-call | flops 10000000000 | bytes 10000000 | tf_op jit(solution)/shard_map/back_block/pallas_call | solution.py:832
  388.4 5.4 %first_sum.3 = (bf16[2,4,80,1024]{3,2,1,0:T(8,128)(2,1)S(1)}, bf16[2,4,80,1024]{3,2,1,0:T(8,128)(2,1)S(1)}, bf16[2,4,80,1024]{3,2,1,0:T(8,128)(2,1)S(1)}, bf16[2,4,80,1024]{3,2,1,0:T(8,128)(2,1)S(1)}) custom-call(s32[5]{0:T(128)S(1)} %copy-done.6, bf16[2,2,2,4,32,1024]{5,4,3,2,1,0:T(8,128)(2,1)} %bitcast.48, ...), custom_call_target="tpu_custom_call" | custom-call | flops 6000000000 | bytes 6000000 | tf_op jit(solution)/shard_map/first_sum/pallas_call | solution.py:1039
  396.8 28.6 %collective-permute-done.13.refs_1_.refs_5_ = bf16[2,4,80,1024]{3,2,1,0:T(8,128)(2,1)S(1)} collective-permute-done((bf16[2,4,80,1024]{3,2,1,0:T(8,128)(2,1)S(1)}, bf16[2,4,80,1024]{3,2,1,0:T(8,128)(2,1)S(1)}, u32[]{:S(2)}, u32[]{:S(2)}) %collective-permute-start.13) | collective-permute-done | bytes 1310752 | tf_op jit(solution)/shard_map/ppermute | solution.py:1265
  433.2 9.3 %all-to-all-done.7.x = bf16[4,2,144,1024]{3,2,1,0:T(8,128)(2,1)} async-done(((bf16[4,2,144,1024]{3,2,1,0:T(8,128)(2,1)}), bf16[4,2,144,1024]{3,2,1,0:T(8,128)(2,1)}, u32[]{:S(2)}, u32[]{:S(2)}) %all-to-all-start.7) | async-done | bytes 2359328 | tf_op jit(solution)/shard_map/all_to_all | solution.py:1297
  449.7 5.3 %collective-permute-done.16 = bf16[64,1024]{1,0:T(8,128)(2,1)S(1)} collective-permute-done((bf16[64,1024]{1,0:T(8,128)(2,1)S(1)}, bf16[64,1024]{1,0:T(8,128)(2,1)S(1)}, u32[]{:S(2)}, u32[]{:S(2)}) %collective-permute-start.16) | collective-permute-done | bytes 131104 | tf_op jit(solution)/shard_map/ppermute | solution.py:1265
  503.9 6.9 %collective-permute-done.30.refs_2_ = bf16[2,80,1024]{2,1,0:T(8,128)(2,1)S(1)} collective-permute-done((bf16[2,80,1024]{2,1,0:T(8,128)(2,1)}, bf16[2,80,1024]{2,1,0:T(8,128)(2,1)S(1)}, u32[]{:S(2)}, u32[]{:S(2)}) %collective-permute-start.30) | collective-permute-done | bytes 327712 | tf_op jit(solution)/shard_map/ppermute | solution.py:1265
  (202 shorter events, 151.2 us)
Async XLA Ops:
  23.9 44.3 %all-to-all-start = ((bf16[8,192,512]{2,1,0:T(8,128)(2,1)}), bf16[8,192,512]{2,1,0:T(8,128)(2,1)S(1)}, u32[]{:S(2)}, u32[]{:S(2)}) async-start(bf16[8,192,512]{2,1,0:T(8,128)(2,1)} %qkv_block.2), calls=%async_computation | async-start | bytes 3145728 | tf_op jit(solution)/shard_map/all_to_all | solution.py:1404
  68.2 41.3 %all-to-all-start.2 = ((bf16[8,192,512]{2,1,0:T(8,128)(2,1)}), bf16[8,192,512]{2,1,0:T(8,128)(2,1)S(1)}, u32[]{:S(2)}, u32[]{:S(2)}) async-start(bf16[8,192,512]{2,1,0:T(8,128)(2,1)} %qkv_block.3), calls=%async_computation.2 | async-start | bytes 3145728 | tf_op jit(solution)/shard_map/all_to_all | solution.py:1404
  110.2 28.5 %all-to-all-start.1 = ((bf16[8,64,512]{2,1,0:T(8,128)(2,1)}), bf16[8,64,512]{2,1,0:T(8,128)(2,1)S(1)}, u32[]{:S(2)}, u32[]{:S(2)}) async-start(bf16[8,64,512]{2,1,0:T(8,128)(2,1)} %get-tuple-element.100.o_ref), calls=%async_computation.1 | async-start | bytes 1048576 | tf_op jit(solution)/shard_map/all_to_all | solution.py:1417
  138.7 20.7 %all-to-all-start.3 = ((bf16[8,64,512]{2,1,0:T(8,128)(2,1)}), bf16[8,64,512]{2,1,0:T(8,128)(2,1)}, u32[]{:S(2)}, u32[]{:S(2)}) async-start(bf16[8,64,512]{2,1,0:T(8,128)(2,1)} %get-tuple-element.104.o_ref), calls=%async_computation.3 | async-start | bytes 1048576 | tf_op jit(solution)/shard_map/all_to_all | solution.py:1417
  210.3 31.1 %all-to-all-start.4 = ((bf16[8,128,512]{2,1,0:T(8,128)(2,1)}), bf16[8,128,512]{2,1,0:T(8,128)(2,1)}, u32[]{:S(2)}, u32[]{:S(2)}) async-start(bf16[8,128,512]{2,1,0:T(8,128)(2,1)} %get-tuple-element.107), calls=%async_computation.4 | async-start | bytes 2097152 | tf_op jit(solution)/shard_map/all_to_all | solution.py:1437
  236.5 40.2 %collective-permute-start.6 = (bf16[2,4,64,1024]{3,2,1,0:T(8,128)(2,1)}, bf16[2,4,64,1024]{3,2,1,0:T(8,128)(2,1)S(1)}, u32[]{:S(2)}, u32[]{:S(2)}) collective-permute-start(bf16[2,4,64,1024]{3,2,1,0:T(8,128)(2,1)} %get-tuple-element.110), channel_id=1, source_target_pairs={{0,8},{8,0},{16,24},{24,16},{1,9},{9,1},{17,25},{25,17},{2,10},{10... | collective-permute-start | bytes 3145736 | tf_op jit(solution)/shard_map/ppermute | solution.py:1265
  238.0 38.7 %collective-permute-start.7 = (bf16[2,4,64,1024]{3,2,1,0:T(8,128)(2,1)}, bf16[2,4,64,1024]{3,2,1,0:T(8,128)(2,1)S(1)}, u32[]{:S(2)}, u32[]{:S(2)}) collective-permute-start(bf16[2,4,64,1024]{3,2,1,0:T(8,128)(2,1)} %get-tuple-element.112), channel_id=1, source_target_pairs={{0,16},{8,24},{16,0},{24,8},{1,17},{9,25},{17,1},{25,9},{2,18},{10... | collective-permute-start | bytes 3145736 | tf_op jit(solution)/shard_map/ppermute | solution.py:1265
  273.6 39.4 %collective-permute-start.5 = (bf16[2,4,80,1024]{3,2,1,0:T(8,128)(2,1)}, bf16[2,4,80,1024]{3,2,1,0:T(8,128)(2,1)}, u32[]{:S(2)}, u32[]{:S(2)}) collective-permute-start(bf16[2,4,80,1024]{3,2,1,0:T(8,128)(2,1)} %copy-done.9), channel_id=1, source_target_pairs={{0,16},{8,24},{16,0},{24,8},{1,17},{9,25},{17,1},{25,9},{2,18},{10... | collective-permute-start | bytes 3932168 | tf_op jit(solution)/shard_map/ppermute | solution.py:1265
  273.6 39.4 %collective-permute-start.4 = (bf16[2,4,80,1024]{3,2,1,0:T(8,128)(2,1)S(1)}, bf16[2,4,80,1024]{3,2,1,0:T(8,128)(2,1)}, u32[]{:S(2)}, u32[]{:S(2)}) collective-permute-start(bf16[2,4,80,1024]{3,2,1,0:T(8,128)(2,1)S(1)} %get-tuple-element.118), channel_id=1, source_target_pairs={{0,8},{8,0},{16,24},{24,16},{1,9},{9,1},{17,25},{25,17},{2,10},{10... | collective-permute-start | bytes 3932168 | tf_op jit(solution)/shard_map/ppermute | solution.py:1265
  276.6 42.1 %all-to-all-start.6 = ((bf16[8,192,512]{2,1,0:T(8,128)(2,1)}), bf16[8,192,512]{2,1,0:T(8,128)(2,1)}, u32[]{:S(2)}, u32[]{:S(2)}) async-start(bf16[8,192,512]{2,1,0:T(8,128)(2,1)} %attend_back.2), calls=%async_computation.6 | async-start | bytes 3145728 | tf_op jit(solution)/shard_map/all_to_all | solution.py:1447
  318.8 44.4 %all-to-all-start.5 = ((bf16[8,192,512]{2,1,0:T(8,128)(2,1)}), bf16[8,192,512]{2,1,0:T(8,128)(2,1)}, u32[]{:S(2)}, u32[]{:S(2)}) async-start(bf16[8,192,512]{2,1,0:T(8,128)(2,1)} %attend_back.3), calls=%async_computation.5 | async-start | bytes 3145728 | tf_op jit(solution)/shard_map/all_to_all | solution.py:1447
  329.1 28.2 %collective-permute-start.9 = (bf16[4,144,1024]{2,1,0:T(8,128)(2,1)S(1)}, bf16[4,144,1024]{2,1,0:T(8,128)(2,1)S(1)}, u32[]{:S(2)}, u32[]{:S(2)}) collective-permute-start(bf16[4,144,1024]{2,1,0:T(8,128)(2,1)S(1)} %get-tuple-element.130), channel_id=1, source_target_pairs={{0,8},{8,0},{16,24},{24,16},{1,9},{9,1},{17,25},{25,17},{2,10},{10... | collective-permute-start | bytes 3538952 | tf_op jit(solution)/shard_map/ppermute | solution.py:1265
  329.1 28.2 %collective-permute-start.8 = (bf16[4,144,1024]{2,1,0:T(8,128)(2,1)S(1)}, bf16[4,144,1024]{2,1,0:T(8,128)(2,1)S(1)}, u32[]{:S(2)}, u32[]{:S(2)}) collective-permute-start(bf16[4,144,1024]{2,1,0:T(8,128)(2,1)S(1)} %get-tuple-element.128), channel_id=1, source_target_pairs={{0,16},{8,24},{16,0},{24,8},{1,17},{9,25},{17,1},{25,9},{2,18},{10... | collective-permute-start | bytes 3538952 | tf_op jit(solution)/shard_map/ppermute | solution.py:1265
  383.4 59.1 %all-to-all-start.7 = ((bf16[4,2,144,1024]{3,2,1,0:T(8,128)(2,1)}), bf16[4,2,144,1024]{3,2,1,0:T(8,128)(2,1)}, u32[]{:S(2)}, u32[]{:S(2)}) async-start(bf16[4,2,144,1024]{3,2,1,0:T(8,128)(2,1)} %third_sum_all.1), calls=%async_computation.7 | async-start | bytes 4718592 | tf_op jit(solution)/shard_map/all_to_all | solution.py:1297
  394.9 30.5 %collective-permute-start.13 = (bf16[2,4,80,1024]{3,2,1,0:T(8,128)(2,1)S(1)}, bf16[2,4,80,1024]{3,2,1,0:T(8,128)(2,1)S(1)}, u32[]{:S(2)}, u32[]{:S(2)}) collective-permute-start(bf16[2,4,80,1024]{3,2,1,0:T(8,128)(2,1)S(1)} %get-tuple-element.153), channel_id=1, source_target_pairs={{0,8},{8,0},{16,24},{24,16},{1,9},{9,1},{17,25},{25,17},{2,10},{10... | collective-permute-start | bytes 3932168 | tf_op jit(solution)/shard_map/ppermute | solution.py:1265
  396.3 30.2 %collective-permute-start.14 = (bf16[2,4,80,1024]{3,2,1,0:T(8,128)(2,1)S(1)}, bf16[2,4,80,1024]{3,2,1,0:T(8,128)(2,1)S(1)}, u32[]{:S(2)}, u32[]{:S(2)}) collective-permute-start(bf16[2,4,80,1024]{3,2,1,0:T(8,128)(2,1)S(1)} %get-tuple-element.155), channel_id=1, source_target_pairs={{0,16},{8,24},{16,0},{24,8},{1,17},{9,25},{17,1},{25,9},{2,18},{10... | collective-permute-start | bytes 3932168 | tf_op jit(solution)/shard_map/ppermute | solution.py:1265
  396.8 36.4 %collective-permute-start.10 = (f32[64,1024]{1,0:T(8,128)S(1)}, f32[64,1024]{1,0:T(8,128)S(1)}, u32[]{:S(2)}, u32[]{:S(2)}) collective-permute-start(f32[64,1024]{1,0:T(8,128)S(1)} %get-tuple-element.146), channel_id=1, source_target_pairs={{0,1},{1,0},{2,3},{3,2},{4,5},{5,4},{6,7},{7,6},{8,9},{9,8},{10,11... | collective-permute-start | bytes 786440 | tf_op jit(solution)/shard_map/ppermute | solution.py:1265
  432.0 23.1 %collective-permute-start.18 = (bf16[4,80,1024]{2,1,0:T(8,128)(2,1)S(1)}, bf16[4,80,1024]{2,1,0:T(8,128)(2,1)}, u32[]{:S(2)}, u32[]{:S(2)}) collective-permute-start(bf16[4,80,1024]{2,1,0:T(8,128)(2,1)S(1)} %get-tuple-element.156), channel_id=1, source_target_pairs={{0,16},{8,24},{16,0},{24,8},{1,17},{9,25},{17,1},{25,9},{2,18},{10... | collective-permute-start | bytes 1966088 | tf_op jit(solution)/shard_map/ppermute | solution.py:1265
  432.5 22.6 %collective-permute-start.19 = (bf16[4,80,1024]{2,1,0:T(8,128)(2,1)S(1)}, bf16[4,80,1024]{2,1,0:T(8,128)(2,1)}, u32[]{:S(2)}, u32[]{:S(2)}) collective-permute-start(bf16[4,80,1024]{2,1,0:T(8,128)(2,1)S(1)} %get-tuple-element.157), channel_id=1, source_target_pairs={{0,8},{8,0},{16,24},{24,16},{1,9},{9,1},{17,25},{25,17},{2,10},{10... | collective-permute-start | bytes 1966088 | tf_op jit(solution)/shard_map/ppermute | solution.py:1265
  463.2 21.1 %collective-permute-start.28 = (bf16[2,80,1024]{2,1,0:T(8,128)(2,1)}, bf16[2,80,1024]{2,1,0:T(8,128)(2,1)}, u32[]{:S(2)}, u32[]{:S(2)}) collective-permute-start(bf16[2,80,1024]{2,1,0:T(8,128)(2,1)} %get-tuple-element.163), channel_id=1, source_target_pairs={{0,6},{1,7},{2,4},{3,5},{4,2},{5,3},{6,0},{7,1},{8,14},{9,15},{10,... | collective-permute-start | bytes 983048 | tf_op jit(solution)/shard_map/ppermute | solution.py:1265
  464.6 26.3 %collective-permute-start.27 = (bf16[2,80,1024]{2,1,0:T(8,128)(2,1)}, bf16[2,80,1024]{2,1,0:T(8,128)(2,1)}, u32[]{:S(2)}, u32[]{:S(2)}) collective-permute-start(bf16[2,80,1024]{2,1,0:T(8,128)(2,1)} %get-tuple-element.162), channel_id=1, source_target_pairs={{0,4},{1,5},{2,6},{3,7},{4,0},{5,1},{6,2},{7,3},{8,12},{9,13},{10,... | collective-permute-start | bytes 983048 | tf_op jit(solution)/shard_map/ppermute | solution.py:1265
  466.6 24.3 %collective-permute-start.26 = (bf16[2,80,1024]{2,1,0:T(8,128)(2,1)}, bf16[2,80,1024]{2,1,0:T(8,128)(2,1)}, u32[]{:S(2)}, u32[]{:S(2)}) collective-permute-start(bf16[2,80,1024]{2,1,0:T(8,128)(2,1)} %get-tuple-element.161), channel_id=1, source_target_pairs={{0,2},{1,3},{2,0},{3,1},{4,6},{5,7},{6,4},{7,5},{8,10},{9,11},{10,... | collective-permute-start | bytes 983048 | tf_op jit(solution)/shard_map/ppermute | solution.py:1265
  468.3 26.6 %collective-permute-start.23 = (bf16[2,144,1024]{2,1,0:T(8,128)(2,1)S(1)}, bf16[2,144,1024]{2,1,0:T(8,128)(2,1)S(1)}, u32[]{:S(2)}, u32[]{:S(2)}) collective-permute-start(bf16[2,144,1024]{2,1,0:T(8,128)(2,1)S(1)} %copy-done.14), channel_id=1, source_target_pairs={{0,8},{8,0},{16,24},{24,16},{1,9},{9,1},{17,25},{25,17},{2,10},{10... | collective-permute-start | bytes 1769480 | tf_op jit(solution)/shard_map/ppermute | solution.py:1265
  470.4 29.2 %collective-permute-start.24 = (bf16[2,144,1024]{2,1,0:T(8,128)(2,1)S(1)}, bf16[2,144,1024]{2,1,0:T(8,128)(2,1)S(1)}, u32[]{:S(2)}, u32[]{:S(2)}) collective-permute-start(bf16[2,144,1024]{2,1,0:T(8,128)(2,1)S(1)} %copy-done.14), channel_id=1, source_target_pairs={{0,16},{8,24},{16,0},{24,8},{1,17},{9,25},{17,1},{25,9},{2,18},{10... | collective-permute-start | bytes 1769480 | tf_op jit(solution)/shard_map/ppermute | solution.py:1265
  (61 other events, 512.8 us)
